TPU v7x, 32 devices: a whole 2x2x4 slice. The times are simulated.
32 devices in a mesh: hi: 8 (over y, x, core), lo: 4 (over z).
Axes of the slice: x: 2, y: 2, z: 4, core: 2. Of those that a mesh axis runs over, the one named last changes fastest.
Arguments:
- track: float32 [8192, 512], P(('hi', 'lo')), may hold values from -6 to 6
- tight_weight: float32 [1536, 512], replicated, may hold values from -0.15625 to 0.15625
- wide_weight: float32 [1536, 512], replicated, may hold values from -0.15625 to 0.15625
- cotangent: float32 [8192, 512], P(('hi', 'lo')), may hold values from -6 to 6
Outputs:
- features_out: float32 [8192, 512], P(('hi', 'lo'))
- grad_track: float32 [8192, 512], P(('hi', 'lo'))
- grad_near: float32 [1536, 512], P('lo')
- grad_far: float32 [1536, 512], P('lo')
All inputs are finite; a program needn't handle non-finite values.
Results may differ from a plain program's by a relative error of at most 0.000073.
Values sent between devices are 32-bit elements; how exact they have to be, the bound alone decides.
No kernel may reach another device: no remote copies, remote signals or barrier semaphores. Data moves between devices by JAX's collectives and lax.ppermute only.
A program may use at most 64 MiB of HBM per device.

v0:
```python
import jax
import jax.numpy as jnp
from jax import lax
from jax.experimental import pallas as pl
from jax.experimental.pallas import tpu as pltpu
from jax.sharding import PartitionSpec as P


NEAR_STEPS = 4
FAR_STEPS = 2
HP = lax.Precision.HIGH
F32 = jnp.float32
BF16 = jnp.bfloat16


def dot(a, b, contract):
    return lax.dot_general(
        a, b, ((contract[:1], contract[1:]), ((), ())), precision=HP, preferred_element_type=jnp.float32
    )


def gelu_fn(value):
    return jax.nn.gelu(value, approximate=True)


def call(body, outs, ids, *args, scratch=(), to_hbm=False, room=4):
    vmem = pl.BlockSpec(memory_space=pltpu.VMEM)
    smem = pl.BlockSpec(memory_space=pltpu.SMEM)
    make = jax.ShapeDtypeStruct if to_hbm else pltpu.VMEM
    return pl.pallas_call(
        body,
        out_shape=[make(shape, dtype) for shape, dtype in outs],
        in_specs=[smem] + [vmem] * len(args),
        out_specs=[vmem] * len(outs),
        scratch_shapes=[pltpu.VMEM(shape, dtype) for shape, dtype in scratch],
        compiler_params=pltpu.CompilerParams(vmem_limit_bytes=room * 1024 * 1024),
    )(ids, *[pltpu.with_memory_space_constraint(arg, pltpu.VMEM) for arg in args])


def swap(value, axis, mask):
    count = lax.axis_size(axis)
    return lax.ppermute(value, axis, [(i, i ^ mask) for i in range(count)])


def bits(ids):
    hi, lo = ids[0], ids[1]
    chip = hi >> 1
    return hi & 1, chip, chip & 1, chip >> 1, lo


def split(value):
    high = value.astype(BF16)
    return high, (value - high.astype(F32)).astype(BF16)


def mul(a, b, contract):
    dims = ((contract[:1], contract[1:]), ((), ()))

    def one(left, right):
        return lax.dot_general(left, right, dims, preferred_element_type=F32)

    return one(a[0], b[0]) + (one(a[0], b[1]) + one(a[1], b[0]))


def rows_of(pair, start, size):
    return tuple(ref[start : start + size] for ref in pair)


def gelu_both(u):
    root = 0.7978845608028654
    square = u * u
    tanh = jnp.tanh(root * (u + 0.044715 * (u * square)))
    half = 0.5 * (1.0 + tanh)
    slope = half + 0.5 * u * (1.0 - tanh * tanh) * (root * (1.0 + 3.0 * 0.044715 * square))
    return u * half, slope


def block(index, size):
    return pl.ds(pl.multiple_of(index * size, size), size)


def weights_body(ids, near, far, near_h, near_l, far_h, far_l, staged, done):
    parts, rows, _ = staged.shape
    each = parts // 2
    copies = []
    for k in range(parts):
        source = (near, far)[k // each].at[pl.ds(k % each * rows, rows)]
        copies.append(pltpu.make_async_copy(source, staged.at[k], done.at[k]))
        copies[-1].start()
    for k in range(parts):
        copies[k].wait()
        start = k % each * rows
        high, low = ((near_h, near_l), (far_h, far_l))[k // each]
        high[start : start + rows], low[start : start + rows] = split(staged[k])


def split_weights(ids, near, far):
    rows, width = near.shape
    smem = pl.BlockSpec(memory_space=pltpu.SMEM)
    whole = pl.BlockSpec(memory_space=pltpu.HBM)
    vmem = pl.BlockSpec(memory_space=pltpu.VMEM)
    return pl.pallas_call(
        weights_body,
        out_shape=[pltpu.VMEM((rows, width), BF16)] * 4,
        in_specs=[smem, whole, whole],
        out_specs=[vmem] * 4,
        scratch_shapes=[pltpu.VMEM((8, rows // 4, width), F32), pltpu.SemaphoreType.DMA((8,))],
        compiler_params=pltpu.CompilerParams(vmem_limit_bytes=8 * 1024 * 1024),
        name="k_weights",
    )(ids, *[pltpu.with_memory_space_constraint(arg, pltpu.HBM) for arg in (near, far)])


def forward_body(ids, p0, p1, p2, p3, q0, q1, q2, q3, near_h, near_l, far_h, far_l,
                 f0, f1, f2, f3, slope_near, slope_far, hid_h, hid_l, own_h, own_l, oth_h, oth_l, field):
    core, chip, _, _, _ = bits(ids)
    rows, width = slope_near.shape
    size = rows // 4
    pad = jnp.zeros((size, width), BF16)
    for ref in (oth_h, oth_l):
        ref[0:size] = pad
        ref[rows + size :] = pad
    for mask, (own, other) in enumerate(((p0, q0), (p1, q1), (p2, q2), (p3, q3))):
        field[block(chip ^ mask, size)] = own[...]
        high, low = split(other[...])
        oth_h[block((chip ^ mask) + 1, size)] = high
        oth_l[block((chip ^ mask) + 1, size)] = low
    track = field[...]
    own_h[...], own_l[...] = split(track)
    before = pl.ds(pl.multiple_of(core * size, size), rows)
    after = pl.ds(pl.multiple_of(core * size + size, size), rows)
    pre = mul((own_h[...], own_l[...]), rows_of((near_h, near_l), width, width), (1, 0))
    pre = pre + mul((oth_h[before], oth_l[before]), rows_of((near_h, near_l), 0, width), (1, 0))
    pre = pre + mul((oth_h[after], oth_l[after]), rows_of((near_h, near_l), 2 * width, width), (1, 0))
    act, slope = gelu_both(pre)
    slope_near[...] = slope
    hidden = track + act
    hid_h[...], hid_l[...] = split(hidden)
    field[...] = mul((hid_h[...], hid_l[...]), rows_of((far_h, far_l), width, width), (1, 0))
    rest = rows - size
    field[size:] += mul(rows_of((hid_h, hid_l), 0, rest), rows_of((far_h, far_l), 0, width), (1, 0))
    field[0:rest] += mul(rows_of((hid_h, hid_l), size, rest), rows_of((far_h, far_l), 2 * width, width), (1, 0))
    act, slope = gelu_both(field[...])
    slope_far[...] = slope
    field[...] = hidden + act
    for mask, out in enumerate((f0, f1, f2, f3)):
        out[...] = field[block(chip ^ mask, size)]


def half_columns(pair, index):
    width = pair[0].shape[1] // 2
    return tuple(jnp.where(index == 0, ref[:, :width].astype(F32), ref[:, width:].astype(F32)).astype(BF16) for ref in pair)


def far_term(hid, grad, store):
    rows, _ = hid[0].shape
    size = rows // 4
    rest = rows - size
    store(0, mul(rows_of(hid, 0, rest), tuple(g[size:] for g in grad), (0, 0)))
    store(1, mul(tuple(h[...] for h in hid), grad, (0, 0)))
    store(2, mul(rows_of(hid, size, rest), tuple(g[:rest] for g in grad), (0, 0)))


def near_term(core, own, other, grad, store):
    rows, _ = own[0].shape
    size = rows // 4
    before = pl.ds(pl.multiple_of(core * size, size), rows)
    after = pl.ds(pl.multiple_of(core * size + size, size), rows)
    store(0, mul(tuple(o[before] for o in other), grad, (0, 0)))
    store(1, mul(tuple(o[...] for o in own), grad, (0, 0)))
    store(2, mul(tuple(o[after] for o in other), grad, (0, 0)))


def far_other_body(ids, c0, c1, c2, c3, slope, hid_h, hid_l, cot, g_h, g_l, term):
    core, chip, _, _, _ = bits(ids)
    rows, width = cot.shape
    size = rows // 4
    for mask, piece in enumerate((c0, c1, c2, c3)):
        cot[block(chip ^ mask, size)] = piece[...]
    g_h[...], g_l[...] = split(cot[...] * slope[...])

    def store(tap, value):
        term[tap * width : (tap + 1) * width] = value

    far_term((hid_h, hid_l), half_columns((g_h, g_l), 1 - core), store)


def quarter(total, ids, outs):
    _, _, x, y, _ = bits(ids)
    x_keep, x_send, y_keep, y_send = outs
    count, half, _ = x_keep.shape
    for z in range(count):
        start = z * 4 * half
        x_keep[z] = total[pl.ds(pl.multiple_of(start + x * half, half), half)]
        x_send[z] = total[pl.ds(pl.multiple_of(start + (1 - x) * half, half), half)]
        y_keep[z] = total[pl.ds(pl.multiple_of(start + (2 + y) * half, half), half)]
        y_send[z] = total[pl.ds(pl.multiple_of(start + (3 - y) * half, half), half)]


def far_own_body(ids, hid_h, hid_l, g_h, g_l, got, x_keep, x_send, y_keep, y_send, total):
    core, _, _, _, _ = bits(ids)
    width = hid_h.shape[1]

    def store(tap, value):
        total[tap * width : (tap + 1) * width] = value + got[tap * width : (tap + 1) * width]

    far_term((hid_h, hid_l), half_columns((g_h, g_l), core), store)
    quarter(total, ids, (x_keep, x_send, y_keep, y_send))


def backward_body(ids, cot, g_h, g_l, far_h, far_l, slope, grad, gn, gn_h, gn_l):
    rows, width = cot.shape
    size = rows // 4
    rest = rows - size
    grad[...] = cot[...] + mul((g_h[...], g_l[...]), rows_of((far_h, far_l), width, width), (1, 1))
    grad[0:rest] += mul(rows_of((g_h, g_l), size, rest), rows_of((far_h, far_l), 0, width), (1, 1))
    grad[size:] += mul(rows_of((g_h, g_l), 0, rest), rows_of((far_h, far_l), 2 * width, width), (1, 1))
    value = grad[...] * slope[...]
    gn[...] = value
    gn_h[...], gn_l[...] = split(value)


def near_other_body(ids, own_h, own_l, oth_h, oth_l, gn_h, gn_l, term):
    core, _, _, _, _ = bits(ids)
    width = own_h.shape[1]

    def store(tap, value):
        term[tap * width : (tap + 1) * width] = value

    near_term(core, (own_h, own_l), (oth_h, oth_l), half_columns((gn_h, gn_l), 1 - core), store)


def near_own_body(ids, own_h, own_l, oth_h, oth_l, gn_h, gn_l, got, x_keep, x_send, y_keep, y_send, total):
    core, _, _, _, _ = bits(ids)
    width = own_h.shape[1]

    def store(tap, value):
        total[tap * width : (tap + 1) * width] = value + got[tap * width : (tap + 1) * width]

    near_term(core, (own_h, own_l), (oth_h, oth_l), half_columns((gn_h, gn_l), core), store)
    quarter(total, ids, (x_keep, x_send, y_keep, y_send))


def track_body(ids, grad, gn_h, gn_l, other, near_h, near_l, t0, t1, t2, t3, oth_h, oth_l, field):
    core, chip, _, _, _ = bits(ids)
    rows, width = grad.shape
    size = rows // 4
    pad = jnp.zeros((size, width), BF16)
    for ref in (oth_h, oth_l):
        ref[0:size] = pad
        ref[rows + size :] = pad
    high, low = split(other[...])
    oth_h[size : rows + size] = high
    oth_l[size : rows + size] = low
    before = pl.ds(pl.multiple_of(core * size, size), rows)
    after = pl.ds(pl.multiple_of(core * size + size, size), rows)
    total = grad[...] + mul((gn_h[...], gn_l[...]), rows_of((near_h, near_l), width, width), (1, 1))
    total = total + mul((oth_h[after], oth_l[after]), rows_of((near_h, near_l), 0, width), (1, 1))
    field[...] = total + mul((oth_h[before], oth_l[before]), rows_of((near_h, near_l), 2 * width, width), (1, 1))
    for mask, out in enumerate((t0, t1, t2, t3)):
        out[...] = field[block(chip ^ mask, size)]


def plane_body(ids, x_kept, x_got, y_kept, y_got, x_keep, x_send, y_keep, y_send):
    _, _, x, y, _ = bits(ids)
    half = x_keep.shape[1]
    for kept, got, bit, keep, send in ((x_kept, x_got, y, x_keep, x_send), (y_kept, y_got, x, y_keep, y_send)):
        for z in range(kept.shape[0]):
            mine, theirs = block(bit, half), block(1 - bit, half)
            keep[z] = kept[z, mine] + got[z, mine]
            send[z] = kept[z, theirs] + got[z, theirs]


def first_lo_body(ids, x_kept, x_got, y_kept, y_got, keep, send):
    lo = bits(ids)[4]
    bit = lo & 1
    for k in range(keep.shape[0]):
        for half, (kept, got) in enumerate(((x_kept, x_got), (y_kept, y_got))):
            keep[k, half] = kept[2 * k + bit] + got[2 * k + bit]
            send[k, half] = kept[2 * k + 1 - bit] + got[2 * k + 1 - bit]


def second_lo_body(ids, kept, got, keep, send):
    bit = bits(ids)[4] >> 1
    keep[...] = kept[bit] + got[bit]
    send[...] = kept[1 - bit] + got[1 - bit]


def sum_pair_body(scale, ids, kept, got, by_x, by_y):
    by_x[...] = (kept[0] + got[0]) * scale
    by_y[...] = (kept[1] + got[1]) * scale


def sum_body(scale, ids, kept, got, out):
    out[...] = (kept[...] + got[...]) * scale


def cross_body(ids, a, a_got, b, b_got, a_out, b_out):
    a_out[...] = a[...] + a_got[...]
    b_out[...] = b[...] + b_got[...]


def far_rows_body(ids, a, a_got, b, b_got, out):
    _, _, x, y, _ = bits(ids)
    half = a.shape[0]
    out[block(x, half)] = a[...]
    out[block(1 - x, half)] = a_got[...]
    out[block(2 + y, half)] = b[...]
    out[block(3 - y, half)] = b_got[...]


def near_rows_body(ids, s0, s1, s2, s3, out):
    _, _, x, y, _ = bits(ids)
    size = s0.shape[1]
    for mask, piece in enumerate((s0, s1, s2, s3)):
        px, py = x ^ (mask & 1), y ^ (mask >> 1)
        out[block(2 * px + py, size)] = piece[0]
        out[block(4 + 2 * py + px, size)] = piece[1]


def columns_body(ids, own, got, out):
    core = bits(ids)[0]
    width = own.shape[1]
    out[:, :width] = jnp.where(core == 0, own[...], got[...])
    out[:, width:] = jnp.where(core == 0, got[...], own[...])


def collect_body(ids, p0, p1, p2, p3, out):
    chip = bits(ids)[1]
    size = p0.shape[0]
    for mask, piece in enumerate((p0, p1, p2, p3)):
        out[block(chip ^ mask, size)] = piece[...]


def pieces(field, chip):
    size = field.shape[0] // 4
    return [lax.dynamic_slice_in_dim(field, (chip ^ mask) * size, size, 0) for mask in range(4)]


def over_chips(parts):
    return [parts[0]] + [swap(parts[mask], "hi", 2 * mask) for mask in range(1, 4)]


def family_shards(track, near_weight, far_weight, cotangent):
    return family_step(track, near_weight, far_weight, cotangent)


def family_step(track, near_weight, far_weight, cotangent):
    rows, width = track.shape
    n_hi = lax.axis_size("hi")
    n_lo = lax.axis_size("lo")
    size = rows // 4
    half = width // 2
    tall = near_weight.shape[0]
    part = tall // n_lo // 4
    hi = lax.axis_index("hi")
    lo = lax.axis_index("lo")
    ids = jnp.stack([hi, lo])
    chip = lax.shift_right_logical(hi, 1)
    scale = 1.0 / float(rows * n_hi * n_lo) ** 0.5
    full, piece = (rows, width), (size, width)
    padded = (rows + 2 * size, width)

    own = over_chips(pieces(track, chip))
    other = [swap(own[mask], "hi", 1) for mask in range(4)]
    cot = over_chips(pieces(cotangent, chip))
    near_h, near_l, far_h, far_l = split_weights(ids, near_weight, far_weight)
    near_w, far_w = (near_h, near_l), (far_h, far_l)
    out = call(
        forward_body,
        [(piece, F32)] * 4 + [(full, F32)] * 2 + [(full, BF16)] * 4 + [(padded, BF16)] * 2,
        ids, *own, *other, *near_w, *far_w, scratch=[(full, F32)], room=16,
    )
    feats, slope_near, slope_far = out[:4], out[4], out[5]
    hid, own_pair, oth_pair = out[6:8], out[8:10], out[10:12]
    cot, g_h, g_l, far_other = call(
        far_other_body, [(full, F32), (full, BF16), (full, BF16), ((tall, half), F32)],
        ids, *cot, slope_far, *hid,
    )
    far_got = swap(far_other, "hi", 1)
    feats = over_chips(feats)
    quarters = [((n_lo, part, half), F32)] * 4
    far_q = call(far_own_body, quarters, ids, *hid, g_h, g_l, far_got, scratch=[((tall, half), F32)], room=12)
    far_x, far_y = swap(far_q[1], "hi", 2), swap(far_q[3], "hi", 4)
    grad, gn, gn_h, gn_l = call(
        backward_body, [(full, F32), (full, F32), (full, BF16), (full, BF16)],
        ids, cot, g_h, g_l, *far_w, slope_near,
    )
    (near_other,) = call(near_other_body, [((tall, half), F32)], ids, *own_pair, *oth_pair, gn_h, gn_l)
    near_got = swap(near_other, "hi", 1)
    gn_got = swap(gn, "hi", 1)
    near_q = call(
        near_own_body, quarters, ids, *own_pair, *oth_pair, gn_h, gn_l, near_got,
        scratch=[((tall, half), F32)], room=12,
    )
    near_x, near_y = swap(near_q[1], "hi", 2), swap(near_q[3], "hi", 4)
    first, second = ((n_lo // 2, 2, part, half), F32), ((2, part, half), F32)
    keep, send = call(first_lo_body, [first] * 2, ids, far_q[0], far_x, far_q[2], far_y)
    got = swap(send, "lo", 1)
    grads = call(
        track_body, [(piece, F32)] * 4, ids, grad, gn_h, gn_l, gn_got, *near_w,
        scratch=[(padded, BF16), (padded, BF16), (full, F32)], room=12,
    )
    keep, send = call(second_lo_body, [second] * 2, ids, keep, got)
    got = swap(send, "lo", 2)
    deep = [((n_lo, part // 2, half), F32)] * 4
    near_q = call(plane_body, deep, ids, near_q[0], near_x, near_q[2], near_y)
    near_x, near_y = swap(near_q[1], "hi", 4), swap(near_q[3], "hi", 2)
    grads = over_chips(grads)
    first, second = ((n_lo // 2, 2, part // 2, half), F32), ((2, part // 2, half), F32)
    n_keep, n_send = call(first_lo_body, [first] * 2, ids, near_q[0], near_x, near_q[2], near_y)
    n_got = swap(n_send, "lo", 1)

    def far_sum(*refs):
        sum_pair_body(scale, *refs)

    def near_sum(*refs):
        sum_body(scale, *refs)

    a, b = call(far_sum, [((part, half), F32)] * 2, ids, keep, got)
    a, b = call(cross_body, [((part, half), F32)] * 2, ids, a, swap(a, "hi", 4), b, swap(b, "hi", 2))
    n_keep, n_send = call(second_lo_body, [second] * 2, ids, n_keep, n_got)
    n_got = swap(n_send, "lo", 2)
    (rows_far,) = call(far_rows_body, [((4 * part, half), F32)], ids, a, swap(a, "hi", 2), b, swap(b, "hi", 4))
    far_cols = swap(rows_far, "hi", 1)
    (near_mine,) = call(near_sum, [second], ids, n_keep, n_got)
    near_all = over_chips([near_mine] * 4)
    (rows_near,) = call(near_rows_body, [((4 * part, half), F32)], ids, *near_all)
    near_cols = swap(rows_near, "hi", 1)
    (features,) = call(collect_body, [(full, F32)], ids, *feats, to_hbm=True)
    (grad_track,) = call(collect_body, [(full, F32)], ids, *grads, to_hbm=True)
    wide = [((4 * part, width), F32)]
    (grad_far,) = call(columns_body, wide, ids, rows_far, far_cols, to_hbm=True)
    (grad_near,) = call(columns_body, wide, ids, rows_near, near_cols, to_hbm=True)
    return features, grad_track, grad_near, grad_far


def from_behind(value, axis, steps):
    count = lax.axis_size(axis)
    initial, last = (max(0, -steps), min(count, count - steps))
    return lax.ppermute(value, axis, [(source, source + steps) for source in range(initial, last)])


def halo_shards(track, tight_weight, wide_weight, cotangent):
    def near_pair(field):
        return from_behind(field, ("hi", "lo"), NEAR_STEPS), from_behind(field, ("hi", "lo"), -NEAR_STEPS)

    def far_pair(field):
        return from_behind(field, "hi", FAR_STEPS), from_behind(field, "hi", -FAR_STEPS)

    def back_product(before, center, after, weights):
        width = center.shape[1]
        total = dot(after, weights[0:width], (1, 1))
        total = total + dot(center, weights[width : 2 * width], (1, 1))
        return total + dot(before, weights[2 * width : 3 * width], (1, 1))

    near_prev, near_next = near_pair(track)
    track_taps = jnp.concatenate([near_prev, track, near_next], axis=1)
    pre_near = dot(track_taps, tight_weight, (1, 0))
    act_near, near_pull = jax.vjp(gelu_fn, pre_near)
    hidden = track + act_near
    far_prev, far_next = far_pair(hidden)
    hidden_taps = jnp.concatenate([far_prev, hidden, far_next], axis=1)
    pre_far = dot(hidden_taps, wide_weight, (1, 0))
    act_far, far_pull = jax.vjp(gelu_fn, pre_far)
    features = hidden + act_far
    g_far = far_pull(cotangent)[0]
    term_far = dot(hidden_taps, g_far, (0, 0))
    gfar_prev, gfar_next = far_pair(g_far)
    grad_hidden = cotangent + back_product(gfar_prev, g_far, gfar_next, wide_weight)
    g_near = near_pull(grad_hidden)[0]
    term_near = dot(track_taps, g_near, (0, 0))
    gnear_prev, gnear_next = near_pair(g_near)
    grad_track = grad_hidden + back_product(gnear_prev, g_near, gnear_next, tight_weight)
    scale = 1.0 / jnp.sqrt(jnp.float32(track.shape[0] * lax.axis_size("hi") * lax.axis_size("lo")))
    summed_near, summed_far = lax.psum((term_near, term_far), "hi")
    rows_near = lax.psum_scatter(summed_near, "lo", scatter_dimension=0, tiled=True)
    rows_far = lax.psum_scatter(summed_far, "lo", scatter_dimension=0, tiled=True)
    return (features, grad_track, rows_near * scale, rows_far * scale)


def solution(mesh):
    n_hi, n_lo = mesh.shape["hi"], mesh.shape["lo"]

    def step(track, tight_weight, wide_weight, cotangent):
        rows = track.shape[0] // (n_hi * n_lo)
        closed = NEAR_STEPS == n_lo and FAR_STEPS == 2 and n_hi == 8
        closed = closed and rows % (8 * n_hi) == 0 and tight_weight.shape[0] % (64 * n_lo) == 0
        closed = closed and tight_weight.shape[1] % 256 == 0
        if closed:
            shards = family_shards
        else:
            shards = halo_shards
        in_specs = (P(("hi", "lo"), None), P(), P(), P(("hi", "lo"), None))
        out_specs = (P(("hi", "lo"), None), P(("hi", "lo"), None), P("lo", None), P("lo", None))
        mapped = jax.shard_map(shards, mesh=mesh, in_specs=in_specs, out_specs=out_specs, check_vma=False)
        return mapped(track, tight_weight, wide_weight, cotangent)

    return step
```

profile of v0, /device:TPU:0, one launch (start us, length us, event | category | flops | bytes accessed | tf_op | source)
XLA Modules:
  0.0 109.2 jit_solution(17376969633703572518)
XLA Ops:
  0.7 1.1 %constant_dynamic-slice_fusion.4 = (f32[64,512]{1,0:T(8,128)S(1)}, f32[64,512]{1,0:T(8,128)S(1)}, f32[64,512]{1,0:T(8,128)S(1)}, f32[64,512]{1,0:T(8,128)S(1)}) fusion(f32[256,512]{1,0:T(8,128)} %param.4, s32[]{:T(128)S(6)} %select_n.19, s32[]{:T(128)S(6)} %select_n.17, s32[]{:T(128)S(6)} %select_n.16, s32[]{:T(128)S(6)} %select_n.18), kind=kLoop, calls=%fused_computation.4 | loop fusion | bytes 1048592 | tf_op jit(solution)/shard_map/dynamic_slice | solution.py:336
  1.8 4.0 %collective-permute-start.2 = (f32[64,512]{1,0:T(8,128)S(1)}, f32[64,512]{1,0:T(8,128)S(1)}, u32[]{:S(2)}, u32[]{:S(2)}) collective-permute-start(f32[64,512]{1,0:T(8,128)S(1)} %get-tuple-element.112), channel_id=1, source_target_pairs={{0,24},{4,28},{8,16},{12,20},{16,8},{20,12},{24,0},{28,4},{1,25},{... | collective-permute-start | bytes 393224 | tf_op jit(solution)/shard_map/ppermute | solution.py:42
  6.4 3.7 %collective-permute-done.2.p3 = f32[64,512]{1,0:T(8,128)S(1)} collective-permute-done((f32[64,512]{1,0:T(8,128)S(1)}, f32[64,512]{1,0:T(8,128)S(1)}, u32[]{:S(2)}, u32[]{:S(2)}) %collective-permute-start.2) | collective-permute-done | bytes 131104 | tf_op jit(solution)/shard_map/ppermute | solution.py:42
  10.1 1.1 %constant_dynamic-slice_fusion = (f32[64,512]{1,0:T(8,128)S(1)}, f32[64,512]{1,0:T(8,128)S(1)}, f32[64,512]{1,0:T(8,128)S(1)}, f32[64,512]{1,0:T(8,128)S(1)}) fusion(f32[256,512]{1,0:T(8,128)} %param.7, s32[]{:T(128)S(6)} %select_n.19, s32[]{:T(128)S(6)} %select_n.17, s32[]{:T(128)S(6)} %select_n.16, s32[]{:T(128)S(6)} %select_n.18), kind=kLoop, calls=%fused_computation | loop fusion | bytes 1048592 | tf_op jit(solution)/shard_map/dynamic_slice | solution.py:336
  11.3 1.1 collective-permute-done.p1
  12.9 2.0 %collective-permute-start.12 = (f32[64,512]{1,0:T(8,128)S(1)}, f32[64,512]{1,0:T(8,128)S(1)}, u32[]{:S(2)}, u32[]{:S(2)}) collective-permute-start(f32[64,512]{1,0:T(8,128)S(1)} %get-tuple-element.108), channel_id=1, source_target_pairs={{0,24},{4,28},{8,16},{12,20},{16,8},{20,12},{24,0},{28,4},{1,25},{... | collective-permute-start | bytes 393224 | tf_op jit(solution)/shard_map/ppermute | solution.py:42
  15.4 0.9 collective-permute-start.11
  16.4 3.5 %k_weights.1 = (bf16[1536,512]{1,0:T(8,128)(2,1)S(1)}, bf16[1536,512]{1,0:T(8,128)(2,1)S(1)}, bf16[1536,512]{1,0:T(8,128)(2,1)S(1)}, bf16[1536,512]{1,0:T(8,128)(2,1)S(1)}) custom-call(s32[2]{0:T(128)S(1)} %pad_add_fusion.ids.refs_0_, f32[1536,512]{1,0:T(8,128)} %near.1, f32[1536,512]{1,0:T(8,128)} %far.1), custom_call_target="tpu_custom_call" | custom-call | tf_op jit(solution)/shard_map/k_weights/pallas_call | solution.py:102
  20.0 3.7 %shard_map.75 = (f32[64,512]{1,0:T(8,128)S(1)}, f32[64,512]{1,0:T(8,128)S(1)}, f32[64,512]{1,0:T(8,128)S(1)}, f32[64,512]{1,0:T(8,128)S(1)}, f32[256,512]{1,0:T(...) custom-call(s32[2]{0:T(128)S(1)} %pad_add_fusion.ids.refs_0_, ...), custom_call_target="tpu_custom_call" | custom-call | tf_op jit(solution)/shard_map/pallas_call | solution.py:30
  23.7 1.5 %shard_map.77 = (f32[256,512]{1,0:T(8,128)S(1)}, bf16[256,512]{1,0:T(8,128)(2,1)S(1)}, bf16[256,512]{1,0:T(8,128)(2,1)S(1)}, f32[1536,256]{1,0:T(8,128)S(1)}) custom-call(s32[2]{0:T(128)S(1)} %pad_add_fusion.ids.refs_0_, f32[64,512]{1,0:T(8,128)S(1)} %get-tuple-element.110.c0, f32[64,512]{1,0:T(8,128)S(1)} %collective-permute-done.10.c1, ...), custom_call_target="tpu_custom_call" | custom-call | tf_op jit(solution)/shard_map/pallas_call | solution.py:30
  25.3 2.1 %shard_map.78 = (f32[256,512]{1,0:T(8,128)S(1)}, f32[256,512]{1,0:T(8,128)S(1)}, bf16[256,512]{1,0:T(8,128)(2,1)S(1)}, bf16[256,512]{1,0:T(8,128)(2,1)S(1)}) custom-call(s32[2]{0:T(128)S(1)} %pad_add_fusion.ids.refs_0_, f32[256,512]{1,0:T(8,128)S(1)} %get-tuple-element.67.cot, bf16[256,512]{1,0:T(8,128)(2,1)S(1)} %get-tuple-element.68.g_h, ...), custom_call_target="tpu_custom_call" | custom-call | tf_op jit(solution)/shard_map/pallas_call | solution.py:30
  27.4 1.4 %shard_map.81 = f32[1536,256]{1,0:T(8,128)S(1)} custom-call(s32[2]{0:T(128)S(1)} %pad_add_fusion.ids.refs_0_, bf16[256,512]{1,0:T(8,128)(2,1)S(1)} %get-tuple-element.79.own_h, bf16[256,512]{1,0:T(8,128)(2,1)S(1)} %get-tuple-element.80.own_l, bf16[384,512]{1,0:T(8,128)(2,1)S(1)} %get-tuple-element.81.oth_h, bf16[384,512]{1,0:T(8,128)(2,1)S(1)} %get-tuple-element.82.oth_l, ...), custom_call_target="tpu_custom_call" | custom-call | tf_op jit(solution)/shard_map/pallas_call | solution.py:30
  29.4 1.6 %shard_map.89 = (f32[4,96,256]{2,1,0:T(8,128)S(1)}, f32[4,96,256]{2,1,0:T(8,128)S(1)}, f32[4,96,256]{2,1,0:T(8,128)S(1)}, f32[4,96,256]{2,1,0:T(8,128)S(1)}) custom-call(s32[2]{0:T(128)S(1)} %pad_add_fusion.ids.refs_0_, bf16[256,512]{1,0:T(8,128)(2,1)S(1)} %get-tuple-element.65.hid_h, bf16[256,512]{1,0:T(8,128)(2,1)S(1)} %get-tuple-element.66.hid_l, ...), custom_call_target="tpu_custom_call" | custom-call | tf_op jit(solution)/shard_map/pallas_call | solution.py:30
  31.0 1.5 %collective-permute-start.29 = (f32[4,96,256]{2,1,0:T(8,128)S(1)}, f32[4,96,256]{2,1,0:T(8,128)S(1)}, u32[]{:S(2)}, u32[]{:S(2)}) collective-permute-start(f32[4,96,256]{2,1,0:T(8,128)S(1)} %get-tuple-element.97), channel_id=1, source_target_pairs={{0,8},{4,12},{8,0},{12,4},{16,24},{20,28},{24,16},{28,20},{1,9},{5... | collective-permute-start | bytes 1179656 | tf_op jit(solution)/shard_map/ppermute | solution.py:42
  32.5 1.1 collective-permute-start.30
  33.6 1.5 %shard_map.82 = (f32[4,96,256]{2,1,0:T(8,128)S(1)}, f32[4,96,256]{2,1,0:T(8,128)S(1)}, f32[4,96,256]{2,1,0:T(8,128)S(1)}, f32[4,96,256]{2,1,0:T(8,128)S(1)}) custom-call(s32[2]{0:T(128)S(1)} %pad_add_fusion.ids.refs_0_, bf16[256,512]{1,0:T(8,128)(2,1)S(1)} %get-tuple-element.79.own_h, bf16[256,512]{1,0:T(8,128)(2,1)S(1)} %get-tuple-element.80.own_l, ...), custom_call_target="tpu_custom_call" | custom-call | tf_op jit(solution)/shard_map/pallas_call | solution.py:30
  35.1 0.6 collective-permute-start.18
  35.7 1.0 collective-permute-start.19
  36.7 6.3 %collective-permute-done.29.x_got = f32[4,96,256]{2,1,0:T(8,128)S(1)} collective-permute-done((f32[4,96,256]{2,1,0:T(8,128)S(1)}, f32[4,96,256]{2,1,0:T(8,128)S(1)}, u32[]{:S(2)}, u32[]{:S(2)}) %collective-permute-start.29) | collective-permute-done | bytes 393248 | tf_op jit(solution)/shard_map/ppermute | solution.py:42
  43.0 1.5 %collective-permute-done.30.y_got = f32[4,96,256]{2,1,0:T(8,128)S(1)} collective-permute-done((f32[4,96,256]{2,1,0:T(8,128)S(1)}, f32[4,96,256]{2,1,0:T(8,128)S(1)}, u32[]{:S(2)}, u32[]{:S(2)}) %collective-permute-start.30) | collective-permute-done | bytes 393248 | tf_op jit(solution)/shard_map/ppermute | solution.py:42
  44.5 0.6 shard_map.90
  45.1 1.7 %collective-permute-start.31 = (f32[2,2,96,256]{3,2,1,0:T(8,128)S(1)}, f32[2,2,96,256]{3,2,1,0:T(8,128)S(1)}, u32[]{:S(2)}, u32[]{:S(2)}) collective-permute-start(f32[2,2,96,256]{3,2,1,0:T(8,128)S(1)} %get-tuple-element.101), channel_id=1, source_target_pairs={{0,1},{1,0},{2,3},{3,2},{4,5},{5,4},{6,7},{7,6},{8,9},{9,8},{10,11... | collective-permute-start | bytes 1179656 | tf_op jit(solution)/shard_map/ppermute | solution.py:42
  46.8 3.7 %collective-permute-done.18.x_got = f32[4,96,256]{2,1,0:T(8,128)S(1)} collective-permute-done((f32[4,96,256]{2,1,0:T(8,128)S(1)}, f32[4,96,256]{2,1,0:T(8,128)S(1)}, u32[]{:S(2)}, u32[]{:S(2)}) %collective-permute-start.18) | collective-permute-done | bytes 393248 | tf_op jit(solution)/shard_map/ppermute | solution.py:42
  50.5 1.2 %collective-permute-done.19.y_got = f32[4,96,256]{2,1,0:T(8,128)S(1)} collective-permute-done((f32[4,96,256]{2,1,0:T(8,128)S(1)}, f32[4,96,256]{2,1,0:T(8,128)S(1)}, u32[]{:S(2)}, u32[]{:S(2)}) %collective-permute-start.19) | collective-permute-done | bytes 393248 | tf_op jit(solution)/shard_map/ppermute | solution.py:42
  51.7 0.6 shard_map.83
  52.3 1.2 %collective-permute-start.20 = (f32[4,48,256]{2,1,0:T(8,128)S(1)}, f32[4,48,256]{2,1,0:T(8,128)S(1)}, u32[]{:S(2)}, u32[]{:S(2)}) collective-permute-start(f32[4,48,256]{2,1,0:T(8,128)S(1)} %get-tuple-element.88), channel_id=1, source_target_pairs={{0,16},{4,20},{8,24},{12,28},{16,0},{20,4},{24,8},{28,12},{1,17},{... | collective-permute-start | bytes 589832 | tf_op jit(solution)/shard_map/ppermute | solution.py:42
  54.0 4.1 %collective-permute-done.20.x_got = f32[4,48,256]{2,1,0:T(8,128)S(1)} collective-permute-done((f32[4,48,256]{2,1,0:T(8,128)S(1)}, f32[4,48,256]{2,1,0:T(8,128)S(1)}, u32[]{:S(2)}, u32[]{:S(2)}) %collective-permute-start.20) | collective-permute-done | bytes 196640 | tf_op jit(solution)/shard_map/ppermute | solution.py:42
  58.1 1.1 collective-permute-done.21.y_got
  59.1 0.6 shard_map.84
  59.7 1.6 %collective-permute-start.22 = (f32[2,2,48,256]{3,2,1,0:T(8,128)S(1)}, f32[2,2,48,256]{3,2,1,0:T(8,128)S(1)}, u32[]{:S(2)}, u32[]{:S(2)}) collective-permute-start(f32[2,2,48,256]{3,2,1,0:T(8,128)S(1)} %get-tuple-element.92), channel_id=1, source_target_pairs={{0,1},{1,0},{2,3},{3,2},{4,5},{5,4},{6,7},{7,6},{8,9},{9,8},{10,11... | collective-permute-start | bytes 589832 | tf_op jit(solution)/shard_map/ppermute | solution.py:42
  61.4 0.6 shard_map.91
  62.0 2.7 %collective-permute-start.32 = (f32[2,96,256]{2,1,0:T(8,128)S(1)}, f32[2,96,256]{2,1,0:T(8,128)S(1)}, u32[]{:S(2)}, u32[]{:S(2)}) collective-permute-start(f32[2,96,256]{2,1,0:T(8,128)S(1)} %get-tuple-element.103), channel_id=1, source_target_pairs={{0,2},{1,3},{2,0},{3,1},{4,6},{5,7},{6,4},{7,5},{8,10},{9,11},{10,... | collective-permute-start | bytes 589832 | tf_op jit(solution)/shard_map/ppermute | solution.py:42
  64.6 2.8 %collective-permute-done.22.got = f32[2,2,48,256]{3,2,1,0:T(8,128)S(1)} collective-permute-done((f32[2,2,48,256]{3,2,1,0:T(8,128)S(1)}, f32[2,2,48,256]{3,2,1,0:T(8,128)S(1)}, u32[]{:S(2)}, u32[]{:S(2)}) %collective-permute-start.22) | collective-permute-done | bytes 196640 | tf_op jit(solution)/shard_map/ppermute | solution.py:42
  67.5 0.6 shard_map.85
  68.0 1.8 %collective-permute-start.23 = (f32[2,48,256]{2,1,0:T(8,128)S(1)}, f32[2,48,256]{2,1,0:T(8,128)S(1)}, u32[]{:S(2)}, u32[]{:S(2)}) collective-permute-start(f32[2,48,256]{2,1,0:T(8,128)S(1)} %get-tuple-element.94), channel_id=1, source_target_pairs={{0,2},{1,3},{2,0},{3,1},{4,6},{5,7},{6,4},{7,5},{8,10},{9,11},{10,... | collective-permute-start | bytes 294920 | tf_op jit(solution)/shard_map/ppermute | solution.py:42
  69.8 3.4 %collective-permute-done.32.refs_2_ = f32[2,96,256]{2,1,0:T(8,128)S(1)} collective-permute-done((f32[2,96,256]{2,1,0:T(8,128)S(1)}, f32[2,96,256]{2,1,0:T(8,128)S(1)}, u32[]{:S(2)}, u32[]{:S(2)}) %collective-permute-start.32) | collective-permute-done | bytes 196640 | tf_op jit(solution)/shard_map/ppermute | solution.py:42
  73.2 0.6 shard_map.92
  73.7 1.0 collective-permute-start.33
  74.8 0.6 collective-permute-start.34
  76.2 1.7 %collective-permute-start.26 = (f32[2,48,256]{2,1,0:T(8,128)S(1)}, f32[2,48,256]{2,1,0:T(8,128)S(1)}, u32[]{:S(2)}, u32[]{:S(2)}) collective-permute-start(f32[2,48,256]{2,1,0:T(8,128)S(1)} %shard_map.86.s0), channel_id=1, source_target_pairs={{0,24},{4,28},{8,16},{12,20},{16,8},{20,12},{24,0},{28,4},{1,25},{... | collective-permute-start | bytes 294920 | tf_op jit(solution)/shard_map/ppermute | solution.py:42
  77.9 1.0 collective-permute-start.25
  78.9 0.9 collective-permute-start.24
  80.1 0.6 shard_map.93
  80.7 0.9 collective-permute-start.35
  81.6 1.3 %collective-permute-done.26.s3 = f32[2,48,256]{2,1,0:T(8,128)S(1)} collective-permute-done((f32[2,48,256]{2,1,0:T(8,128)S(1)}, f32[2,48,256]{2,1,0:T(8,128)S(1)}, u32[]{:S(2)}, u32[]{:S(2)}) %collective-permute-start.26) | collective-permute-done | bytes 98336 | tf_op jit(solution)/shard_map/ppermute | solution.py:42
  82.8 1.0 collective-permute-start.36
  83.8 0.8 collective-permute-done.24.s1
  84.6 0.6 shard_map.87.own
  85.7 1.7 %collective-permute-done.36.b_got = f32[96,256]{1,0:T(8,128)S(1)} collective-permute-done((f32[96,256]{1,0:T(8,128)S(1)}, f32[96,256]{1,0:T(8,128)S(1)}, u32[]{:S(2)}, u32[]{:S(2)}) %collective-permute-start.36) | collective-permute-done | bytes 98336 | tf_op jit(solution)/shard_map/ppermute | solution.py:42
  87.4 0.6 shard_map.94.own
  88.1 1.2 %collective-permute-start.7 = (f32[64,512]{1,0:T(8,128)S(1)}, f32[64,512]{1,0:T(8,128)S(1)}, u32[]{:S(2)}, u32[]{:S(2)}) collective-permute-start(f32[64,512]{1,0:T(8,128)S(1)} %get-tuple-element.61), channel_id=1, source_target_pairs={{0,8},{4,12},{8,0},{12,4},{16,24},{20,28},{24,16},{28,20},{1,9},{5... | collective-permute-start | bytes 393224 | tf_op jit(solution)/shard_map/ppermute | solution.py:42
  89.3 1.0 collective-permute-start.8
  90.4 1.3 %collective-permute-start.9 = (f32[64,512]{1,0:T(8,128)S(1)}, f32[64,512]{1,0:T(8,128)S(1)}, u32[]{:S(2)}, u32[]{:S(2)}) collective-permute-start(f32[64,512]{1,0:T(8,128)S(1)} %get-tuple-element.63), channel_id=1, source_target_pairs={{0,24},{4,28},{8,16},{12,20},{16,8},{20,12},{24,0},{28,4},{1,25},{... | collective-permute-start | bytes 393224 | tf_op jit(solution)/shard_map/ppermute | solution.py:42
  91.7 2.0 %shard_map.79 = (f32[64,512]{1,0:T(8,128)S(1)}, f32[64,512]{1,0:T(8,128)S(1)}, f32[64,512]{1,0:T(8,128)S(1)}, f32[64,512]{1,0:T(8,128)S(1)}) custom-call(s32[2]{0:T(128)S(1)} %pad_add_fusion.ids.refs_0_, f32[256,512]{1,0:T(8,128)S(1)} %get-tuple-element.71.grad, bf16[256,512]{1,0:T(8,128)(2,1)S(1)} %get-tuple-element.72.gn_h, ...), custom_call_target="tpu_custom_call" | custom-call | tf_op jit(solution)/shard_map/pallas_call | solution.py:30
  93.7 0.9 collective-permute-done.7.p1
  94.5 1.2 %collective-permute-start.14 = (f32[64,512]{1,0:T(8,128)S(1)}, f32[64,512]{1,0:T(8,128)S(1)}, u32[]{:S(2)}, u32[]{:S(2)}) collective-permute-start(f32[64,512]{1,0:T(8,128)S(1)} %get-tuple-element.76), channel_id=1, source_target_pairs={{0,8},{4,12},{8,0},{12,4},{16,24},{20,28},{24,16},{28,20},{1,9},{5... | collective-permute-start | bytes 393224 | tf_op jit(solution)/shard_map/ppermute | solution.py:42
  95.7 2.3 %collective-permute-done.8.p2 = f32[64,512]{1,0:T(8,128)S(1)} collective-permute-done((f32[64,512]{1,0:T(8,128)S(1)}, f32[64,512]{1,0:T(8,128)S(1)}, u32[]{:S(2)}, u32[]{:S(2)}) %collective-permute-start.8) | collective-permute-done | bytes 131104 | tf_op jit(solution)/shard_map/ppermute | solution.py:42
  98.0 1.0 collective-permute-start.15
  99.5 1.4 %shard_map.76 = f32[256,512]{1,0:T(8,128)} custom-call(s32[2]{0:T(128)S(1)} %pad_add_fusion.ids.refs_0_, f32[64,512]{1,0:T(8,128)S(1)} %get-tuple-element.60.p0, f32[64,512]{1,0:T(8,128)S(1)} %collective-permute-done.7.p1, f32[64,512]{1,0:T(8,128)S(1)} %collective-permute-done.8.p2, f32[64,512]{1,0:T(8,128)S(1)} %collective-permute-done.9.p3), custom_call_target="tpu_custom_call" | custom-call | tf_op jit(solution)/shard_map/pallas_call | solution.py:30
  100.8 2.3 %collective-permute-done.15.p2 = f32[64,512]{1,0:T(8,128)S(1)} collective-permute-done((f32[64,512]{1,0:T(8,128)S(1)}, f32[64,512]{1,0:T(8,128)S(1)}, u32[]{:S(2)}, u32[]{:S(2)}) %collective-permute-start.15) | collective-permute-done | bytes 131104 | tf_op jit(solution)/shard_map/ppermute | solution.py:42
  103.1 1.7 %collective-permute-done.16.p3 = f32[64,512]{1,0:T(8,128)S(1)} collective-permute-done((f32[64,512]{1,0:T(8,128)S(1)}, f32[64,512]{1,0:T(8,128)S(1)}, u32[]{:S(2)}, u32[]{:S(2)}) %collective-permute-start.16) | collective-permute-done | bytes 131104 | tf_op jit(solution)/shard_map/ppermute | solution.py:42
  104.9 1.4 %shard_map.80 = f32[256,512]{1,0:T(8,128)} custom-call(s32[2]{0:T(128)S(1)} %pad_add_fusion.ids.refs_0_, f32[64,512]{1,0:T(8,128)S(1)} %get-tuple-element.75.p0, f32[64,512]{1,0:T(8,128)S(1)} %collective-permute-done.14.p1, f32[64,512]{1,0:T(8,128)S(1)} %collective-permute-done.15.p2, f32[64,512]{1,0:T(8,128)S(1)} %collective-permute-done.16.p3), custom_call_target="tpu_custom_call" | custom-call | tf_op jit(solution)/shard_map/pallas_call | solution.py:30
  106.3 1.5 %shard_map.88 = f32[384,512]{1,0:T(8,128)} custom-call(s32[2]{0:T(128)S(1)} %pad_add_fusion.ids.refs_0_, f32[384,256]{1,0:T(8,128)S(1)} %shard_map.87.own, f32[384,256]{1,0:T(8,128)S(1)} %collective-permute-done.27.got), custom_call_target="tpu_custom_call" | custom-call | tf_op jit(solution)/shard_map/pallas_call | solution.py:30
  107.7 1.5 %shard_map.95 = f32[384,512]{1,0:T(8,128)} custom-call(s32[2]{0:T(128)S(1)} %pad_add_fusion.ids.refs_0_, f32[384,256]{1,0:T(8,128)S(1)} %shard_map.94.own, f32[384,256]{1,0:T(8,128)S(1)} %collective-permute-done.37.got), custom_call_target="tpu_custom_call" | custom-call | tf_op jit(solution)/shard_map/pallas_call | solution.py:30
  (37 shorter events, 5.2 us)
Async XLA Ops:
  1.8 8.3 %collective-permute-start.2 = (f32[64,512]{1,0:T(8,128)S(1)}, f32[64,512]{1,0:T(8,128)S(1)}, u32[]{:S(2)}, u32[]{:S(2)}) collective-permute-start(f32[64,512]{1,0:T(8,128)S(1)} %get-tuple-element.112), channel_id=1, source_target_pairs={{0,24},{4,28},{8,16},{12,20},{16,8},{20,12},{24,0},{28,4},{1,25},{... | collective-permute-start | bytes 393224 | tf_op jit(solution)/shard_map/ppermute | solution.py:42
  5.8 6.6 %collective-permute-start = (f32[64,512]{1,0:T(8,128)S(1)}, f32[64,512]{1,0:T(8,128)S(1)}, u32[]{:S(2)}, u32[]{:S(2)}) collective-permute-start(f32[64,512]{1,0:T(8,128)S(1)} %get-tuple-element.113), channel_id=1, source_target_pairs={{0,8},{4,12},{8,0},{12,4},{16,24},{20,28},{24,16},{28,20},{1,9},{5... | collective-permute-start | bytes 393224 | tf_op jit(solution)/shard_map/ppermute | solution.py:42
  6.3 6.0 %collective-permute-start.1 = (f32[64,512]{1,0:T(8,128)S(1)}, f32[64,512]{1,0:T(8,128)S(1)}, u32[]{:S(2)}, u32[]{:S(2)}) collective-permute-start(f32[64,512]{1,0:T(8,128)S(1)} %get-tuple-element.115), channel_id=1, source_target_pairs={{0,16},{4,20},{8,24},{12,28},{16,0},{20,4},{24,8},{28,12},{1,17},{... | collective-permute-start | bytes 393224 | tf_op jit(solution)/shard_map/ppermute | solution.py:42
  6.4 8.4 %collective-permute-start.3 = (f32[64,512]{1,0:T(8,128)S(1)}, f32[64,512]{1,0:T(8,128)S(1)}, u32[]{:S(2)}, u32[]{:S(2)}) collective-permute-start(f32[64,512]{1,0:T(8,128)S(1)} %get-tuple-element.114.p0), channel_id=1, source_target_pairs={{0,4},{4,0},{8,12},{12,8},{16,20},{20,16},{24,28},{28,24},{1,5},{5... | collective-permute-start | bytes 393224 | tf_op jit(solution)/shard_map/ppermute | solution.py:42
  10.1 5.3 %collective-permute-start.6 = (f32[64,512]{1,0:T(8,128)S(1)}, f32[64,512]{1,0:T(8,128)S(1)}, u32[]{:S(2)}, u32[]{:S(2)}) collective-permute-start(f32[64,512]{1,0:T(8,128)S(1)} %collective-permute-done.2.p3), channel_id=1, source_target_pairs={{0,4},{4,0},{8,12},{12,8},{16,20},{20,16},{24,28},{28,24},{1,5},{5... | collective-permute-start | bytes 393224 | tf_op jit(solution)/shard_map/ppermute | solution.py:42
  12.3 7.6 %collective-permute-start.4 = (f32[64,512]{1,0:T(8,128)S(1)}, f32[64,512]{1,0:T(8,128)S(1)}, u32[]{:S(2)}, u32[]{:S(2)}) collective-permute-start(f32[64,512]{1,0:T(8,128)S(1)} %collective-permute-done.p1), channel_id=1, source_target_pairs={{0,4},{4,0},{8,12},{12,8},{16,20},{20,16},{24,28},{28,24},{1,5},{5... | collective-permute-start | bytes 393224 | tf_op jit(solution)/shard_map/ppermute | solution.py:42
  12.3 7.6 %collective-permute-start.5 = (f32[64,512]{1,0:T(8,128)S(1)}, f32[64,512]{1,0:T(8,128)S(1)}, u32[]{:S(2)}, u32[]{:S(2)}) collective-permute-start(f32[64,512]{1,0:T(8,128)S(1)} %collective-permute-done.1.p2), channel_id=1, source_target_pairs={{0,4},{4,0},{8,12},{12,8},{16,20},{20,16},{24,28},{28,24},{1,5},{5... | collective-permute-start | bytes 393224 | tf_op jit(solution)/shard_map/ppermute | solution.py:42
  12.9 10.8 %collective-permute-start.12 = (f32[64,512]{1,0:T(8,128)S(1)}, f32[64,512]{1,0:T(8,128)S(1)}, u32[]{:S(2)}, u32[]{:S(2)}) collective-permute-start(f32[64,512]{1,0:T(8,128)S(1)} %get-tuple-element.108), channel_id=1, source_target_pairs={{0,24},{4,28},{8,16},{12,20},{16,8},{20,12},{24,0},{28,4},{1,25},{... | collective-permute-start | bytes 393224 | tf_op jit(solution)/shard_map/ppermute | solution.py:42
  14.9 8.9 %collective-permute-start.10 = (f32[64,512]{1,0:T(8,128)S(1)}, f32[64,512]{1,0:T(8,128)S(1)}, u32[]{:S(2)}, u32[]{:S(2)}) collective-permute-start(f32[64,512]{1,0:T(8,128)S(1)} %get-tuple-element.109), channel_id=1, source_target_pairs={{0,8},{4,12},{8,0},{12,4},{16,24},{20,28},{24,16},{28,20},{1,9},{5... | collective-permute-start | bytes 393224 | tf_op jit(solution)/shard_map/ppermute | solution.py:42
  15.4 8.3 %collective-permute-start.11 = (f32[64,512]{1,0:T(8,128)S(1)}, f32[64,512]{1,0:T(8,128)S(1)}, u32[]{:S(2)}, u32[]{:S(2)}) collective-permute-start(f32[64,512]{1,0:T(8,128)S(1)} %get-tuple-element.111), channel_id=1, source_target_pairs={{0,16},{4,20},{8,24},{12,28},{16,0},{20,4},{24,8},{28,12},{1,17},{... | collective-permute-start | bytes 393224 | tf_op jit(solution)/shard_map/ppermute | solution.py:42
  25.2 4.2 %collective-permute-start.28 = (f32[1536,256]{1,0:T(8,128)S(1)}, f32[1536,256]{1,0:T(8,128)S(1)}, u32[]{:S(2)}, u32[]{:S(2)}) collective-permute-start(f32[1536,256]{1,0:T(8,128)S(1)} %get-tuple-element.95), channel_id=1, source_target_pairs={{0,4},{4,0},{8,12},{12,8},{16,20},{20,16},{24,28},{28,24},{1,5},{5... | collective-permute-start | bytes 4718600 | tf_op jit(solution)/shard_map/ppermute | solution.py:42
  28.8 4.7 %collective-permute-start.17 = (f32[1536,256]{1,0:T(8,128)S(1)}, f32[1536,256]{1,0:T(8,128)S(1)}, u32[]{:S(2)}, u32[]{:S(2)}) collective-permute-start(f32[1536,256]{1,0:T(8,128)S(1)} %shard_map.81), channel_id=1, source_target_pairs={{0,4},{4,0},{8,12},{12,8},{16,20},{20,16},{24,28},{28,24},{1,5},{5... | collective-permute-start | bytes 4718600 | tf_op jit(solution)/shard_map/ppermute | solution.py:42
  31.0 12.1 %collective-permute-start.29 = (f32[4,96,256]{2,1,0:T(8,128)S(1)}, f32[4,96,256]{2,1,0:T(8,128)S(1)}, u32[]{:S(2)}, u32[]{:S(2)}) collective-permute-start(f32[4,96,256]{2,1,0:T(8,128)S(1)} %get-tuple-element.97), channel_id=1, source_target_pairs={{0,8},{4,12},{8,0},{12,4},{16,24},{20,28},{24,16},{28,20},{1,9},{5... | collective-permute-start | bytes 1179656 | tf_op jit(solution)/shard_map/ppermute | solution.py:42
  32.5 12.0 %collective-permute-start.30 = (f32[4,96,256]{2,1,0:T(8,128)S(1)}, f32[4,96,256]{2,1,0:T(8,128)S(1)}, u32[]{:S(2)}, u32[]{:S(2)}) collective-permute-start(f32[4,96,256]{2,1,0:T(8,128)S(1)} %get-tuple-element.99), channel_id=1, source_target_pairs={{0,16},{4,20},{8,24},{12,28},{16,0},{20,4},{24,8},{28,12},{1,17},{... | collective-permute-start | bytes 1179656 | tf_op jit(solution)/shard_map/ppermute | solution.py:42
  35.1 15.4 %collective-permute-start.18 = (f32[4,96,256]{2,1,0:T(8,128)S(1)}, f32[4,96,256]{2,1,0:T(8,128)S(1)}, u32[]{:S(2)}, u32[]{:S(2)}) collective-permute-start(f32[4,96,256]{2,1,0:T(8,128)S(1)} %get-tuple-element.84), channel_id=1, source_target_pairs={{0,8},{4,12},{8,0},{12,4},{16,24},{20,28},{24,16},{28,20},{1,9},{5... | collective-permute-start | bytes 1179656 | tf_op jit(solution)/shard_map/ppermute | solution.py:42
  35.7 16.0 %collective-permute-start.19 = (f32[4,96,256]{2,1,0:T(8,128)S(1)}, f32[4,96,256]{2,1,0:T(8,128)S(1)}, u32[]{:S(2)}, u32[]{:S(2)}) collective-permute-start(f32[4,96,256]{2,1,0:T(8,128)S(1)} %get-tuple-element.86), channel_id=1, source_target_pairs={{0,16},{4,20},{8,24},{12,28},{16,0},{20,4},{24,8},{28,12},{1,17},{... | collective-permute-start | bytes 1179656 | tf_op jit(solution)/shard_map/ppermute | solution.py:42
  45.1 16.3 %collective-permute-start.31 = (f32[2,2,96,256]{3,2,1,0:T(8,128)S(1)}, f32[2,2,96,256]{3,2,1,0:T(8,128)S(1)}, u32[]{:S(2)}, u32[]{:S(2)}) collective-permute-start(f32[2,2,96,256]{3,2,1,0:T(8,128)S(1)} %get-tuple-element.101), channel_id=1, source_target_pairs={{0,1},{1,0},{2,3},{3,2},{4,5},{5,4},{6,7},{7,6},{8,9},{9,8},{10,11... | collective-permute-start | bytes 1179656 | tf_op jit(solution)/shard_map/ppermute | solution.py:42
  52.3 5.8 %collective-permute-start.20 = (f32[4,48,256]{2,1,0:T(8,128)S(1)}, f32[4,48,256]{2,1,0:T(8,128)S(1)}, u32[]{:S(2)}, u32[]{:S(2)}) collective-permute-start(f32[4,48,256]{2,1,0:T(8,128)S(1)} %get-tuple-element.88), channel_id=1, source_target_pairs={{0,16},{4,20},{8,24},{12,28},{16,0},{20,4},{24,8},{28,12},{1,17},{... | collective-permute-start | bytes 589832 | tf_op jit(solution)/shard_map/ppermute | solution.py:42
  53.5 5.7 %collective-permute-start.21 = (f32[4,48,256]{2,1,0:T(8,128)S(1)}, f32[4,48,256]{2,1,0:T(8,128)S(1)}, u32[]{:S(2)}, u32[]{:S(2)}) collective-permute-start(f32[4,48,256]{2,1,0:T(8,128)S(1)} %get-tuple-element.90), channel_id=1, source_target_pairs={{0,8},{4,12},{8,0},{12,4},{16,24},{20,28},{24,16},{28,20},{1,9},{5... | collective-permute-start | bytes 589832 | tf_op jit(solution)/shard_map/ppermute | solution.py:42
  59.7 7.7 %collective-permute-start.22 = (f32[2,2,48,256]{3,2,1,0:T(8,128)S(1)}, f32[2,2,48,256]{3,2,1,0:T(8,128)S(1)}, u32[]{:S(2)}, u32[]{:S(2)}) collective-permute-start(f32[2,2,48,256]{3,2,1,0:T(8,128)S(1)} %get-tuple-element.92), channel_id=1, source_target_pairs={{0,1},{1,0},{2,3},{3,2},{4,5},{5,4},{6,7},{7,6},{8,9},{9,8},{10,11... | collective-permute-start | bytes 589832 | tf_op jit(solution)/shard_map/ppermute | solution.py:42
  62.0 11.2 %collective-permute-start.32 = (f32[2,96,256]{2,1,0:T(8,128)S(1)}, f32[2,96,256]{2,1,0:T(8,128)S(1)}, u32[]{:S(2)}, u32[]{:S(2)}) collective-permute-start(f32[2,96,256]{2,1,0:T(8,128)S(1)} %get-tuple-element.103), channel_id=1, source_target_pairs={{0,2},{1,3},{2,0},{3,1},{4,6},{5,7},{6,4},{7,5},{8,10},{9,11},{10,... | collective-permute-start | bytes 589832 | tf_op jit(solution)/shard_map/ppermute | solution.py:42
  64.6 25.8 %collective-permute-start.13 = (f32[256,512]{1,0:T(8,128)S(1)}, f32[256,512]{1,0:T(8,128)S(1)}, u32[]{:S(2)}, u32[]{:S(2)}) collective-permute-start(f32[256,512]{1,0:T(8,128)S(1)} %get-tuple-element.74), channel_id=1, source_target_pairs={{0,4},{4,0},{8,12},{12,8},{16,20},{20,16},{24,28},{28,24},{1,5},{5... | collective-permute-start | bytes 1572872 | tf_op jit(solution)/shard_map/ppermute | solution.py:42
  68.0 7.6 %collective-permute-start.23 = (f32[2,48,256]{2,1,0:T(8,128)S(1)}, f32[2,48,256]{2,1,0:T(8,128)S(1)}, u32[]{:S(2)}, u32[]{:S(2)}) collective-permute-start(f32[2,48,256]{2,1,0:T(8,128)S(1)} %get-tuple-element.94), channel_id=1, source_target_pairs={{0,2},{1,3},{2,0},{3,1},{4,6},{5,7},{6,4},{7,5},{8,10},{9,11},{10,... | collective-permute-start | bytes 294920 | tf_op jit(solution)/shard_map/ppermute | solution.py:42
  73.7 5.2 %collective-permute-start.33 = (f32[96,256]{1,0:T(8,128)S(1)}, f32[96,256]{1,0:T(8,128)S(1)}, u32[]{:S(2)}, u32[]{:S(2)}) collective-permute-start(f32[96,256]{1,0:T(8,128)S(1)} %get-tuple-element.104.a), channel_id=1, source_target_pairs={{0,16},{4,20},{8,24},{12,28},{16,0},{20,4},{24,8},{28,12},{1,17},{... | collective-permute-start | bytes 294920 | tf_op jit(solution)/shard_map/ppermute | solution.py:42
  74.8 5.3 %collective-permute-start.34 = (f32[96,256]{1,0:T(8,128)S(1)}, f32[96,256]{1,0:T(8,128)S(1)}, u32[]{:S(2)}, u32[]{:S(2)}) collective-permute-start(f32[96,256]{1,0:T(8,128)S(1)} %get-tuple-element.105.b), channel_id=1, source_target_pairs={{0,8},{4,12},{8,0},{12,4},{16,24},{20,28},{24,16},{28,20},{1,9},{5... | collective-permute-start | bytes 294920 | tf_op jit(solution)/shard_map/ppermute | solution.py:42
  76.2 6.6 %collective-permute-start.26 = (f32[2,48,256]{2,1,0:T(8,128)S(1)}, f32[2,48,256]{2,1,0:T(8,128)S(1)}, u32[]{:S(2)}, u32[]{:S(2)}) collective-permute-start(f32[2,48,256]{2,1,0:T(8,128)S(1)} %shard_map.86.s0), channel_id=1, source_target_pairs={{0,24},{4,28},{8,16},{12,20},{16,8},{20,12},{24,0},{28,4},{1,25},{... | collective-permute-start | bytes 294920 | tf_op jit(solution)/shard_map/ppermute | solution.py:42
  77.9 5.9 %collective-permute-start.25 = (f32[2,48,256]{2,1,0:T(8,128)S(1)}, f32[2,48,256]{2,1,0:T(8,128)S(1)}, u32[]{:S(2)}, u32[]{:S(2)}) collective-permute-start(f32[2,48,256]{2,1,0:T(8,128)S(1)} %shard_map.86.s0), channel_id=1, source_target_pairs={{0,16},{4,20},{8,24},{12,28},{16,0},{20,4},{24,8},{28,12},{1,17},{... | collective-permute-start | bytes 294920 | tf_op jit(solution)/shard_map/ppermute | solution.py:42
  78.9 5.7 %collective-permute-start.24 = (f32[2,48,256]{2,1,0:T(8,128)S(1)}, f32[2,48,256]{2,1,0:T(8,128)S(1)}, u32[]{:S(2)}, u32[]{:S(2)}) collective-permute-start(f32[2,48,256]{2,1,0:T(8,128)S(1)} %shard_map.86.s0), channel_id=1, source_target_pairs={{0,8},{4,12},{8,0},{12,4},{16,24},{20,28},{24,16},{28,20},{1,9},{5... | collective-permute-start | bytes 294920 | tf_op jit(solution)/shard_map/ppermute | solution.py:42
  80.7 5.1 %collective-permute-start.35 = (f32[96,256]{1,0:T(8,128)S(1)}, f32[96,256]{1,0:T(8,128)S(1)}, u32[]{:S(2)}, u32[]{:S(2)}) collective-permute-start(f32[96,256]{1,0:T(8,128)S(1)} %get-tuple-element.106.a), channel_id=1, source_target_pairs={{0,8},{4,12},{8,0},{12,4},{16,24},{20,28},{24,16},{28,20},{1,9},{5... | collective-permute-start | bytes 294920 | tf_op jit(solution)/shard_map/ppermute | solution.py:42
  82.8 4.6 %collective-permute-start.36 = (f32[96,256]{1,0:T(8,128)S(1)}, f32[96,256]{1,0:T(8,128)S(1)}, u32[]{:S(2)}, u32[]{:S(2)}) collective-permute-start(f32[96,256]{1,0:T(8,128)S(1)} %get-tuple-element.107.b), channel_id=1, source_target_pairs={{0,16},{4,20},{8,24},{12,28},{16,0},{20,4},{24,8},{28,12},{1,17},{... | collective-permute-start | bytes 294920 | tf_op jit(solution)/shard_map/ppermute | solution.py:42
  85.1 21.1 %collective-permute-start.27 = (f32[384,256]{1,0:T(8,128)S(1)}, f32[384,256]{1,0:T(8,128)S(1)}, u32[]{:S(2)}, u32[]{:S(2)}) collective-permute-start(f32[384,256]{1,0:T(8,128)S(1)} %shard_map.87.own), channel_id=1, source_target_pairs={{0,4},{4,0},{8,12},{12,8},{16,20},{20,16},{24,28},{28,24},{1,5},{5... | collective-permute-start | bytes 1179656 | tf_op jit(solution)/shard_map/ppermute | solution.py:42
  88.0 19.7 %collective-permute-start.37 = (f32[384,256]{1,0:T(8,128)S(1)}, f32[384,256]{1,0:T(8,128)S(1)}, u32[]{:S(2)}, u32[]{:S(2)}) collective-permute-start(f32[384,256]{1,0:T(8,128)S(1)} %shard_map.94.own), channel_id=1, source_target_pairs={{0,4},{4,0},{8,12},{12,8},{16,20},{20,16},{24,28},{28,24},{1,5},{5... | collective-permute-start | bytes 1179656 | tf_op jit(solution)/shard_map/ppermute | solution.py:42
  88.1 6.4 %collective-permute-start.7 = (f32[64,512]{1,0:T(8,128)S(1)}, f32[64,512]{1,0:T(8,128)S(1)}, u32[]{:S(2)}, u32[]{:S(2)}) collective-permute-start(f32[64,512]{1,0:T(8,128)S(1)} %get-tuple-element.61), channel_id=1, source_target_pairs={{0,8},{4,12},{8,0},{12,4},{16,24},{20,28},{24,16},{28,20},{1,9},{5... | collective-permute-start | bytes 393224 | tf_op jit(solution)/shard_map/ppermute | solution.py:42
  89.3 8.6 %collective-permute-start.8 = (f32[64,512]{1,0:T(8,128)S(1)}, f32[64,512]{1,0:T(8,128)S(1)}, u32[]{:S(2)}, u32[]{:S(2)}) collective-permute-start(f32[64,512]{1,0:T(8,128)S(1)} %get-tuple-element.62), channel_id=1, source_target_pairs={{0,16},{4,20},{8,24},{12,28},{16,0},{20,4},{24,8},{28,12},{1,17},{... | collective-permute-start | bytes 393224 | tf_op jit(solution)/shard_map/ppermute | solution.py:42
  90.4 8.6 %collective-permute-start.9 = (f32[64,512]{1,0:T(8,128)S(1)}, f32[64,512]{1,0:T(8,128)S(1)}, u32[]{:S(2)}, u32[]{:S(2)}) collective-permute-start(f32[64,512]{1,0:T(8,128)S(1)} %get-tuple-element.63), channel_id=1, source_target_pairs={{0,24},{4,28},{8,16},{12,20},{16,8},{20,12},{24,0},{28,4},{1,25},{... | collective-permute-start | bytes 393224 | tf_op jit(solution)/shard_map/ppermute | solution.py:42
  94.5 6.3 %collective-permute-start.14 = (f32[64,512]{1,0:T(8,128)S(1)}, f32[64,512]{1,0:T(8,128)S(1)}, u32[]{:S(2)}, u32[]{:S(2)}) collective-permute-start(f32[64,512]{1,0:T(8,128)S(1)} %get-tuple-element.76), channel_id=1, source_target_pairs={{0,8},{4,12},{8,0},{12,4},{16,24},{20,28},{24,16},{28,20},{1,9},{5... | collective-permute-start | bytes 393224 | tf_op jit(solution)/shard_map/ppermute | solution.py:42
  98.0 5.2 %collective-permute-start.15 = (f32[64,512]{1,0:T(8,128)S(1)}, f32[64,512]{1,0:T(8,128)S(1)}, u32[]{:S(2)}, u32[]{:S(2)}) collective-permute-start(f32[64,512]{1,0:T(8,128)S(1)} %get-tuple-element.77), channel_id=1, source_target_pairs={{0,16},{4,20},{8,24},{12,28},{16,0},{20,4},{24,8},{28,12},{1,17},{... | collective-permute-start | bytes 393224 | tf_op jit(solution)/shard_map/ppermute | solution.py:42
  99.0 5.9 %collective-permute-start.16 = (f32[64,512]{1,0:T(8,128)S(1)}, f32[64,512]{1,0:T(8,128)S(1)}, u32[]{:S(2)}, u32[]{:S(2)}) collective-permute-start(f32[64,512]{1,0:T(8,128)S(1)} %get-tuple-element.78), channel_id=1, source_target_pairs={{0,24},{4,28},{8,16},{12,20},{16,8},{20,12},{24,0},{28,4},{1,25},{... | collective-permute-start | bytes 393224 | tf_op jit(solution)/shard_map/ppermute | solution.py:42
where the time goes:
time: 109 us
  waiting for transfers between devices  40.9 us (38%)
  starting transfers between devices  36.2 us (33%)
  Pallas kernels  28.9 us (27%)
  local copies, waits for them, and re-layouts  2.27 us (2%)
    ppermute x38, waiting for transfers between devices, swap(): return lax.ppermute(value, axis, [(i, i ^ mask) for i in range(count)])  40.9 us
    ppermute x38, starting transfers between devices, swap(): return lax.ppermute(value, axis, [(i, i ^ mask) for i in range(count)])  36.2 us
    pallas_call x21, Pallas kernels, call(): pl.pallas_call(body, out_shape=[make(shape, dtype) for shape, dtype in ou...  25.3 us
    pallas_call x1, Pallas kernels, split_weights(): pl.pallas_call(weights_body, out_shape=[pltpu.VMEM((rows, width), BF16)]...  3.54 us
    dynamic_slice x2, local copies, waits for them, and re-layouts, pieces(): lax.dynamic_slice_in_dim(field, (chip ^ mask) * size, size, 0)  2.27 us
  transfers between devices with their start and end apart: 38, of which 20 were waited for; matrix products, arithmetic and copies ran while one was open for 1% of the time, Pallas kernels for 24%

commit v1 on v0

v1 whole, which is shorter than its diff:
```python
import jax
import jax.numpy as jnp
from jax import lax
from jax.experimental import pallas as pl
from jax.experimental.pallas import tpu as pltpu
from jax.sharding import PartitionSpec as P


NEAR_STEPS = 4
FAR_STEPS = 2
HP = lax.Precision.HIGH
F32 = jnp.float32
BF16 = jnp.bfloat16


def dot(a, b, contract):
    return lax.dot_general(
        a, b, ((contract[:1], contract[1:]), ((), ())), precision=HP, preferred_element_type=jnp.float32
    )


def gelu_fn(value):
    return jax.nn.gelu(value, approximate=True)


def call(body, outs, ids, *args, scratch=(), to_hbm=False, room=4):
    vmem = pl.BlockSpec(memory_space=pltpu.VMEM)
    smem = pl.BlockSpec(memory_space=pltpu.SMEM)
    make = jax.ShapeDtypeStruct if to_hbm else pltpu.VMEM
    return pl.pallas_call(
        body,
        out_shape=[make(shape, dtype) for shape, dtype in outs],
        in_specs=[smem] + [vmem] * len(args),
        out_specs=[vmem] * len(outs),
        scratch_shapes=[pltpu.VMEM(shape, dtype) for shape, dtype in scratch],
        compiler_params=pltpu.CompilerParams(vmem_limit_bytes=room * 1024 * 1024),
    )(ids, *[pltpu.with_memory_space_constraint(arg, pltpu.VMEM) for arg in args])


def swap(value, axis, mask):
    count = lax.axis_size(axis)
    return lax.ppermute(value, axis, [(i, i ^ mask) for i in range(count)])


def plane_swap(value, turn):
    count = lax.axis_size("hi")
    return lax.ppermute(value, "hi", [(i, i ^ (2 << (i + turn) % 2)) for i in range(count)])


def bits(ids):
    hi, lo = ids[0], ids[1]
    return hi & 1, hi >> 1, lo


def turns(core, chip):
    return (chip >> core) & 1, (chip >> (1 - core)) & 1


def split(value):
    high = value.astype(BF16)
    return high, (value - high.astype(F32)).astype(BF16)


def mul(a, b, contract):
    dims = ((contract[:1], contract[1:]), ((), ()))

    def one(left, right):
        return lax.dot_general(left, right, dims, preferred_element_type=F32)

    return one(a[0], b[0]) + (one(a[0], b[1]) + one(a[1], b[0]))


def rows_of(pair, start, size):
    return tuple(ref[start : start + size] for ref in pair)


def gelu_both(u):
    root = 0.7978845608028654
    square = u * u
    tanh = jnp.tanh(root * (u + 0.044715 * (u * square)))
    half = 0.5 * (1.0 + tanh)
    slope = half + 0.5 * u * (1.0 - tanh * tanh) * (root * (1.0 + 3.0 * 0.044715 * square))
    return u * half, slope


def block(index, size):
    return pl.ds(pl.multiple_of(index * size, size), size)


def weights_body(ids, near, far, cot, near_h, near_l, far_h, far_l, c0, c1, c2, c3, staged, done, moved):
    chip = bits(ids)[1]
    parts, rows, _ = staged.shape
    each = parts // 2
    size = c0.shape[0]
    cuts = [
        pltpu.make_async_copy(cot.at[block(chip ^ mask, size)], out, moved.at[mask])
        for mask, out in enumerate((c0, c1, c2, c3))
    ]
    copies = [
        pltpu.make_async_copy((near, far)[k // each].at[pl.ds(k % each * rows, rows)], staged.at[k], done.at[k])
        for k in range(parts)
    ]
    for copy in copies[:each] + cuts + copies[each:]:
        copy.start()
    for k in range(parts):
        copies[k].wait()
        start = k % each * rows
        high, low = ((near_h, near_l), (far_h, far_l))[k // each]
        high[start : start + rows], low[start : start + rows] = split(staged[k])
    for copy in cuts:
        copy.wait()


def hbm_call(body, outs, specs, ids, args, scratch, room):
    smem = pl.BlockSpec(memory_space=pltpu.SMEM)
    places = {pltpu.HBM: pl.BlockSpec(memory_space=pltpu.HBM), pltpu.VMEM: pl.BlockSpec(memory_space=pltpu.VMEM)}
    ins, out_place = specs
    return pl.pallas_call(
        body,
        out_shape=[out_place(shape, dtype) for shape, dtype in outs],
        in_specs=[smem] + [places[ins]] * len(args),
        out_specs=[places[out_place]] * len(outs),
        scratch_shapes=scratch,
        compiler_params=pltpu.CompilerParams(vmem_limit_bytes=room * 1024 * 1024),
    )(ids, *[pltpu.with_memory_space_constraint(arg, ins) for arg in args])


def forward_body(ids, p0, p1, p2, p3, q0, q1, q2, q3, near_h, near_l, far_h, far_l,
                 f0, f1, f2, f3, slope_near, slope_far, hid_h, hid_l, own_h, own_l, oth_h, oth_l, field):
    core, chip, _ = bits(ids)
    rows, width = slope_near.shape
    size = rows // 4
    pad = jnp.zeros((size, width), BF16)
    for ref in (own_h, own_l, oth_h, oth_l):
        ref[0:size] = pad
        ref[rows + size :] = pad
    for mask, (own, other) in enumerate(((p0, q0), (p1, q1), (p2, q2), (p3, q3))):
        field[block(chip ^ mask, size)] = own[...]
        high, low = split(other[...])
        oth_h[block((chip ^ mask) + 1, size)] = high
        oth_l[block((chip ^ mask) + 1, size)] = low
    track = field[...]
    own_h[size : rows + size], own_l[size : rows + size] = split(track)
    before = pl.ds(pl.multiple_of(core * size, size), rows)
    after = pl.ds(pl.multiple_of(core * size + size, size), rows)
    pre = mul(rows_of((own_h, own_l), size, rows), rows_of((near_h, near_l), width, width), (1, 0))
    pre = pre + mul((oth_h[before], oth_l[before]), rows_of((near_h, near_l), 0, width), (1, 0))
    pre = pre + mul((oth_h[after], oth_l[after]), rows_of((near_h, near_l), 2 * width, width), (1, 0))
    act, slope = gelu_both(pre)
    slope_near[...] = slope
    hidden = track + act
    hid_h[...], hid_l[...] = split(hidden)
    field[...] = mul((hid_h[...], hid_l[...]), rows_of((far_h, far_l), width, width), (1, 0))
    rest = rows - size
    field[size:] += mul(rows_of((hid_h, hid_l), 0, rest), rows_of((far_h, far_l), 0, width), (1, 0))
    field[0:rest] += mul(rows_of((hid_h, hid_l), size, rest), rows_of((far_h, far_l), 2 * width, width), (1, 0))
    act, slope = gelu_both(field[...])
    slope_far[...] = slope
    field[...] = hidden + act
    for mask, out in enumerate((f0, f1, f2, f3)):
        out[...] = field[block(chip ^ mask, size)]


def half_columns(pair, index):
    width = pair[0].shape[1] // 2
    return tuple(jnp.where(index == 0, ref[:, :width].astype(F32), ref[:, width:].astype(F32)).astype(BF16) for ref in pair)


def far_term(hid, grad, store):
    rows, _ = hid[0].shape
    size = rows // 4
    rest = rows - size
    store(0, mul(rows_of(hid, 0, rest), tuple(g[size:] for g in grad), (0, 0)))
    store(1, mul(tuple(h[...] for h in hid), grad, (0, 0)))
    store(2, mul(rows_of(hid, size, rest), tuple(g[:rest] for g in grad), (0, 0)))


def near_term(core, center, sides, grad, store):
    rows = grad[0].shape[0]
    size = rows // 4
    before = pl.ds(pl.multiple_of(core * size, size), rows)
    after = pl.ds(pl.multiple_of(core * size + size, size), rows)
    store(0, mul(tuple(ref[before] for ref in sides), grad, (0, 0)))
    store(1, mul(rows_of(center, size, rows), grad, (0, 0)))
    store(2, mul(tuple(ref[after] for ref in sides), grad, (0, 0)))


def far_other_body(ids, c0, c1, c2, c3, slope, hid_h, hid_l, cot, g_h, g_l, term):
    core, chip, _ = bits(ids)
    rows, width = cot.shape
    size = rows // 4
    for mask, piece in enumerate((c0, c1, c2, c3)):
        cot[block(chip ^ mask, size)] = piece[...]
    g_h[...], g_l[...] = split(cot[...] * slope[...])

    def store(tap, value):
        term[tap * width : (tap + 1) * width] = value

    far_term((hid_h, hid_l), half_columns((g_h, g_l), 1 - core), store)


def halve(total, bit, keep, send):
    count, half, _ = keep.shape
    for z in range(count):
        keep[z] = total[pl.ds(pl.multiple_of((2 * z + bit) * half, 32), half)]
        send[z] = total[pl.ds(pl.multiple_of((2 * z + 1 - bit) * half, 32), half)]


def far_own_body(ids, hid_h, hid_l, g_h, g_l, got, keep, send, total):
    core, chip, _ = bits(ids)
    width = hid_h.shape[1]

    def store(tap, value):
        total[tap * width : (tap + 1) * width] = value + got[tap * width : (tap + 1) * width]

    far_term((hid_h, hid_l), half_columns((g_h, g_l), core), store)
    halve(total, turns(core, chip)[0], keep, send)


def backward_body(ids, cot, g_h, g_l, far_h, far_l, slope, grad, gn, gn_h, gn_l):
    rows, width = cot.shape
    size = rows // 4
    rest = rows - size
    grad[...] = cot[...] + mul((g_h[...], g_l[...]), rows_of((far_h, far_l), width, width), (1, 1))
    grad[0:rest] += mul(rows_of((g_h, g_l), size, rest), rows_of((far_h, far_l), 0, width), (1, 1))
    grad[size:] += mul(rows_of((g_h, g_l), 0, rest), rows_of((far_h, far_l), 2 * width, width), (1, 1))
    value = grad[...] * slope[...]
    gn[...] = value
    gn_h[...], gn_l[...] = split(value)


def near_mine_body(ids, own_h, own_l, oth_h, oth_l, gn_h, gn_l, term):
    core, _, _ = bits(ids)
    width = own_h.shape[1]

    def store(tap, value):
        term[tap * width : (tap + 1) * width] = value

    near_term(core, (own_h, own_l), (oth_h, oth_l), half_columns((gn_h, gn_l), core), store)


def near_both_body(ids, term, own_h, own_l, oth_h, oth_l, other, keep, send, total):
    core, chip, _ = bits(ids)
    width = own_h.shape[1]
    half = width // 2

    def store(tap, value):
        total[tap * width : (tap + 1) * width] = value + term[tap * width : (tap + 1) * width]

    grad = split(jnp.where(core == 0, other[:, :half], other[:, half:]))
    near_term(1 - core, (oth_h, oth_l), (own_h, own_l), grad, store)
    halve(total, turns(core, chip)[0], keep, send)


def track_body(ids, grad, gn_h, gn_l, other, near_h, near_l, t0, t1, t2, t3, oth_h, oth_l, field):
    core, chip, _ = bits(ids)
    rows, width = grad.shape
    size = rows // 4
    pad = jnp.zeros((size, width), BF16)
    for ref in (oth_h, oth_l):
        ref[0:size] = pad
        ref[rows + size :] = pad
    high, low = split(other[...])
    oth_h[size : rows + size] = high
    oth_l[size : rows + size] = low
    before = pl.ds(pl.multiple_of(core * size, size), rows)
    after = pl.ds(pl.multiple_of(core * size + size, size), rows)
    total = grad[...] + mul((gn_h[...], gn_l[...]), rows_of((near_h, near_l), width, width), (1, 1))
    total = total + mul((oth_h[after], oth_l[after]), rows_of((near_h, near_l), 0, width), (1, 1))
    field[...] = total + mul((oth_h[before], oth_l[before]), rows_of((near_h, near_l), 2 * width, width), (1, 1))
    for mask, out in enumerate((t0, t1, t2, t3)):
        out[...] = field[block(chip ^ mask, size)]


def plane_body(ids, kept, got, keep, send):
    core, chip, _ = bits(ids)
    bit = turns(core, chip)[1]
    half = keep.shape[1]
    mine = pl.ds(pl.multiple_of(bit * half, 32), half)
    theirs = pl.ds(pl.multiple_of((1 - bit) * half, 32), half)
    keep[...] = kept[:, mine] + got[:, mine]
    send[...] = kept[:, theirs] + got[:, theirs]


def pick_body(ids, kept, got, p0, p1, p2, p3):
    lo = bits(ids)[2]
    for mask, out in enumerate((p0, p1, p2, p3)):
        out[...] = kept[lo ^ mask] + got[lo ^ mask]


def total_body(scale, ids, p0, p1, p2, p3, out):
    out[...] = ((p0[...] + p1[...]) + (p2[...] + p3[...])) * scale


def cross_body(ids, own, got, out):
    out[...] = own[...] + got[...]


def far_rows_body(ids, own, got, out):
    core, chip, _ = bits(ids)
    bit = turns(core, chip)[0]
    half = own.shape[0]
    out[pl.ds(pl.multiple_of(bit * half, 32), half)] = own[...]
    out[pl.ds(pl.multiple_of((1 - bit) * half, 32), half)] = got[...]


def near_rows_body(ids, s0, s1, s2, s3, out):
    core, chip, _ = bits(ids)
    size = s0.shape[0]
    for mask, piece in enumerate((s0, s1, s2, s3)):
        first, second = turns(core, chip ^ mask)
        out[pl.ds(pl.multiple_of((2 * first + second) * size, 32), size)] = piece[...]


def run_copies(copies):
    for copy in copies:
        copy.start()
    for copy in copies:
        copy.wait()


def place_columns(core, own, got, out, done, others=()):
    width = own.shape[1]

    def place(left, right):
        run_copies(
            [
                pltpu.make_async_copy(part, out.at[:, pl.ds(k * width, width)], done.at[k])
                for k, part in enumerate((left, right))
            ]
            + list(others)
        )

    @pl.when(core == 0)
    def _():
        place(own, got)

    @pl.when(core != 0)
    def _():
        place(got, own)


def columns_body(ids, own, got, out, done):
    place_columns(bits(ids)[0], own, got, out, done)


def collect_body(ids, f0, f1, f2, f3, g0, g1, g2, g3, own, got, features, grads, out, done, moved):
    core, chip, _ = bits(ids)
    size = f0.shape[0]
    copies = [
        pltpu.make_async_copy(piece, to.at[block(chip ^ mask, size)], moved.at[4 * k + mask])
        for k, (to, parts) in enumerate(((features, (f0, f1, f2, f3)), (grads, (g0, g1, g2, g3))))
        for mask, piece in enumerate(parts)
    ]
    place_columns(core, own, got, out, done, copies)


def pieces(field, chip):
    size = field.shape[0] // 4
    return [lax.dynamic_slice_in_dim(field, (chip ^ mask) * size, size, 0) for mask in range(4)]


def over_chips(parts):
    return [parts[0]] + [swap(parts[mask], "hi", 2 * mask) for mask in range(1, 4)]


def family_shards(track, near_weight, far_weight, cotangent):
    return family_step(track, near_weight, far_weight, cotangent)


def family_step(track, near_weight, far_weight, cotangent):
    rows, width = track.shape
    n_hi = lax.axis_size("hi")
    n_lo = lax.axis_size("lo")
    size = rows // 4
    half = width // 2
    tall = near_weight.shape[0]
    part = tall // n_lo
    hi = lax.axis_index("hi")
    lo = lax.axis_index("lo")
    ids = jnp.stack([hi, lo])
    chip = lax.shift_right_logical(hi, 1)
    scale = 1.0 / float(rows * n_hi * n_lo) ** 0.5
    full, piece = (rows, width), (size, width)
    padded = (rows + 2 * size, width)

    own = over_chips(pieces(track, chip))
    other = [swap(own[mask], "hi", 1) for mask in range(4)]
    out = hbm_call(
        weights_body, [(near_weight.shape, BF16)] * 4 + [(piece, F32)] * 4, (pltpu.HBM, pltpu.VMEM),
        ids, (near_weight, far_weight, cotangent),
        [pltpu.VMEM((8, tall // 4, width), F32), pltpu.SemaphoreType.DMA((8,)), pltpu.SemaphoreType.DMA((4,))], 8,
    )
    near_h, near_l, far_h, far_l = out[:4]
    cot = over_chips(out[4:])
    near_w, far_w = (near_h, near_l), (far_h, far_l)
    out = call(
        forward_body,
        [(piece, F32)] * 4 + [(full, F32)] * 2 + [(full, BF16)] * 2 + [(padded, BF16)] * 4,
        ids, *own, *other, *near_w, *far_w, scratch=[(full, F32)], room=16,
    )
    feats, slope_near, slope_far = over_chips(out[:4]), out[4], out[5]
    hid, own_pair, oth_pair = out[6:8], out[8:10], out[10:12]
    cot, g_h, g_l, far_other = call(
        far_other_body, [(full, F32), (full, BF16), (full, BF16), ((tall, half), F32)],
        ids, *cot, slope_far, *hid,
    )
    far_got = swap(far_other, "hi", 1)
    halves = [((n_lo, part // 2, half), F32)] * 2
    far_keep, far_send = call(
        far_own_body, halves, ids, *hid, g_h, g_l, far_got, scratch=[((tall, half), F32)], room=12
    )
    far_got = plane_swap(far_send, 0)
    grad, gn, gn_h, gn_l = call(
        backward_body, [(full, F32), (full, F32), (full, BF16), (full, BF16)],
        ids, cot, g_h, g_l, *far_w, slope_near,
    )
    gn_got = swap(gn, "hi", 1)
    (near_term,) = call(near_mine_body, [((tall, half), F32)], ids, *own_pair, *oth_pair, gn_h, gn_l)
    near_keep, near_send = call(
        near_both_body, halves, ids, near_term, *own_pair, *oth_pair, gn_got,
        scratch=[((tall, half), F32)], room=12,
    )
    near_got = plane_swap(near_send, 0)
    grads = call(
        track_body, [(piece, F32)] * 4, ids, grad, gn_h, gn_l, gn_got, *near_w,
        scratch=[(padded, BF16), (padded, BF16), (full, F32)], room=12,
    )
    grads = over_chips(grads)

    def scaled_total(*refs):
        total_body(scale, *refs)

    def lo_sum(kept, got):
        one = [(kept.shape[1:], F32)]
        parts = call(pick_body, one * 4, ids, kept, got)
        parts = [parts[0]] + [swap(parts[mask], "lo", mask) for mask in (1, 2, 3)]
        return call(scaled_total, one, ids, *parts)[0]

    far_mine = lo_sum(far_keep, far_got)
    wide_half = [((part // 2, half), F32)]
    (far_mine,) = call(cross_body, wide_half, ids, far_mine, plane_swap(far_mine, 1))
    rows_all = [((part, half), F32)]
    (rows_far,) = call(far_rows_body, rows_all, ids, far_mine, plane_swap(far_mine, 0))
    far_cols = swap(rows_far, "hi", 1)
    quarters = [((n_lo, part // 4, half), F32)] * 2
    near_keep, near_send = call(plane_body, quarters, ids, near_keep, near_got)
    near_mine = lo_sum(near_keep, plane_swap(near_send, 1))
    near_all = over_chips([near_mine] * 4)
    (rows_near,) = call(near_rows_body, rows_all, ids, *near_all)
    near_cols = swap(rows_near, "hi", 1)
    to_hbm = (pltpu.VMEM, pltpu.HBM)
    to_hbm = (pltpu.VMEM, pltpu.HBM)
    wide = ((part, width), F32)
    sems = [pltpu.SemaphoreType.DMA((2,))]
    features, grad_track, grad_far = hbm_call(
        collect_body, [(full, F32)] * 2 + [wide], to_hbm, ids, (*feats, *grads, rows_far, far_cols),
        sems + [pltpu.SemaphoreType.DMA((8,))], 2,
    )
    (grad_near,) = hbm_call(columns_body, [wide], to_hbm, ids, (rows_near, near_cols), sems, 2)
    return features, grad_track, grad_near, grad_far


def from_behind(value, axis, steps):
    count = lax.axis_size(axis)
    initial, last = (max(0, -steps), min(count, count - steps))
    return lax.ppermute(value, axis, [(source, source + steps) for source in range(initial, last)])


def halo_shards(track, tight_weight, wide_weight, cotangent):
    def near_pair(field):
        return from_behind(field, ("hi", "lo"), NEAR_STEPS), from_behind(field, ("hi", "lo"), -NEAR_STEPS)

    def far_pair(field):
        return from_behind(field, "hi", FAR_STEPS), from_behind(field, "hi", -FAR_STEPS)

    def back_product(before, center, after, weights):
        width = center.shape[1]
        total = dot(after, weights[0:width], (1, 1))
        total = total + dot(center, weights[width : 2 * width], (1, 1))
        return total + dot(before, weights[2 * width : 3 * width], (1, 1))

    near_prev, near_next = near_pair(track)
    track_taps = jnp.concatenate([near_prev, track, near_next], axis=1)
    pre_near = dot(track_taps, tight_weight, (1, 0))
    act_near, near_pull = jax.vjp(gelu_fn, pre_near)
    hidden = track + act_near
    far_prev, far_next = far_pair(hidden)
    hidden_taps = jnp.concatenate([far_prev, hidden, far_next], axis=1)
    pre_far = dot(hidden_taps, wide_weight, (1, 0))
    act_far, far_pull = jax.vjp(gelu_fn, pre_far)
    features = hidden + act_far
    g_far = far_pull(cotangent)[0]
    term_far = dot(hidden_taps, g_far, (0, 0))
    gfar_prev, gfar_next = far_pair(g_far)
    grad_hidden = cotangent + back_product(gfar_prev, g_far, gfar_next, wide_weight)
    g_near = near_pull(grad_hidden)[0]
    term_near = dot(track_taps, g_near, (0, 0))
    gnear_prev, gnear_next = near_pair(g_near)
    grad_track = grad_hidden + back_product(gnear_prev, g_near, gnear_next, tight_weight)
    scale = 1.0 / jnp.sqrt(jnp.float32(track.shape[0] * lax.axis_size("hi") * lax.axis_size("lo")))
    summed_near, summed_far = lax.psum((term_near, term_far), "hi")
    rows_near = lax.psum_scatter(summed_near, "lo", scatter_dimension=0, tiled=True)
    rows_far = lax.psum_scatter(summed_far, "lo", scatter_dimension=0, tiled=True)
    return (features, grad_track, rows_near * scale, rows_far * scale)


def solution(mesh):
    n_hi, n_lo = mesh.shape["hi"], mesh.shape["lo"]

    def step(track, tight_weight, wide_weight, cotangent):
        rows = track.shape[0] // (n_hi * n_lo)
        closed = NEAR_STEPS == n_lo and FAR_STEPS == 2 and n_hi == 8
        closed = closed and rows % (8 * n_hi) == 0 and tight_weight.shape[0] % (64 * n_lo) == 0
        closed = closed and tight_weight.shape[1] % 256 == 0
        if closed:
            shards = family_shards
        else:
            shards = halo_shards
        in_specs = (P(("hi", "lo"), None), P(), P(), P(("hi", "lo"), None))
        out_specs = (P(("hi", "lo"), None), P(("hi", "lo"), None), P("lo", None), P("lo", None))
        mapped = jax.shard_map(shards, mesh=mesh, in_specs=in_specs, out_specs=out_specs, check_vma=False)
        return mapped(track, tight_weight, wide_weight, cotangent)

    return step
```

time: 109 us -> 120 us (1.10)
  waiting for transfers between devices: 40.9 us -> 56.7 us
  Pallas kernels: 28.9 us -> 25.6 us
    ppermute x0 -> x5, waiting for transfers between devices: none -> 20.9 us  [plane_swap(): lax.ppermute(value, 'hi', [(i, i ^ 2 << (i + turn) % 2) for i in range(co...]
    ppermute x38 -> x29, starting transfers between devices: 36.2 us -> 29.3 us  [swap(): return lax.ppermute(value, axis, [(i, i ^ mask) for i in range(count)])]
    pallas_call x21 -> x15, Pallas kernels: 25.3 us -> 18.6 us  [call(): pl.pallas_call(body, out_shape=[make(shape, dtype) for shape, dtype in ou...]
    ppermute x0 -> x5, starting transfers between devices: none -> 6.21 us  [plane_swap(): lax.ppermute(value, 'hi', [(i, i ^ 2 << (i + turn) % 2) for i in range(co...]
    ppermute x38 -> x29, waiting for transfers between devices: 40.9 us -> 35.8 us  [swap(): return lax.ppermute(value, axis, [(i, i ^ mask) for i in range(count)])]
    pallas_call x1 -> x3, Pallas kernels: 3.54 us -> 7.02 us  [hbm_call(): pl.pallas_call(body, out_shape=[out_place(shape, dtype) for shape, dtype...]
  transfers between devices with their start and end apart: 38 -> 34, of which waited for: 20 -> 18; matrix products, arithmetic and copies ran while one was open for 1% -> 0% of each run, Pallas kernels for 24% -> 19%
where the time goes in v1:
time: 120 us
  waiting for transfers between devices  56.7 us (47%)
  starting transfers between devices  35.5 us (30%)
  Pallas kernels  25.6 us (21%)
    ppermute x29, waiting for transfers between devices, swap(): return lax.ppermute(value, axis, [(i, i ^ mask) for i in range(count)])  35.8 us
    ppermute x29, starting transfers between devices, swap(): return lax.ppermute(value, axis, [(i, i ^ mask) for i in range(count)])  29.3 us
    ppermute x5, waiting for transfers between devices, plane_swap(): lax.ppermute(value, 'hi', [(i, i ^ 2 << (i + turn) % 2) for i in range(co...  20.9 us
    pallas_call x15, Pallas kernels, call(): pl.pallas_call(body, out_shape=[make(shape, dtype) for shape, dtype in ou...  18.6 us
    pallas_call x3, Pallas kernels, hbm_call(): pl.pallas_call(body, out_shape=[out_place(shape, dtype) for shape, dtype...  7.02 us
    ppermute x5, starting transfers between devices, plane_swap(): lax.ppermute(value, 'hi', [(i, i ^ 2 << (i + turn) % 2) for i in range(co...  6.21 us
  transfers between devices with their start and end apart: 34, of which 18 were waited for; matrix products, arithmetic and copies ran while one was open for 0% of the time, Pallas kernels for 19%

profile of v1, /device:TPU:0, one launch (start us, length us, event | category | flops | bytes accessed | tf_op | source)
XLA Modules:
  0.0 119.9 jit_solution(11643592425038275598)
XLA Ops:
  0.7 1.1 constant_dynamic-slice_fusion
  1.8 4.0 %collective-permute-start.2 = (f32[64,512]{1,0:T(8,128)S(1)}, f32[64,512]{1,0:T(8,128)S(1)}, u32[]{:S(2)}, u32[]{:S(2)}) collective-permute-start(f32[64,512]{1,0:T(8,128)S(1)} %get-tuple-element.102), channel_id=1, source_target_pairs={{0,24},{4,28},{8,16},{12,20},{16,8},{20,12},{24,0},{28,4},{1,25},{... | collective-permute-start | bytes 393224 | tf_op jit(solution)/shard_map/ppermute | solution.py:42
  5.8 0.5 collective-permute-start
  6.3 0.1 collective-permute-start.1
  6.4 3.7 %collective-permute-done.2.p3 = f32[64,512]{1,0:T(8,128)S(1)} collective-permute-done((f32[64,512]{1,0:T(8,128)S(1)}, f32[64,512]{1,0:T(8,128)S(1)}, u32[]{:S(2)}, u32[]{:S(2)}) %collective-permute-start.2) | collective-permute-done | bytes 131104 | tf_op jit(solution)/shard_map/ppermute | solution.py:42
  10.2 3.7 %shard_map.75 = (bf16[1536,512]{1,0:T(8,128)(2,1)S(1)}, bf16[1536,512]{1,0:T(8,128)(2,1)S(1)}, bf16[1536,512]{1,0:T(8,128)(2,1)S(1)}, bf16[1536,512]{1,0:T(8,128...) custom-call(s32[2]{0:T(128)S(1)} %pad_add_fusion.ids.refs_0_, ...), custom_call_target="tpu_custom_call" | custom-call | tf_op jit(solution)/shard_map/pallas_call | solution.py:118
  14.0 0.6 collective-permute-start.4
  14.5 0.1 collective-permute-start.5
  14.6 2.0 %collective-permute-start.10 = (f32[64,512]{1,0:T(8,128)S(1)}, f32[64,512]{1,0:T(8,128)S(1)}, u32[]{:S(2)}, u32[]{:S(2)}) collective-permute-start(f32[64,512]{1,0:T(8,128)S(1)} %get-tuple-element.62), channel_id=1, source_target_pairs={{0,8},{4,12},{8,0},{12,4},{16,24},{20,28},{24,16},{28,20},{1,9},{5... | collective-permute-start | bytes 393224 | tf_op jit(solution)/shard_map/ppermute | solution.py:42
  16.6 1.5 %collective-permute-start.11 = (f32[64,512]{1,0:T(8,128)S(1)}, f32[64,512]{1,0:T(8,128)S(1)}, u32[]{:S(2)}, u32[]{:S(2)}) collective-permute-start(f32[64,512]{1,0:T(8,128)S(1)} %get-tuple-element.63), channel_id=1, source_target_pairs={{0,16},{4,20},{8,24},{12,28},{16,0},{20,4},{24,8},{28,12},{1,17},{... | collective-permute-start | bytes 393224 | tf_op jit(solution)/shard_map/ppermute | solution.py:42
  18.2 3.7 %shard_map.76 = (f32[64,512]{1,0:T(8,128)S(1)}, f32[64,512]{1,0:T(8,128)S(1)}, f32[64,512]{1,0:T(8,128)S(1)}, f32[64,512]{1,0:T(8,128)S(1)}, f32[256,512]{1,0:T(...) custom-call(s32[2]{0:T(128)S(1)} %pad_add_fusion.ids.refs_0_, ...), custom_call_target="tpu_custom_call" | custom-call | tf_op jit(solution)/shard_map/pallas_call | solution.py:30
  21.9 3.1 %collective-permute-done.11.c2 = f32[64,512]{1,0:T(8,128)S(1)} collective-permute-done((f32[64,512]{1,0:T(8,128)S(1)}, f32[64,512]{1,0:T(8,128)S(1)}, u32[]{:S(2)}, u32[]{:S(2)}) %collective-permute-start.11) | collective-permute-done | bytes 131104 | tf_op jit(solution)/shard_map/ppermute | solution.py:42
  24.9 1.4 %shard_map.77 = (f32[256,512]{1,0:T(8,128)S(1)}, bf16[256,512]{1,0:T(8,128)(2,1)S(1)}, bf16[256,512]{1,0:T(8,128)(2,1)S(1)}, f32[1536,256]{1,0:T(8,128)S(1)}) custom-call(s32[2]{0:T(128)S(1)} %pad_add_fusion.ids.refs_0_, f32[64,512]{1,0:T(8,128)S(1)} %get-tuple-element.61.c0, f32[64,512]{1,0:T(8,128)S(1)} %collective-permute-done.10.c1, ...), custom_call_target="tpu_custom_call" | custom-call | tf_op jit(solution)/shard_map/pallas_call | solution.py:30
  26.5 2.1 %shard_map.78 = (f32[256,512]{1,0:T(8,128)S(1)}, f32[256,512]{1,0:T(8,128)S(1)}, bf16[256,512]{1,0:T(8,128)(2,1)S(1)}, bf16[256,512]{1,0:T(8,128)(2,1)S(1)}) custom-call(s32[2]{0:T(128)S(1)} %pad_add_fusion.ids.refs_0_, f32[256,512]{1,0:T(8,128)S(1)} %get-tuple-element.68.cot, bf16[256,512]{1,0:T(8,128)(2,1)S(1)} %get-tuple-element.69.g_h, ...), custom_call_target="tpu_custom_call" | custom-call | tf_op jit(solution)/shard_map/pallas_call | solution.py:30
  28.6 0.6 collective-permute-start.13
  29.2 1.4 %shard_map.86.term = f32[1536,256]{1,0:T(8,128)S(1)} custom-call(s32[2]{0:T(128)S(1)} %pad_add_fusion.ids.refs_0_, bf16[384,512]{1,0:T(8,128)(2,1)S(1)} %get-tuple-element.89.own_h, bf16[384,512]{1,0:T(8,128)(2,1)S(1)} %get-tuple-element.90.own_l, bf16[384,512]{1,0:T(8,128)(2,1)S(1)} %get-tuple-element.91.oth_h, ...), custom_call_target="tpu_custom_call" | custom-call | tf_op jit(solution)/shard_map/pallas_call | solution.py:30
  30.6 0.2 collective-permute-done.13.other
  30.7 1.6 %shard_map.87 = (f32[4,192,256]{2,1,0:T(8,128)S(1)}, f32[4,192,256]{2,1,0:T(8,128)S(1)}) custom-call(s32[2]{0:T(128)S(1)} %pad_add_fusion.ids.refs_0_, f32[1536,256]{1,0:T(8,128)S(1)} %shard_map.86.term, bf16[384,512]{1,0:T(8,128)(2,1)S(1)} %get-tuple-element.89.own_h, bf16[384,512]{1,0:T(8,128)(2,1)S(1)} %get-tuple-element.90.own_l, ...), custom_call_target="tpu_custom_call" | custom-call | tf_op jit(solution)/shard_map/pallas_call | solution.py:30
  32.4 1.3 %collective-permute-start.25 = (f32[4,192,256]{2,1,0:T(8,128)S(1)}, f32[4,192,256]{2,1,0:T(8,128)S(1)}, u32[]{:S(2)}, u32[]{:S(2)}) collective-permute-start(f32[4,192,256]{2,1,0:T(8,128)S(1)} %get-tuple-element.94), channel_id=1, source_target_pairs={{0,8},{4,20},{8,0},{12,28},{16,24},{20,4},{24,16},{28,12},{1,9},{5... | collective-permute-start | bytes 2359304 | tf_op jit(solution)/shard_map/ppermute | solution.py:47
  33.7 1.6 %shard_map.80 = (f32[4,192,256]{2,1,0:T(8,128)S(1)}, f32[4,192,256]{2,1,0:T(8,128)S(1)}) custom-call(s32[2]{0:T(128)S(1)} %pad_add_fusion.ids.refs_0_, bf16[256,512]{1,0:T(8,128)(2,1)S(1)} %get-tuple-element.66.hid_h, bf16[256,512]{1,0:T(8,128)(2,1)S(1)} %get-tuple-element.67.hid_l, bf16[256,512]{1,0:T(8,128)(2,1)S(1)} %get-tuple-element.69.g_h, ...), custom_call_target="tpu_custom_call" | custom-call | tf_op jit(solution)/shard_map/pallas_call | solution.py:30
  35.3 0.9 collective-permute-start.18
  36.2 8.3 %collective-permute-done.25.got = f32[4,192,256]{2,1,0:T(8,128)S(1)} collective-permute-done((f32[4,192,256]{2,1,0:T(8,128)S(1)}, f32[4,192,256]{2,1,0:T(8,128)S(1)}, u32[]{:S(2)}, u32[]{:S(2)}) %collective-permute-start.25) | collective-permute-done | bytes 786464 | tf_op jit(solution)/shard_map/ppermute | solution.py:47
  44.4 0.6 shard_map.88
  45.1 1.6 %collective-permute-start.26 = (f32[4,96,256]{2,1,0:T(8,128)S(1)}, f32[4,96,256]{2,1,0:T(8,128)S(1)}, u32[]{:S(2)}, u32[]{:S(2)}) collective-permute-start(f32[4,96,256]{2,1,0:T(8,128)S(1)} %get-tuple-element.96), channel_id=1, source_target_pairs={{0,16},{4,12},{8,24},{12,4},{16,0},{20,28},{24,8},{28,20},{1,17},{... | collective-permute-start | bytes 1179656 | tf_op jit(solution)/shard_map/ppermute | solution.py:47
  46.7 10.4 %collective-permute-done.18.got = f32[4,192,256]{2,1,0:T(8,128)S(1)} collective-permute-done((f32[4,192,256]{2,1,0:T(8,128)S(1)}, f32[4,192,256]{2,1,0:T(8,128)S(1)}, u32[]{:S(2)}, u32[]{:S(2)}) %collective-permute-start.18) | collective-permute-done | bytes 786464 | tf_op jit(solution)/shard_map/ppermute | solution.py:47
  57.1 0.6 shard_map.81
  57.7 1.6 %collective-permute-start.19 = (f32[192,256]{1,0:T(8,128)S(1)}, f32[192,256]{1,0:T(8,128)S(1)}, u32[]{:S(2)}, u32[]{:S(2)}) collective-permute-start(f32[192,256]{1,0:T(8,128)S(1)} %get-tuple-element.84), channel_id=1, source_target_pairs={{0,1},{1,0},{2,3},{3,2},{4,5},{5,4},{6,7},{7,6},{8,9},{9,8},{10,11... | collective-permute-start | bytes 589832 | tf_op jit(solution)/shard_map/ppermute | solution.py:42
  59.4 2.6 %collective-permute-start.20 = (f32[192,256]{1,0:T(8,128)S(1)}, f32[192,256]{1,0:T(8,128)S(1)}, u32[]{:S(2)}, u32[]{:S(2)}) collective-permute-start(f32[192,256]{1,0:T(8,128)S(1)} %get-tuple-element.85), channel_id=1, source_target_pairs={{0,2},{1,3},{2,0},{3,1},{4,6},{5,7},{6,4},{7,5},{8,10},{9,11},{10,... | collective-permute-start | bytes 589832 | tf_op jit(solution)/shard_map/ppermute | solution.py:42
  62.0 0.2 collective-permute-start.21
  62.2 4.0 %collective-permute-done.19.refs_2_ = f32[192,256]{1,0:T(8,128)S(1)} collective-permute-done((f32[192,256]{1,0:T(8,128)S(1)}, f32[192,256]{1,0:T(8,128)S(1)}, u32[]{:S(2)}, u32[]{:S(2)}) %collective-permute-start.19) | collective-permute-done | bytes 196640 | tf_op jit(solution)/shard_map/ppermute | solution.py:42
  66.1 10.1 %collective-permute-done.20.refs_3_ = f32[192,256]{1,0:T(8,128)S(1)} collective-permute-done((f32[192,256]{1,0:T(8,128)S(1)}, f32[192,256]{1,0:T(8,128)S(1)}, u32[]{:S(2)}, u32[]{:S(2)}) %collective-permute-start.20) | collective-permute-done | bytes 196640 | tf_op jit(solution)/shard_map/ppermute | solution.py:42
  76.2 0.6 shard_map.82.own
  76.8 1.6 %collective-permute-start.22 = (f32[192,256]{1,0:T(8,128)S(1)}, f32[192,256]{1,0:T(8,128)S(1)}, u32[]{:S(2)}, u32[]{:S(2)}) collective-permute-start(f32[192,256]{1,0:T(8,128)S(1)} %shard_map.82.own), channel_id=1, source_target_pairs={{0,16},{4,12},{8,24},{12,4},{16,0},{20,28},{24,8},{28,20},{1,17},{... | collective-permute-start | bytes 589832 | tf_op jit(solution)/shard_map/ppermute | solution.py:47
  78.4 0.6 shard_map.89
  79.0 2.7 %collective-permute-start.27 = (f32[96,256]{1,0:T(8,128)S(1)}, f32[96,256]{1,0:T(8,128)S(1)}, u32[]{:S(2)}, u32[]{:S(2)}) collective-permute-start(f32[96,256]{1,0:T(8,128)S(1)} %get-tuple-element.98), channel_id=1, source_target_pairs={{0,1},{1,0},{2,3},{3,2},{4,5},{5,4},{6,7},{7,6},{8,9},{9,8},{10,11... | collective-permute-start | bytes 294920 | tf_op jit(solution)/shard_map/ppermute | solution.py:42
  81.7 1.1 collective-permute-start.28
  82.8 1.4 %collective-permute-start.29 = (f32[96,256]{1,0:T(8,128)S(1)}, f32[96,256]{1,0:T(8,128)S(1)}, u32[]{:S(2)}, u32[]{:S(2)}) collective-permute-start(f32[96,256]{1,0:T(8,128)S(1)} %get-tuple-element.100), channel_id=1, source_target_pairs={{0,3},{1,2},{2,1},{3,0},{4,7},{5,6},{6,5},{7,4},{8,11},{9,10},{10,... | collective-permute-start | bytes 294920 | tf_op jit(solution)/shard_map/ppermute | solution.py:42
  84.2 0.1 collective-permute-done.27.refs_2_
  84.3 5.7 %collective-permute-done.28.refs_3_ = f32[96,256]{1,0:T(8,128)S(1)} collective-permute-done((f32[96,256]{1,0:T(8,128)S(1)}, f32[96,256]{1,0:T(8,128)S(1)}, u32[]{:S(2)}, u32[]{:S(2)}) %collective-permute-start.28) | collective-permute-done | bytes 98336 | tf_op jit(solution)/shard_map/ppermute | solution.py:42
  90.0 0.6 shard_map.90.s0
  90.6 1.8 %collective-permute-start.32 = (f32[96,256]{1,0:T(8,128)S(1)}, f32[96,256]{1,0:T(8,128)S(1)}, u32[]{:S(2)}, u32[]{:S(2)}) collective-permute-start(f32[96,256]{1,0:T(8,128)S(1)} %shard_map.90.s0), channel_id=1, source_target_pairs={{0,24},{4,28},{8,16},{12,20},{16,8},{20,12},{24,0},{28,4},{1,25},{... | collective-permute-start | bytes 294920 | tf_op jit(solution)/shard_map/ppermute | solution.py:42
  92.4 0.5 collective-permute-start.31
  92.9 1.2 %collective-permute-start.30 = (f32[96,256]{1,0:T(8,128)S(1)}, f32[96,256]{1,0:T(8,128)S(1)}, u32[]{:S(2)}, u32[]{:S(2)}) collective-permute-start(f32[96,256]{1,0:T(8,128)S(1)} %shard_map.90.s0), channel_id=1, source_target_pairs={{0,8},{4,12},{8,0},{12,4},{16,24},{20,28},{24,16},{28,20},{1,9},{5... | collective-permute-start | bytes 294920 | tf_op jit(solution)/shard_map/ppermute | solution.py:42
  94.2 0.6 shard_map.83.own
  94.7 0.9 collective-permute-start.23
  95.6 0.6 collective-permute-done.32.s3
  96.2 1.0 collective-permute-done.31.s2
  97.2 0.3 collective-permute-done.30.s1
  97.6 0.6 shard_map.91.own
  98.2 2.2 %collective-permute-done.23.got = f32[192,256]{1,0:T(8,128)S(1)} collective-permute-done((f32[192,256]{1,0:T(8,128)S(1)}, f32[192,256]{1,0:T(8,128)S(1)}, u32[]{:S(2)}, u32[]{:S(2)}) %collective-permute-start.23) | collective-permute-done | bytes 196640 | tf_op jit(solution)/shard_map/ppermute | solution.py:47
  100.5 0.6 shard_map.84.own
  101.1 0.9 collective-permute-start.7
  102.0 1.5 %collective-permute-start.8 = (f32[64,512]{1,0:T(8,128)S(1)}, f32[64,512]{1,0:T(8,128)S(1)}, u32[]{:S(2)}, u32[]{:S(2)}) collective-permute-start(f32[64,512]{1,0:T(8,128)S(1)} %get-tuple-element.59), channel_id=1, source_target_pairs={{0,16},{4,20},{8,24},{12,28},{16,0},{20,4},{24,8},{28,12},{1,17},{... | collective-permute-start | bytes 393224 | tf_op jit(solution)/shard_map/ppermute | solution.py:42
  103.5 1.2 collective-permute-start.9
  104.7 2.0 %shard_map.79 = (f32[64,512]{1,0:T(8,128)S(1)}, f32[64,512]{1,0:T(8,128)S(1)}, f32[64,512]{1,0:T(8,128)S(1)}, f32[64,512]{1,0:T(8,128)S(1)}) custom-call(s32[2]{0:T(128)S(1)} %pad_add_fusion.ids.refs_0_, f32[256,512]{1,0:T(8,128)S(1)} %get-tuple-element.72.grad, bf16[256,512]{1,0:T(8,128)(2,1)S(1)} %get-tuple-element.73.gn_h, ...), custom_call_target="tpu_custom_call" | custom-call | tf_op jit(solution)/shard_map/pallas_call | solution.py:30
  106.7 0.9 collective-permute-done.7.f1
  107.6 0.8 collective-permute-start.14
  108.4 1.7 %collective-permute-done.8.f2 = f32[64,512]{1,0:T(8,128)S(1)} collective-permute-done((f32[64,512]{1,0:T(8,128)S(1)}, f32[64,512]{1,0:T(8,128)S(1)}, u32[]{:S(2)}, u32[]{:S(2)}) %collective-permute-start.8) | collective-permute-done | bytes 131104 | tf_op jit(solution)/shard_map/ppermute | solution.py:42
  110.0 2.1 %collective-permute-start.15 = (f32[64,512]{1,0:T(8,128)S(1)}, f32[64,512]{1,0:T(8,128)S(1)}, u32[]{:S(2)}, u32[]{:S(2)}) collective-permute-start(f32[64,512]{1,0:T(8,128)S(1)} %get-tuple-element.78), channel_id=1, source_target_pairs={{0,16},{4,20},{8,24},{12,28},{16,0},{20,4},{24,8},{28,12},{1,17},{... | collective-permute-start | bytes 393224 | tf_op jit(solution)/shard_map/ppermute | solution.py:42
  112.2 1.4 %shard_map.92 = f32[384,512]{1,0:T(8,128)} custom-call(s32[2]{0:T(128)S(1)} %pad_add_fusion.ids.refs_0_, f32[384,256]{1,0:T(8,128)S(1)} %shard_map.91.own, f32[384,256]{1,0:T(8,128)S(1)} %collective-permute-done.33.got), custom_call_target="tpu_custom_call" | custom-call | tf_op jit(solution)/shard_map/pallas_call | solution.py:118
  113.7 0.3 collective-permute-done.14.g1
  113.9 2.2 %collective-permute-done.15.g2 = f32[64,512]{1,0:T(8,128)S(1)} collective-permute-done((f32[64,512]{1,0:T(8,128)S(1)}, f32[64,512]{1,0:T(8,128)S(1)}, u32[]{:S(2)}, u32[]{:S(2)}) %collective-permute-start.15) | collective-permute-done | bytes 131104 | tf_op jit(solution)/shard_map/ppermute | solution.py:42
  116.1 1.9 %collective-permute-done.16.g3 = f32[64,512]{1,0:T(8,128)S(1)} collective-permute-done((f32[64,512]{1,0:T(8,128)S(1)}, f32[64,512]{1,0:T(8,128)S(1)}, u32[]{:S(2)}, u32[]{:S(2)}) %collective-permute-start.16) | collective-permute-done | bytes 131104 | tf_op jit(solution)/shard_map/ppermute | solution.py:42
  118.1 1.8 %shard_map.85 = (f32[256,512]{1,0:T(8,128)}, f32[256,512]{1,0:T(8,128)}, f32[384,512]{1,0:T(8,128)}) custom-call(s32[2]{0:T(128)S(1)} %pad_add_fusion.ids.refs_0_, f32[64,512]{1,0:T(8,128)S(1)} %get-tuple-element.57.f0, f32[64,512]{1,0:T(8,128)S(1)} %collective-permute-done.7.f1, f32[64,512]{1,0:T(8,128)S(1)} %collective-permute-done.8.f2, ...), custom_call_target="tpu_custom_call" | custom-call | tf_op jit(solution)/shard_map/pallas_call | solution.py:118
  (24 shorter events, 0.4 us)
Async XLA Ops:
  1.8 8.3 %collective-permute-start.2 = (f32[64,512]{1,0:T(8,128)S(1)}, f32[64,512]{1,0:T(8,128)S(1)}, u32[]{:S(2)}, u32[]{:S(2)}) collective-permute-start(f32[64,512]{1,0:T(8,128)S(1)} %get-tuple-element.102), channel_id=1, source_target_pairs={{0,24},{4,28},{8,16},{12,20},{16,8},{20,12},{24,0},{28,4},{1,25},{... | collective-permute-start | bytes 393224 | tf_op jit(solution)/shard_map/ppermute | solution.py:42
  5.8 8.2 %collective-permute-start = (f32[64,512]{1,0:T(8,128)S(1)}, f32[64,512]{1,0:T(8,128)S(1)}, u32[]{:S(2)}, u32[]{:S(2)}) collective-permute-start(f32[64,512]{1,0:T(8,128)S(1)} %get-tuple-element.103), channel_id=1, source_target_pairs={{0,8},{4,12},{8,0},{12,4},{16,24},{20,28},{24,16},{28,20},{1,9},{5... | collective-permute-start | bytes 393224 | tf_op jit(solution)/shard_map/ppermute | solution.py:42
  6.3 8.2 %collective-permute-start.1 = (f32[64,512]{1,0:T(8,128)S(1)}, f32[64,512]{1,0:T(8,128)S(1)}, u32[]{:S(2)}, u32[]{:S(2)}) collective-permute-start(f32[64,512]{1,0:T(8,128)S(1)} %get-tuple-element.105), channel_id=1, source_target_pairs={{0,16},{4,20},{8,24},{12,28},{16,0},{20,4},{24,8},{28,12},{1,17},{... | collective-permute-start | bytes 393224 | tf_op jit(solution)/shard_map/ppermute | solution.py:42
  6.4 10.2 %collective-permute-start.3 = (f32[64,512]{1,0:T(8,128)S(1)}, f32[64,512]{1,0:T(8,128)S(1)}, u32[]{:S(2)}, u32[]{:S(2)}) collective-permute-start(f32[64,512]{1,0:T(8,128)S(1)} %get-tuple-element.104.p0), channel_id=1, source_target_pairs={{0,4},{4,0},{8,12},{12,8},{16,20},{20,16},{24,28},{28,24},{1,5},{5... | collective-permute-start | bytes 393224 | tf_op jit(solution)/shard_map/ppermute | solution.py:42
  10.1 8.0 %collective-permute-start.6 = (f32[64,512]{1,0:T(8,128)S(1)}, f32[64,512]{1,0:T(8,128)S(1)}, u32[]{:S(2)}, u32[]{:S(2)}) collective-permute-start(f32[64,512]{1,0:T(8,128)S(1)} %collective-permute-done.2.p3), channel_id=1, source_target_pairs={{0,4},{4,0},{8,12},{12,8},{16,20},{20,16},{24,28},{28,24},{1,5},{5... | collective-permute-start | bytes 393224 | tf_op jit(solution)/shard_map/ppermute | solution.py:42
  14.0 4.2 %collective-permute-start.4 = (f32[64,512]{1,0:T(8,128)S(1)}, f32[64,512]{1,0:T(8,128)S(1)}, u32[]{:S(2)}, u32[]{:S(2)}) collective-permute-start(f32[64,512]{1,0:T(8,128)S(1)} %collective-permute-done.p1), channel_id=1, source_target_pairs={{0,4},{4,0},{8,12},{12,8},{16,20},{20,16},{24,28},{28,24},{1,5},{5... | collective-permute-start | bytes 393224 | tf_op jit(solution)/shard_map/ppermute | solution.py:42
  14.5 3.6 %collective-permute-start.5 = (f32[64,512]{1,0:T(8,128)S(1)}, f32[64,512]{1,0:T(8,128)S(1)}, u32[]{:S(2)}, u32[]{:S(2)}) collective-permute-start(f32[64,512]{1,0:T(8,128)S(1)} %collective-permute-done.1.p2), channel_id=1, source_target_pairs={{0,4},{4,0},{8,12},{12,8},{16,20},{20,16},{24,28},{28,24},{1,5},{5... | collective-permute-start | bytes 393224 | tf_op jit(solution)/shard_map/ppermute | solution.py:42
  14.6 7.2 %collective-permute-start.10 = (f32[64,512]{1,0:T(8,128)S(1)}, f32[64,512]{1,0:T(8,128)S(1)}, u32[]{:S(2)}, u32[]{:S(2)}) collective-permute-start(f32[64,512]{1,0:T(8,128)S(1)} %get-tuple-element.62), channel_id=1, source_target_pairs={{0,8},{4,12},{8,0},{12,4},{16,24},{20,28},{24,16},{28,20},{1,9},{5... | collective-permute-start | bytes 393224 | tf_op jit(solution)/shard_map/ppermute | solution.py:42
  16.6 8.4 %collective-permute-start.11 = (f32[64,512]{1,0:T(8,128)S(1)}, f32[64,512]{1,0:T(8,128)S(1)}, u32[]{:S(2)}, u32[]{:S(2)}) collective-permute-start(f32[64,512]{1,0:T(8,128)S(1)} %get-tuple-element.63), channel_id=1, source_target_pairs={{0,16},{4,20},{8,24},{12,28},{16,0},{20,4},{24,8},{28,12},{1,17},{... | collective-permute-start | bytes 393224 | tf_op jit(solution)/shard_map/ppermute | solution.py:42
  18.1 6.8 %collective-permute-start.12 = (f32[64,512]{1,0:T(8,128)S(1)}, f32[64,512]{1,0:T(8,128)S(1)}, u32[]{:S(2)}, u32[]{:S(2)}) collective-permute-start(f32[64,512]{1,0:T(8,128)S(1)} %get-tuple-element.64), channel_id=1, source_target_pairs={{0,24},{4,28},{8,16},{12,20},{16,8},{20,12},{24,0},{28,4},{1,25},{... | collective-permute-start | bytes 393224 | tf_op jit(solution)/shard_map/ppermute | solution.py:42
  26.4 7.3 %collective-permute-start.17 = (f32[1536,256]{1,0:T(8,128)S(1)}, f32[1536,256]{1,0:T(8,128)S(1)}, u32[]{:S(2)}, u32[]{:S(2)}) collective-permute-start(f32[1536,256]{1,0:T(8,128)S(1)} %get-tuple-element.80), channel_id=1, source_target_pairs={{0,4},{4,0},{8,12},{12,8},{16,20},{20,16},{24,28},{28,24},{1,5},{5... | collective-permute-start | bytes 4718600 | tf_op jit(solution)/shard_map/ppermute | solution.py:42
  28.6 2.1 %collective-permute-start.13 = (f32[256,512]{1,0:T(8,128)S(1)}, f32[256,512]{1,0:T(8,128)S(1)}, u32[]{:S(2)}, u32[]{:S(2)}) collective-permute-start(f32[256,512]{1,0:T(8,128)S(1)} %get-tuple-element.75), channel_id=1, source_target_pairs={{0,4},{4,0},{8,12},{12,8},{16,20},{20,16},{24,28},{28,24},{1,5},{5... | collective-permute-start | bytes 1572872 | tf_op jit(solution)/shard_map/ppermute | solution.py:42
  32.4 12.1 %collective-permute-start.25 = (f32[4,192,256]{2,1,0:T(8,128)S(1)}, f32[4,192,256]{2,1,0:T(8,128)S(1)}, u32[]{:S(2)}, u32[]{:S(2)}) collective-permute-start(f32[4,192,256]{2,1,0:T(8,128)S(1)} %get-tuple-element.94), channel_id=1, source_target_pairs={{0,8},{4,20},{8,0},{12,28},{16,24},{20,4},{24,16},{28,12},{1,9},{5... | collective-permute-start | bytes 2359304 | tf_op jit(solution)/shard_map/ppermute | solution.py:47
  35.3 21.8 %collective-permute-start.18 = (f32[4,192,256]{2,1,0:T(8,128)S(1)}, f32[4,192,256]{2,1,0:T(8,128)S(1)}, u32[]{:S(2)}, u32[]{:S(2)}) collective-permute-start(f32[4,192,256]{2,1,0:T(8,128)S(1)} %get-tuple-element.82), channel_id=1, source_target_pairs={{0,8},{4,20},{8,0},{12,28},{16,24},{20,4},{24,16},{28,12},{1,9},{5... | collective-permute-start | bytes 2359304 | tf_op jit(solution)/shard_map/ppermute | solution.py:47
  45.1 33.3 %collective-permute-start.26 = (f32[4,96,256]{2,1,0:T(8,128)S(1)}, f32[4,96,256]{2,1,0:T(8,128)S(1)}, u32[]{:S(2)}, u32[]{:S(2)}) collective-permute-start(f32[4,96,256]{2,1,0:T(8,128)S(1)} %get-tuple-element.96), channel_id=1, source_target_pairs={{0,16},{4,12},{8,24},{12,4},{16,0},{20,28},{24,8},{28,20},{1,17},{... | collective-permute-start | bytes 1179656 | tf_op jit(solution)/shard_map/ppermute | solution.py:47
  57.7 8.4 %collective-permute-start.19 = (f32[192,256]{1,0:T(8,128)S(1)}, f32[192,256]{1,0:T(8,128)S(1)}, u32[]{:S(2)}, u32[]{:S(2)}) collective-permute-start(f32[192,256]{1,0:T(8,128)S(1)} %get-tuple-element.84), channel_id=1, source_target_pairs={{0,1},{1,0},{2,3},{3,2},{4,5},{5,4},{6,7},{7,6},{8,9},{9,8},{10,11... | collective-permute-start | bytes 589832 | tf_op jit(solution)/shard_map/ppermute | solution.py:42
  59.4 16.9 %collective-permute-start.20 = (f32[192,256]{1,0:T(8,128)S(1)}, f32[192,256]{1,0:T(8,128)S(1)}, u32[]{:S(2)}, u32[]{:S(2)}) collective-permute-start(f32[192,256]{1,0:T(8,128)S(1)} %get-tuple-element.85), channel_id=1, source_target_pairs={{0,2},{1,3},{2,0},{3,1},{4,6},{5,7},{6,4},{7,5},{8,10},{9,11},{10,... | collective-permute-start | bytes 589832 | tf_op jit(solution)/shard_map/ppermute | solution.py:42
  62.0 14.3 %collective-permute-start.21 = (f32[192,256]{1,0:T(8,128)S(1)}, f32[192,256]{1,0:T(8,128)S(1)}, u32[]{:S(2)}, u32[]{:S(2)}) collective-permute-start(f32[192,256]{1,0:T(8,128)S(1)} %get-tuple-element.86), channel_id=1, source_target_pairs={{0,3},{1,2},{2,1},{3,0},{4,7},{5,6},{6,5},{7,4},{8,11},{9,10},{10,... | collective-permute-start | bytes 589832 | tf_op jit(solution)/shard_map/ppermute | solution.py:42
  76.8 17.3 %collective-permute-start.22 = (f32[192,256]{1,0:T(8,128)S(1)}, f32[192,256]{1,0:T(8,128)S(1)}, u32[]{:S(2)}, u32[]{:S(2)}) collective-permute-start(f32[192,256]{1,0:T(8,128)S(1)} %shard_map.82.own), channel_id=1, source_target_pairs={{0,16},{4,12},{8,24},{12,4},{16,0},{20,28},{24,8},{28,20},{1,17},{... | collective-permute-start | bytes 589832 | tf_op jit(solution)/shard_map/ppermute | solution.py:47
  79.0 5.3 %collective-permute-start.27 = (f32[96,256]{1,0:T(8,128)S(1)}, f32[96,256]{1,0:T(8,128)S(1)}, u32[]{:S(2)}, u32[]{:S(2)}) collective-permute-start(f32[96,256]{1,0:T(8,128)S(1)} %get-tuple-element.98), channel_id=1, source_target_pairs={{0,1},{1,0},{2,3},{3,2},{4,5},{5,4},{6,7},{7,6},{8,9},{9,8},{10,11... | collective-permute-start | bytes 294920 | tf_op jit(solution)/shard_map/ppermute | solution.py:42
  81.7 8.3 %collective-permute-start.28 = (f32[96,256]{1,0:T(8,128)S(1)}, f32[96,256]{1,0:T(8,128)S(1)}, u32[]{:S(2)}, u32[]{:S(2)}) collective-permute-start(f32[96,256]{1,0:T(8,128)S(1)} %get-tuple-element.99), channel_id=1, source_target_pairs={{0,2},{1,3},{2,0},{3,1},{4,6},{5,7},{6,4},{7,5},{8,10},{9,11},{10,... | collective-permute-start | bytes 294920 | tf_op jit(solution)/shard_map/ppermute | solution.py:42
  82.8 7.2 %collective-permute-start.29 = (f32[96,256]{1,0:T(8,128)S(1)}, f32[96,256]{1,0:T(8,128)S(1)}, u32[]{:S(2)}, u32[]{:S(2)}) collective-permute-start(f32[96,256]{1,0:T(8,128)S(1)} %get-tuple-element.100), channel_id=1, source_target_pairs={{0,3},{1,2},{2,1},{3,0},{4,7},{5,6},{6,5},{7,4},{8,11},{9,10},{10,... | collective-permute-start | bytes 294920 | tf_op jit(solution)/shard_map/ppermute | solution.py:42
  90.6 5.6 %collective-permute-start.32 = (f32[96,256]{1,0:T(8,128)S(1)}, f32[96,256]{1,0:T(8,128)S(1)}, u32[]{:S(2)}, u32[]{:S(2)}) collective-permute-start(f32[96,256]{1,0:T(8,128)S(1)} %shard_map.90.s0), channel_id=1, source_target_pairs={{0,24},{4,28},{8,16},{12,20},{16,8},{20,12},{24,0},{28,4},{1,25},{... | collective-permute-start | bytes 294920 | tf_op jit(solution)/shard_map/ppermute | solution.py:42
  92.4 4.8 %collective-permute-start.31 = (f32[96,256]{1,0:T(8,128)S(1)}, f32[96,256]{1,0:T(8,128)S(1)}, u32[]{:S(2)}, u32[]{:S(2)}) collective-permute-start(f32[96,256]{1,0:T(8,128)S(1)} %shard_map.90.s0), channel_id=1, source_target_pairs={{0,16},{4,20},{8,24},{12,28},{16,0},{20,4},{24,8},{28,12},{1,17},{... | collective-permute-start | bytes 294920 | tf_op jit(solution)/shard_map/ppermute | solution.py:42
  92.9 4.6 %collective-permute-start.30 = (f32[96,256]{1,0:T(8,128)S(1)}, f32[96,256]{1,0:T(8,128)S(1)}, u32[]{:S(2)}, u32[]{:S(2)}) collective-permute-start(f32[96,256]{1,0:T(8,128)S(1)} %shard_map.90.s0), channel_id=1, source_target_pairs={{0,8},{4,12},{8,0},{12,4},{16,24},{20,28},{24,16},{28,20},{1,9},{5... | collective-permute-start | bytes 294920 | tf_op jit(solution)/shard_map/ppermute | solution.py:42
  94.7 5.7 %collective-permute-start.23 = (f32[192,256]{1,0:T(8,128)S(1)}, f32[192,256]{1,0:T(8,128)S(1)}, u32[]{:S(2)}, u32[]{:S(2)}) collective-permute-start(f32[192,256]{1,0:T(8,128)S(1)} %shard_map.83.own), channel_id=1, source_target_pairs={{0,8},{4,20},{8,0},{12,28},{16,24},{20,4},{24,16},{28,12},{1,9},{5... | collective-permute-start | bytes 589832 | tf_op jit(solution)/shard_map/ppermute | solution.py:47
  98.1 14.1 %collective-permute-start.33 = (f32[384,256]{1,0:T(8,128)S(1)}, f32[384,256]{1,0:T(8,128)S(1)}, u32[]{:S(2)}, u32[]{:S(2)}) collective-permute-start(f32[384,256]{1,0:T(8,128)S(1)} %shard_map.91.own), channel_id=1, source_target_pairs={{0,4},{4,0},{8,12},{12,8},{16,20},{20,16},{24,28},{28,24},{1,5},{5... | collective-permute-start | bytes 1179656 | tf_op jit(solution)/shard_map/ppermute | solution.py:42
  101.0 17.0 %collective-permute-start.24 = (f32[384,256]{1,0:T(8,128)S(1)}, f32[384,256]{1,0:T(8,128)S(1)}, u32[]{:S(2)}, u32[]{:S(2)}) collective-permute-start(f32[384,256]{1,0:T(8,128)S(1)} %shard_map.84.own), channel_id=1, source_target_pairs={{0,4},{4,0},{8,12},{12,8},{16,20},{20,16},{24,28},{28,24},{1,5},{5... | collective-permute-start | bytes 1179656 | tf_op jit(solution)/shard_map/ppermute | solution.py:42
  101.1 6.4 %collective-permute-start.7 = (f32[64,512]{1,0:T(8,128)S(1)}, f32[64,512]{1,0:T(8,128)S(1)}, u32[]{:S(2)}, u32[]{:S(2)}) collective-permute-start(f32[64,512]{1,0:T(8,128)S(1)} %get-tuple-element.58), channel_id=1, source_target_pairs={{0,8},{4,12},{8,0},{12,4},{16,24},{20,28},{24,16},{28,20},{1,9},{5... | collective-permute-start | bytes 393224 | tf_op jit(solution)/shard_map/ppermute | solution.py:42
  102.0 8.1 %collective-permute-start.8 = (f32[64,512]{1,0:T(8,128)S(1)}, f32[64,512]{1,0:T(8,128)S(1)}, u32[]{:S(2)}, u32[]{:S(2)}) collective-permute-start(f32[64,512]{1,0:T(8,128)S(1)} %get-tuple-element.59), channel_id=1, source_target_pairs={{0,16},{4,20},{8,24},{12,28},{16,0},{20,4},{24,8},{28,12},{1,17},{... | collective-permute-start | bytes 393224 | tf_op jit(solution)/shard_map/ppermute | solution.py:42
  103.5 10.1 %collective-permute-start.9 = (f32[64,512]{1,0:T(8,128)S(1)}, f32[64,512]{1,0:T(8,128)S(1)}, u32[]{:S(2)}, u32[]{:S(2)}) collective-permute-start(f32[64,512]{1,0:T(8,128)S(1)} %get-tuple-element.60), channel_id=1, source_target_pairs={{0,24},{4,28},{8,16},{12,20},{16,8},{20,12},{24,0},{28,4},{1,25},{... | collective-permute-start | bytes 393224 | tf_op jit(solution)/shard_map/ppermute | solution.py:42
  107.6 6.4 %collective-permute-start.14 = (f32[64,512]{1,0:T(8,128)S(1)}, f32[64,512]{1,0:T(8,128)S(1)}, u32[]{:S(2)}, u32[]{:S(2)}) collective-permute-start(f32[64,512]{1,0:T(8,128)S(1)} %get-tuple-element.77), channel_id=1, source_target_pairs={{0,8},{4,12},{8,0},{12,4},{16,24},{20,28},{24,16},{28,20},{1,9},{5... | collective-permute-start | bytes 393224 | tf_op jit(solution)/shard_map/ppermute | solution.py:42
  110.0 6.1 %collective-permute-start.15 = (f32[64,512]{1,0:T(8,128)S(1)}, f32[64,512]{1,0:T(8,128)S(1)}, u32[]{:S(2)}, u32[]{:S(2)}) collective-permute-start(f32[64,512]{1,0:T(8,128)S(1)} %get-tuple-element.78), channel_id=1, source_target_pairs={{0,16},{4,20},{8,24},{12,28},{16,0},{20,4},{24,8},{28,12},{1,17},{... | collective-permute-start | bytes 393224 | tf_op jit(solution)/shard_map/ppermute | solution.py:42
  112.2 5.9 %collective-permute-start.16 = (f32[64,512]{1,0:T(8,128)S(1)}, f32[64,512]{1,0:T(8,128)S(1)}, u32[]{:S(2)}, u32[]{:S(2)}) collective-permute-start(f32[64,512]{1,0:T(8,128)S(1)} %get-tuple-element.79), channel_id=1, source_target_pairs={{0,24},{4,28},{8,16},{12,20},{16,8},{20,12},{24,0},{28,4},{1,25},{... | collective-permute-start | bytes 393224 | tf_op jit(solution)/shard_map/ppermute | solution.py:42

commit v2 on v1

--- a/solution.py
+++ b/solution.py
@@ -23,18 +23,17 @@
     return jax.nn.gelu(value, approximate=True)
 
 
-def call(body, outs, ids, *args, scratch=(), to_hbm=False, room=4):
+def call(body, outs, *args, scratch=(), to_hbm=False, room=4):
     vmem = pl.BlockSpec(memory_space=pltpu.VMEM)
-    smem = pl.BlockSpec(memory_space=pltpu.SMEM)
     make = jax.ShapeDtypeStruct if to_hbm else pltpu.VMEM
     return pl.pallas_call(
         body,
         out_shape=[make(shape, dtype) for shape, dtype in outs],
-        in_specs=[smem] + [vmem] * len(args),
+        in_specs=[vmem] * len(args),
         out_specs=[vmem] * len(outs),
         scratch_shapes=[pltpu.VMEM(shape, dtype) for shape, dtype in scratch],
         compiler_params=pltpu.CompilerParams(vmem_limit_bytes=room * 1024 * 1024),
-    )(ids, *[pltpu.with_memory_space_constraint(arg, pltpu.VMEM) for arg in args])
+    )(*[pltpu.with_memory_space_constraint(arg, pltpu.VMEM) for arg in args])
 
 
 def swap(value, axis, mask):
@@ -47,9 +46,9 @@
     return lax.ppermute(value, "hi", [(i, i ^ (2 << (i + turn) % 2)) for i in range(count)])
 
 
-def bits(ids):
-    hi, lo = ids[0], ids[1]
-    return hi & 1, hi >> 1, lo
+def bits():
+    hi = lax.axis_index("hi")
+    return hi & 1, hi >> 1, lax.axis_index("lo")
 
 
 def turns(core, chip):
@@ -87,8 +86,8 @@
     return pl.ds(pl.multiple_of(index * size, size), size)
 
 
-def weights_body(ids, near, far, cot, near_h, near_l, far_h, far_l, c0, c1, c2, c3, staged, done, moved):
-    chip = bits(ids)[1]
+def weights_body(near, far, cot, near_h, near_l, far_h, far_l, c0, c1, c2, c3, staged, done, moved):
+    chip = bits()[1]
     parts, rows, _ = staged.shape
     each = parts // 2
     size = c0.shape[0]
@@ -111,23 +110,22 @@
         copy.wait()
 
 
-def hbm_call(body, outs, specs, ids, args, scratch, room):
-    smem = pl.BlockSpec(memory_space=pltpu.SMEM)
+def hbm_call(body, outs, specs, args, scratch, room):
     places = {pltpu.HBM: pl.BlockSpec(memory_space=pltpu.HBM), pltpu.VMEM: pl.BlockSpec(memory_space=pltpu.VMEM)}
     ins, out_place = specs
     return pl.pallas_call(
         body,
         out_shape=[out_place(shape, dtype) for shape, dtype in outs],
-        in_specs=[smem] + [places[ins]] * len(args),
+        in_specs=[places[ins]] * len(args),
         out_specs=[places[out_place]] * len(outs),
         scratch_shapes=scratch,
         compiler_params=pltpu.CompilerParams(vmem_limit_bytes=room * 1024 * 1024),
-    )(ids, *[pltpu.with_memory_space_constraint(arg, ins) for arg in args])
-
-
-def forward_body(ids, p0, p1, p2, p3, q0, q1, q2, q3, near_h, near_l, far_h, far_l,
+    )(*[pltpu.with_memory_space_constraint(arg, ins) for arg in args])
+
+
+def forward_body(p0, p1, p2, p3, q0, q1, q2, q3, near_h, near_l, far_h, far_l,
                  f0, f1, f2, f3, slope_near, slope_far, hid_h, hid_l, own_h, own_l, oth_h, oth_l, field):
-    core, chip, _ = bits(ids)
+    core, chip, _ = bits()
     rows, width = slope_near.shape
     size = rows // 4
     pad = jnp.zeros((size, width), BF16)
@@ -185,8 +183,8 @@
     store(2, mul(tuple(ref[after] for ref in sides), grad, (0, 0)))
 
 
-def far_other_body(ids, c0, c1, c2, c3, slope, hid_h, hid_l, cot, g_h, g_l, term):
-    core, chip, _ = bits(ids)
+def far_other_body(c0, c1, c2, c3, slope, hid_h, hid_l, cot, g_h, g_l, term):
+    core, chip, _ = bits()
     rows, width = cot.shape
     size = rows // 4
     for mask, piece in enumerate((c0, c1, c2, c3)):
@@ -206,8 +204,8 @@
         send[z] = total[pl.ds(pl.multiple_of((2 * z + 1 - bit) * half, 32), half)]
 
 
-def far_own_body(ids, hid_h, hid_l, g_h, g_l, got, keep, send, total):
-    core, chip, _ = bits(ids)
+def far_own_body(hid_h, hid_l, g_h, g_l, got, keep, send, total):
+    core, chip, _ = bits()
     width = hid_h.shape[1]
 
     def store(tap, value):
@@ -217,7 +215,7 @@
     halve(total, turns(core, chip)[0], keep, send)
 
 
-def backward_body(ids, cot, g_h, g_l, far_h, far_l, slope, grad, gn, gn_h, gn_l):
+def backward_body(cot, g_h, g_l, far_h, far_l, slope, grad, gn, gn_h, gn_l):
     rows, width = cot.shape
     size = rows // 4
     rest = rows - size
@@ -229,8 +227,8 @@
     gn_h[...], gn_l[...] = split(value)
 
 
-def near_mine_body(ids, own_h, own_l, oth_h, oth_l, gn_h, gn_l, term):
-    core, _, _ = bits(ids)
+def near_mine_body(own_h, own_l, oth_h, oth_l, gn_h, gn_l, term):
+    core, _, _ = bits()
     width = own_h.shape[1]
 
     def store(tap, value):
@@ -239,8 +237,8 @@
     near_term(core, (own_h, own_l), (oth_h, oth_l), half_columns((gn_h, gn_l), core), store)
 
 
-def near_both_body(ids, term, own_h, own_l, oth_h, oth_l, other, keep, send, total):
-    core, chip, _ = bits(ids)
+def near_both_body(term, own_h, own_l, oth_h, oth_l, other, keep, send, total):
+    core, chip, _ = bits()
     width = own_h.shape[1]
     half = width // 2
 
@@ -252,8 +250,8 @@
     halve(total, turns(core, chip)[0], keep, send)
 
 
-def track_body(ids, grad, gn_h, gn_l, other, near_h, near_l, t0, t1, t2, t3, oth_h, oth_l, field):
-    core, chip, _ = bits(ids)
+def track_body(grad, gn_h, gn_l, other, near_h, near_l, t0, t1, t2, t3, oth_h, oth_l, field):
+    core, chip, _ = bits()
     rows, width = grad.shape
     size = rows // 4
     pad = jnp.zeros((size, width), BF16)
@@ -272,8 +270,8 @@
         out[...] = field[block(chip ^ mask, size)]
 
 
-def plane_body(ids, kept, got, keep, send):
-    core, chip, _ = bits(ids)
+def plane_body(kept, got, keep, send):
+    core, chip, _ = bits()
     bit = turns(core, chip)[1]
     half = keep.shape[1]
     mine = pl.ds(pl.multiple_of(bit * half, 32), half)
@@ -282,30 +280,30 @@
     send[...] = kept[:, theirs] + got[:, theirs]
 
 
-def pick_body(ids, kept, got, p0, p1, p2, p3):
-    lo = bits(ids)[2]
+def pick_body(kept, got, p0, p1, p2, p3):
+    lo = bits()[2]
     for mask, out in enumerate((p0, p1, p2, p3)):
         out[...] = kept[lo ^ mask] + got[lo ^ mask]
 
 
-def total_body(scale, ids, p0, p1, p2, p3, out):
+def total_body(scale, p0, p1, p2, p3, out):
     out[...] = ((p0[...] + p1[...]) + (p2[...] + p3[...])) * scale
 
 
-def cross_body(ids, own, got, out):
+def cross_body(own, got, out):
     out[...] = own[...] + got[...]
 
 
-def far_rows_body(ids, own, got, out):
-    core, chip, _ = bits(ids)
+def far_rows_body(own, got, out):
+    core, chip, _ = bits()
     bit = turns(core, chip)[0]
     half = own.shape[0]
     out[pl.ds(pl.multiple_of(bit * half, 32), half)] = own[...]
     out[pl.ds(pl.multiple_of((1 - bit) * half, 32), half)] = got[...]
 
 
-def near_rows_body(ids, s0, s1, s2, s3, out):
-    core, chip, _ = bits(ids)
+def near_rows_body(s0, s1, s2, s3, out):
+    core, chip, _ = bits()
     size = s0.shape[0]
     for mask, piece in enumerate((s0, s1, s2, s3)):
         first, second = turns(core, chip ^ mask)
@@ -319,40 +317,34 @@
         copy.wait()
 
 
-def place_columns(core, own, got, out, done, others=()):
-    width = own.shape[1]
-
-    def place(left, right):
+def collect_body(f0, f1, f2, f3, g0, g1, g2, g3, far, far_got, near, near_got,
+                 features, grads, grad_far, grad_near, sems):
+    core, chip, _ = bits()
+    size = f0.shape[0]
+    width = far.shape[1]
+    copies = [
+        (piece, to.at[block(chip ^ mask, size)])
+        for to, parts in ((features, (f0, f1, f2, f3)), (grads, (g0, g1, g2, g3)))
+        for mask, piece in enumerate(parts)
+    ]
+
+    def place(swapped):
+        columns = [
+            (part, out.at[:, pl.ds((k ^ swapped) * width, width)])
+            for out, parts in ((grad_far, (far, far_got)), (grad_near, (near, near_got)))
+            for k, part in enumerate(parts)
+        ]
         run_copies(
-            [
-                pltpu.make_async_copy(part, out.at[:, pl.ds(k * width, width)], done.at[k])
-                for k, part in enumerate((left, right))
-            ]
-            + list(others)
+            [pltpu.make_async_copy(*pair, sems.at[k]) for k, pair in enumerate(copies + columns)]
         )
 
     @pl.when(core == 0)
     def _():
-        place(own, got)
+        place(0)
 
     @pl.when(core != 0)
     def _():
-        place(got, own)
-
-
-def columns_body(ids, own, got, out, done):
-    place_columns(bits(ids)[0], own, got, out, done)
-
-
-def collect_body(ids, f0, f1, f2, f3, g0, g1, g2, g3, own, got, features, grads, out, done, moved):
-    core, chip, _ = bits(ids)
-    size = f0.shape[0]
-    copies = [
-        pltpu.make_async_copy(piece, to.at[block(chip ^ mask, size)], moved.at[4 * k + mask])
-        for k, (to, parts) in enumerate(((features, (f0, f1, f2, f3)), (grads, (g0, g1, g2, g3))))
-        for mask, piece in enumerate(parts)
-    ]
-    place_columns(core, own, got, out, done, copies)
+        place(1)
 
 
 def pieces(field, chip):
@@ -377,8 +369,6 @@
     tall = near_weight.shape[0]
     part = tall // n_lo
     hi = lax.axis_index("hi")
-    lo = lax.axis_index("lo")
-    ids = jnp.stack([hi, lo])
     chip = lax.shift_right_logical(hi, 1)
     scale = 1.0 / float(rows * n_hi * n_lo) ** 0.5
     full, piece = (rows, width), (size, width)
@@ -388,7 +378,7 @@
     other = [swap(own[mask], "hi", 1) for mask in range(4)]
     out = hbm_call(
         weights_body, [(near_weight.shape, BF16)] * 4 + [(piece, F32)] * 4, (pltpu.HBM, pltpu.VMEM),
-        ids, (near_weight, far_weight, cotangent),
+        (near_weight, far_weight, cotangent),
         [pltpu.VMEM((8, tall // 4, width), F32), pltpu.SemaphoreType.DMA((8,)), pltpu.SemaphoreType.DMA((4,))], 8,
     )
     near_h, near_l, far_h, far_l = out[:4]
@@ -397,33 +387,31 @@
     out = call(
         forward_body,
         [(piece, F32)] * 4 + [(full, F32)] * 2 + [(full, BF16)] * 2 + [(padded, BF16)] * 4,
-        ids, *own, *other, *near_w, *far_w, scratch=[(full, F32)], room=16,
+        *own, *other, *near_w, *far_w, scratch=[(full, F32)], room=16,
     )
     feats, slope_near, slope_far = over_chips(out[:4]), out[4], out[5]
     hid, own_pair, oth_pair = out[6:8], out[8:10], out[10:12]
     cot, g_h, g_l, far_other = call(
         far_other_body, [(full, F32), (full, BF16), (full, BF16), ((tall, half), F32)],
-        ids, *cot, slope_far, *hid,
+        *cot, slope_far, *hid,
     )
     far_got = swap(far_other, "hi", 1)
     halves = [((n_lo, part // 2, half), F32)] * 2
-    far_keep, far_send = call(
-        far_own_body, halves, ids, *hid, g_h, g_l, far_got, scratch=[((tall, half), F32)], room=12
-    )
+    far_keep, far_send = call(far_own_body, halves, *hid, g_h, g_l, far_got, scratch=[((tall, half), F32)], room=12)
     far_got = plane_swap(far_send, 0)
     grad, gn, gn_h, gn_l = call(
         backward_body, [(full, F32), (full, F32), (full, BF16), (full, BF16)],
-        ids, cot, g_h, g_l, *far_w, slope_near,
+        cot, g_h, g_l, *far_w, slope_near,
     )
     gn_got = swap(gn, "hi", 1)
-    (near_term,) = call(near_mine_body, [((tall, half), F32)], ids, *own_pair, *oth_pair, gn_h, gn_l)
+    (near_term,) = call(near_mine_body, [((tall, half), F32)], *own_pair, *oth_pair, gn_h, gn_l)
     near_keep, near_send = call(
-        near_both_body, halves, ids, near_term, *own_pair, *oth_pair, gn_got,
+        near_both_body, halves, near_term, *own_pair, *oth_pair, gn_got,
         scratch=[((tall, half), F32)], room=12,
     )
     near_got = plane_swap(near_send, 0)
     grads = call(
-        track_body, [(piece, F32)] * 4, ids, grad, gn_h, gn_l, gn_got, *near_w,
+        track_body, [(piece, F32)] * 4, grad, gn_h, gn_l, gn_got, *near_w,
         scratch=[(padded, BF16), (padded, BF16), (full, F32)], room=12,
     )
     grads = over_chips(grads)
@@ -433,31 +421,27 @@
 
     def lo_sum(kept, got):
         one = [(kept.shape[1:], F32)]
-        parts = call(pick_body, one * 4, ids, kept, got)
+        parts = call(pick_body, one * 4, kept, got)
         parts = [parts[0]] + [swap(parts[mask], "lo", mask) for mask in (1, 2, 3)]
-        return call(scaled_total, one, ids, *parts)[0]
+        return call(scaled_total, one, *parts)[0]
 
     far_mine = lo_sum(far_keep, far_got)
     wide_half = [((part // 2, half), F32)]
-    (far_mine,) = call(cross_body, wide_half, ids, far_mine, plane_swap(far_mine, 1))
+    (far_mine,) = call(cross_body, wide_half, far_mine, plane_swap(far_mine, 1))
     rows_all = [((part, half), F32)]
-    (rows_far,) = call(far_rows_body, rows_all, ids, far_mine, plane_swap(far_mine, 0))
+    (rows_far,) = call(far_rows_body, rows_all, far_mine, plane_swap(far_mine, 0))
     far_cols = swap(rows_far, "hi", 1)
     quarters = [((n_lo, part // 4, half), F32)] * 2
-    near_keep, near_send = call(plane_body, quarters, ids, near_keep, near_got)
+    near_keep, near_send = call(plane_body, quarters, near_keep, near_got)
     near_mine = lo_sum(near_keep, plane_swap(near_send, 1))
     near_all = over_chips([near_mine] * 4)
-    (rows_near,) = call(near_rows_body, rows_all, ids, *near_all)
+    (rows_near,) = call(near_rows_body, rows_all, *near_all)
     near_cols = swap(rows_near, "hi", 1)
-    to_hbm = (pltpu.VMEM, pltpu.HBM)
-    to_hbm = (pltpu.VMEM, pltpu.HBM)
     wide = ((part, width), F32)
-    sems = [pltpu.SemaphoreType.DMA((2,))]
-    features, grad_track, grad_far = hbm_call(
-        collect_body, [(full, F32)] * 2 + [wide], to_hbm, ids, (*feats, *grads, rows_far, far_cols),
-        sems + [pltpu.SemaphoreType.DMA((8,))], 2,
-    )
-    (grad_near,) = hbm_call(columns_body, [wide], to_hbm, ids, (rows_near, near_cols), sems, 2)
+    features, grad_track, grad_far, grad_near = hbm_call(
+        collect_body, [(full, F32)] * 2 + [wide] * 2, (pltpu.VMEM, pltpu.HBM),
+        (*feats, *grads, rows_far, far_cols, rows_near, near_cols), [pltpu.SemaphoreType.DMA((12,))], 2,
+    )
     return features, grad_track, grad_near, grad_far
 
 

time: 120 us -> 112 us (0.933)
  Pallas kernels: 25.6 us -> 15.2 us
  starting transfers between devices: 35.5 us -> 37.7 us
    pallas_call x15, Pallas kernels: 18.6 us -> 10.4 us  [call(): pl.pallas_call(body, out_shape=[make(shape, dtype) for shape, dtype in ou...]
    ppermute x29, starting transfers between devices: 29.3 us -> 31.8 us  [swap(): return lax.ppermute(value, axis, [(i, i ^ mask) for i in range(count)])]
    pallas_call x3 -> x2, Pallas kernels: 7.02 us -> 4.77 us  [hbm_call(): pl.pallas_call(body, out_shape=[out_place(shape, dtype) for shape, dtype...]
    ppermute x29, waiting for transfers between devices: 35.8 us -> 37.3 us  [swap(): return lax.ppermute(value, axis, [(i, i ^ mask) for i in range(count)])]
  transfers between devices with their start and end apart: 34 -> 34, of which waited for: 18 -> 15; matrix products, arithmetic and copies ran while one was open for 0% -> 0% of each run, Pallas kernels for 19% -> 11%
where the time goes in v2:
time: 112 us
  waiting for transfers between devices  57.1 us (51%)
  starting transfers between devices  37.7 us (34%)
  Pallas kernels  15.2 us (14%)
  local copies, waits for them, and re-layouts  1.14 us (1%)
    ppermute x29, waiting for transfers between devices, swap(): return lax.ppermute(value, axis, [(i, i ^ mask) for i in range(count)])  37.3 us
    ppermute x29, starting transfers between devices, swap(): return lax.ppermute(value, axis, [(i, i ^ mask) for i in range(count)])  31.8 us
    ppermute x5, waiting for transfers between devices, plane_swap(): lax.ppermute(value, 'hi', [(i, i ^ 2 << (i + turn) % 2) for i in range(co...  19.8 us
    pallas_call x15, Pallas kernels, call(): pl.pallas_call(body, out_shape=[make(shape, dtype) for shape, dtype in ou...  10.4 us
    ppermute x5, starting transfers between devices, plane_swap(): lax.ppermute(value, 'hi', [(i, i ^ 2 << (i + turn) % 2) for i in range(co...  5.92 us
    pallas_call x2, Pallas kernels, hbm_call(): pl.pallas_call(body, out_shape=[out_place(shape, dtype) for shape, dtype...  4.77 us
  transfers between devices with their start and end apart: 34, of which 15 were waited for; matrix products, arithmetic and copies ran while one was open for 0% of the time, Pallas kernels for 11%

profile of v2, /device:TPU:0, one launch (start us, length us, event | category | flops | bytes accessed | tf_op | source)
XLA Modules:
  0.0 112.0 jit_solution(6478689372995823237)
XLA Ops:
  0.7 1.1 %constant_dynamic-slice_fusion = (f32[64,512]{1,0:T(8,128)S(1)}, f32[64,512]{1,0:T(8,128)S(1)}, f32[64,512]{1,0:T(8,128)S(1)}, f32[64,512]{1,0:T(8,128)S(1)}) fusion(f32[256,512]{1,0:T(8,128)} %param.4, s32[]{:T(128)S(6)} %select_n.15, s32[]{:T(128)S(6)} %select_n.13, s32[]{:T(128)S(6)} %select_n.12, s32[]{:T(128)S(6)} %select_n.14), kind=kLoop, calls=%fused_computation | loop fusion | bytes 1048592 | tf_op jit(solution)/shard_map/dynamic_slice | solution.py:352
  1.8 4.0 %collective-permute-start.2 = (f32[64,512]{1,0:T(8,128)S(1)}, f32[64,512]{1,0:T(8,128)S(1)}, u32[]{:S(2)}, u32[]{:S(2)}) collective-permute-start(f32[64,512]{1,0:T(8,128)S(1)} %get-tuple-element.104), channel_id=1, source_target_pairs={{0,24},{4,28},{8,16},{12,20},{16,8},{20,12},{24,0},{28,4},{1,25},{... | collective-permute-start | bytes 393224 | tf_op jit(solution)/shard_map/ppermute | solution.py:41
  5.8 0.5 collective-permute-start
  6.3 0.1 collective-permute-start.1
  6.4 0.0 collective-permute-start.3
  6.4 3.7 %collective-permute-done.2.p3 = f32[64,512]{1,0:T(8,128)S(1)} collective-permute-done((f32[64,512]{1,0:T(8,128)S(1)}, f32[64,512]{1,0:T(8,128)S(1)}, u32[]{:S(2)}, u32[]{:S(2)}) %collective-permute-start.2) | collective-permute-done | bytes 131104 | tf_op jit(solution)/shard_map/ppermute | solution.py:41
  10.1 3.2 %shard_map.75 = (bf16[1536,512]{1,0:T(8,128)(2,1)S(1)}, bf16[1536,512]{1,0:T(8,128)(2,1)S(1)}, bf16[1536,512]{1,0:T(8,128)(2,1)S(1)}, bf16[1536,512]{1,0:T(8,128...) custom-call(f32[1536,512]{1,0:T(8,128)} %near.1, ...), custom_call_target="tpu_custom_call" | custom-call | tf_op jit(solution)/shard_map/pallas_call | solution.py:116
  13.3 0.0 collective-permute-done.p1
  13.3 0.6 collective-permute-start.4
  13.9 0.1 collective-permute-start.5
  14.0 2.0 %collective-permute-start.10 = (f32[64,512]{1,0:T(8,128)S(1)}, f32[64,512]{1,0:T(8,128)S(1)}, u32[]{:S(2)}, u32[]{:S(2)}) collective-permute-start(f32[64,512]{1,0:T(8,128)S(1)} %get-tuple-element.63), channel_id=1, source_target_pairs={{0,8},{4,12},{8,0},{12,4},{16,24},{20,28},{24,16},{28,20},{1,9},{5... | collective-permute-start | bytes 393224 | tf_op jit(solution)/shard_map/ppermute | solution.py:41
  16.0 1.5 %collective-permute-start.11 = (f32[64,512]{1,0:T(8,128)S(1)}, f32[64,512]{1,0:T(8,128)S(1)}, u32[]{:S(2)}, u32[]{:S(2)}) collective-permute-start(f32[64,512]{1,0:T(8,128)S(1)} %get-tuple-element.64), channel_id=1, source_target_pairs={{0,16},{4,20},{8,24},{12,28},{16,0},{20,4},{24,8},{28,12},{1,17},{... | collective-permute-start | bytes 393224 | tf_op jit(solution)/shard_map/ppermute | solution.py:41
  17.5 0.0 collective-permute-start.12
  17.5 3.1 %shard_map.76 = (f32[64,512]{1,0:T(8,128)S(1)}, f32[64,512]{1,0:T(8,128)S(1)}, f32[64,512]{1,0:T(8,128)S(1)}, f32[64,512]{1,0:T(8,128)S(1)}, f32[256,512]{1,0:T(...) custom-call(f32[64,512]{1,0:T(8,128)S(1)} %get-tuple-element.106.p0,, ...), custom_call_target="tpu_custom_call" | custom-call | tf_op jit(solution)/shard_map/pallas_call | solution.py:29
  20.7 3.7 %collective-permute-done.11.c2 = f32[64,512]{1,0:T(8,128)S(1)} collective-permute-done((f32[64,512]{1,0:T(8,128)S(1)}, f32[64,512]{1,0:T(8,128)S(1)}, u32[]{:S(2)}, u32[]{:S(2)}) %collective-permute-start.11) | collective-permute-done | bytes 131104 | tf_op jit(solution)/shard_map/ppermute | solution.py:41
  24.3 0.9 shard_map.77
  25.2 0.1 collective-permute-start.17
  25.3 1.6 %shard_map.78 = (f32[256,512]{1,0:T(8,128)S(1)}, f32[256,512]{1,0:T(8,128)S(1)}, bf16[256,512]{1,0:T(8,128)(2,1)S(1)}, bf16[256,512]{1,0:T(8,128)(2,1)S(1)}) custom-call(f32[256,512]{1,0:T(8,128)S(1)} %get-tuple-element.69.cot, bf16[256,512]{1,0:T(8,128)(2,1)S(1)} %get-tuple-element.70.g_h, bf16[256,512]{1,0:T(8,128)(2,1)S(1)} %get-tuple-element.71.g_l, ...), custom_call_target="tpu_custom_call" | custom-call | tf_op jit(solution)/shard_map/pallas_call | solution.py:29
  26.9 0.6 collective-permute-start.13
  27.5 0.8 shard_map.85.term
  28.3 1.1 %collective-permute-done.13.other = f32[256,512]{1,0:T(8,128)S(1)} collective-permute-done((f32[256,512]{1,0:T(8,128)S(1)}, f32[256,512]{1,0:T(8,128)S(1)}, u32[]{:S(2)}, u32[]{:S(2)}) %collective-permute-start.13) | collective-permute-done | bytes 524320 | tf_op jit(solution)/shard_map/ppermute | solution.py:41
  29.5 1.1 shard_map.86
  30.6 1.3 %collective-permute-start.25 = (f32[4,192,256]{2,1,0:T(8,128)S(1)}, f32[4,192,256]{2,1,0:T(8,128)S(1)}, u32[]{:S(2)}, u32[]{:S(2)}) collective-permute-start(f32[4,192,256]{2,1,0:T(8,128)S(1)} %get-tuple-element.93), channel_id=1, source_target_pairs={{0,8},{4,20},{8,0},{12,28},{16,24},{20,4},{24,16},{28,12},{1,9},{5... | collective-permute-start | bytes 2359304 | tf_op jit(solution)/shard_map/ppermute | solution.py:46
  31.9 0.0 collective-permute-done.17.got
  31.9 1.1 shard_map.80
  32.9 0.9 collective-permute-start.18
  33.8 8.8 %collective-permute-done.25.got = f32[4,192,256]{2,1,0:T(8,128)S(1)} collective-permute-done((f32[4,192,256]{2,1,0:T(8,128)S(1)}, f32[4,192,256]{2,1,0:T(8,128)S(1)}, u32[]{:S(2)}, u32[]{:S(2)}) %collective-permute-start.25) | collective-permute-done | bytes 786464 | tf_op jit(solution)/shard_map/ppermute | solution.py:46
  42.6 0.1 shard_map.87
  42.7 1.6 %collective-permute-start.26 = (f32[4,96,256]{2,1,0:T(8,128)S(1)}, f32[4,96,256]{2,1,0:T(8,128)S(1)}, u32[]{:S(2)}, u32[]{:S(2)}) collective-permute-start(f32[4,96,256]{2,1,0:T(8,128)S(1)} %get-tuple-element.95), channel_id=1, source_target_pairs={{0,16},{4,12},{8,24},{12,4},{16,0},{20,28},{24,8},{28,20},{1,17},{... | collective-permute-start | bytes 1179656 | tf_op jit(solution)/shard_map/ppermute | solution.py:46
  44.3 11.0 %collective-permute-done.18.got = f32[4,192,256]{2,1,0:T(8,128)S(1)} collective-permute-done((f32[4,192,256]{2,1,0:T(8,128)S(1)}, f32[4,192,256]{2,1,0:T(8,128)S(1)}, u32[]{:S(2)}, u32[]{:S(2)}) %collective-permute-start.18) | collective-permute-done | bytes 786464 | tf_op jit(solution)/shard_map/ppermute | solution.py:46
  55.3 0.1 shard_map.81
  55.3 1.6 %collective-permute-start.19 = (f32[192,256]{1,0:T(8,128)S(1)}, f32[192,256]{1,0:T(8,128)S(1)}, u32[]{:S(2)}, u32[]{:S(2)}) collective-permute-start(f32[192,256]{1,0:T(8,128)S(1)} %get-tuple-element.85), channel_id=1, source_target_pairs={{0,1},{1,0},{2,3},{3,2},{4,5},{5,4},{6,7},{7,6},{8,9},{9,8},{10,11... | collective-permute-start | bytes 589832 | tf_op jit(solution)/shard_map/ppermute | solution.py:41
  57.0 2.6 %collective-permute-start.20 = (f32[192,256]{1,0:T(8,128)S(1)}, f32[192,256]{1,0:T(8,128)S(1)}, u32[]{:S(2)}, u32[]{:S(2)}) collective-permute-start(f32[192,256]{1,0:T(8,128)S(1)} %get-tuple-element.86), channel_id=1, source_target_pairs={{0,2},{1,3},{2,0},{3,1},{4,6},{5,7},{6,4},{7,5},{8,10},{9,11},{10,... | collective-permute-start | bytes 589832 | tf_op jit(solution)/shard_map/ppermute | solution.py:41
  59.6 0.2 collective-permute-start.21
  59.8 4.1 %collective-permute-done.19.refs_1_ = f32[192,256]{1,0:T(8,128)S(1)} collective-permute-done((f32[192,256]{1,0:T(8,128)S(1)}, f32[192,256]{1,0:T(8,128)S(1)}, u32[]{:S(2)}, u32[]{:S(2)}) %collective-permute-start.19) | collective-permute-done | bytes 196640 | tf_op jit(solution)/shard_map/ppermute | solution.py:41
  63.9 10.1 %collective-permute-done.20.refs_2_ = f32[192,256]{1,0:T(8,128)S(1)} collective-permute-done((f32[192,256]{1,0:T(8,128)S(1)}, f32[192,256]{1,0:T(8,128)S(1)}, u32[]{:S(2)}, u32[]{:S(2)}) %collective-permute-start.20) | collective-permute-done | bytes 196640 | tf_op jit(solution)/shard_map/ppermute | solution.py:41
  74.0 1.6 %collective-permute-start.22 = (f32[192,256]{1,0:T(8,128)S(1)}, f32[192,256]{1,0:T(8,128)S(1)}, u32[]{:S(2)}, u32[]{:S(2)}) collective-permute-start(f32[192,256]{1,0:T(8,128)S(1)} %shard_map.82.own), channel_id=1, source_target_pairs={{0,16},{4,12},{8,24},{12,4},{16,0},{20,28},{24,8},{28,20},{1,17},{... | collective-permute-start | bytes 589832 | tf_op jit(solution)/shard_map/ppermute | solution.py:46
  75.6 0.0 collective-permute-done.26.got
  75.6 2.7 %collective-permute-start.27 = (f32[96,256]{1,0:T(8,128)S(1)}, f32[96,256]{1,0:T(8,128)S(1)}, u32[]{:S(2)}, u32[]{:S(2)}) collective-permute-start(f32[96,256]{1,0:T(8,128)S(1)} %get-tuple-element.97), channel_id=1, source_target_pairs={{0,1},{1,0},{2,3},{3,2},{4,5},{5,4},{6,7},{7,6},{8,9},{9,8},{10,11... | collective-permute-start | bytes 294920 | tf_op jit(solution)/shard_map/ppermute | solution.py:41
  78.3 1.1 collective-permute-start.28
  79.4 1.4 %collective-permute-start.29 = (f32[96,256]{1,0:T(8,128)S(1)}, f32[96,256]{1,0:T(8,128)S(1)}, u32[]{:S(2)}, u32[]{:S(2)}) collective-permute-start(f32[96,256]{1,0:T(8,128)S(1)} %get-tuple-element.99), channel_id=1, source_target_pairs={{0,3},{1,2},{2,1},{3,0},{4,7},{5,6},{6,5},{7,4},{8,11},{9,10},{10,... | collective-permute-start | bytes 294920 | tf_op jit(solution)/shard_map/ppermute | solution.py:41
  80.8 0.0 collective-permute-done.22.got
  80.8 0.6 collective-permute-start.23
  81.4 5.2 %collective-permute-done.28.refs_2_ = f32[96,256]{1,0:T(8,128)S(1)} collective-permute-done((f32[96,256]{1,0:T(8,128)S(1)}, f32[96,256]{1,0:T(8,128)S(1)}, u32[]{:S(2)}, u32[]{:S(2)}) %collective-permute-start.28) | collective-permute-done | bytes 98336 | tf_op jit(solution)/shard_map/ppermute | solution.py:41
  86.7 1.8 %collective-permute-start.32 = (f32[96,256]{1,0:T(8,128)S(1)}, f32[96,256]{1,0:T(8,128)S(1)}, u32[]{:S(2)}, u32[]{:S(2)}) collective-permute-start(f32[96,256]{1,0:T(8,128)S(1)} %shard_map.89.s0), channel_id=1, source_target_pairs={{0,24},{4,28},{8,16},{12,20},{16,8},{20,12},{24,0},{28,4},{1,25},{... | collective-permute-start | bytes 294920 | tf_op jit(solution)/shard_map/ppermute | solution.py:41
  88.5 0.5 collective-permute-start.31
  89.0 1.2 %collective-permute-start.30 = (f32[96,256]{1,0:T(8,128)S(1)}, f32[96,256]{1,0:T(8,128)S(1)}, u32[]{:S(2)}, u32[]{:S(2)}) collective-permute-start(f32[96,256]{1,0:T(8,128)S(1)} %shard_map.89.s0), channel_id=1, source_target_pairs={{0,8},{4,12},{8,0},{12,4},{16,24},{20,28},{24,16},{28,20},{1,9},{5... | collective-permute-start | bytes 294920 | tf_op jit(solution)/shard_map/ppermute | solution.py:41
  90.2 2.0 %collective-permute-done.32.s3 = f32[96,256]{1,0:T(8,128)S(1)} collective-permute-done((f32[96,256]{1,0:T(8,128)S(1)}, f32[96,256]{1,0:T(8,128)S(1)}, u32[]{:S(2)}, u32[]{:S(2)}) %collective-permute-start.32) | collective-permute-done | bytes 98336 | tf_op jit(solution)/shard_map/ppermute | solution.py:41
  92.3 1.0 collective-permute-done.31.s2
  93.3 0.3 collective-permute-done.30.s1
  93.7 0.1 collective-permute-start.33
  93.8 0.5 collective-permute-start.24
  94.4 1.2 %collective-permute-start.7 = (f32[64,512]{1,0:T(8,128)S(1)}, f32[64,512]{1,0:T(8,128)S(1)}, u32[]{:S(2)}, u32[]{:S(2)}) collective-permute-start(f32[64,512]{1,0:T(8,128)S(1)} %get-tuple-element.59), channel_id=1, source_target_pairs={{0,8},{4,12},{8,0},{12,4},{16,24},{20,28},{24,16},{28,20},{1,9},{5... | collective-permute-start | bytes 393224 | tf_op jit(solution)/shard_map/ppermute | solution.py:41
  95.6 0.8 collective-permute-start.8
  96.4 1.4 %collective-permute-start.9 = (f32[64,512]{1,0:T(8,128)S(1)}, f32[64,512]{1,0:T(8,128)S(1)}, u32[]{:S(2)}, u32[]{:S(2)}) collective-permute-start(f32[64,512]{1,0:T(8,128)S(1)} %get-tuple-element.61), channel_id=1, source_target_pairs={{0,24},{4,28},{8,16},{12,20},{16,8},{20,12},{24,0},{28,4},{1,25},{... | collective-permute-start | bytes 393224 | tf_op jit(solution)/shard_map/ppermute | solution.py:41
  97.9 1.4 %shard_map.79 = (f32[64,512]{1,0:T(8,128)S(1)}, f32[64,512]{1,0:T(8,128)S(1)}, f32[64,512]{1,0:T(8,128)S(1)}, f32[64,512]{1,0:T(8,128)S(1)}) custom-call(f32[256,512]{1,0:T(8,128)S(1)} %get-tuple-element.73.grad, bf16[256,512]{1,0:T(8,128)(2,1)S(1)} %get-tuple-element.74.gn_h, bf16[256,512]{1,0:T(8,128)(2,1)S(1)} %get-tuple-element.75.gn_l, ...), custom_call_target="tpu_custom_call" | custom-call | tf_op jit(solution)/shard_map/pallas_call | solution.py:29
  99.3 1.2 %collective-permute-done.7.f1 = f32[64,512]{1,0:T(8,128)S(1)} collective-permute-done((f32[64,512]{1,0:T(8,128)S(1)}, f32[64,512]{1,0:T(8,128)S(1)}, u32[]{:S(2)}, u32[]{:S(2)}) %collective-permute-start.7) | collective-permute-done | bytes 131104 | tf_op jit(solution)/shard_map/ppermute | solution.py:41
  100.5 1.5 %collective-permute-start.14 = (f32[64,512]{1,0:T(8,128)S(1)}, f32[64,512]{1,0:T(8,128)S(1)}, u32[]{:S(2)}, u32[]{:S(2)}) collective-permute-start(f32[64,512]{1,0:T(8,128)S(1)} %get-tuple-element.78), channel_id=1, source_target_pairs={{0,8},{4,12},{8,0},{12,4},{16,24},{20,28},{24,16},{28,20},{1,9},{5... | collective-permute-start | bytes 393224 | tf_op jit(solution)/shard_map/ppermute | solution.py:41
  102.0 2.4 %collective-permute-start.15 = (f32[64,512]{1,0:T(8,128)S(1)}, f32[64,512]{1,0:T(8,128)S(1)}, u32[]{:S(2)}, u32[]{:S(2)}) collective-permute-start(f32[64,512]{1,0:T(8,128)S(1)} %get-tuple-element.79), channel_id=1, source_target_pairs={{0,16},{4,20},{8,24},{12,28},{16,0},{20,4},{24,8},{28,12},{1,17},{... | collective-permute-start | bytes 393224 | tf_op jit(solution)/shard_map/ppermute | solution.py:41
  104.4 0.2 collective-permute-done.9.f3
  104.5 1.2 %collective-permute-start.16 = (f32[64,512]{1,0:T(8,128)S(1)}, f32[64,512]{1,0:T(8,128)S(1)}, u32[]{:S(2)}, u32[]{:S(2)}) collective-permute-start(f32[64,512]{1,0:T(8,128)S(1)} %get-tuple-element.80), channel_id=1, source_target_pairs={{0,24},{4,28},{8,16},{12,20},{16,8},{20,12},{24,0},{28,4},{1,25},{... | collective-permute-start | bytes 393224 | tf_op jit(solution)/shard_map/ppermute | solution.py:41
  105.7 3.0 %collective-permute-done.15.g2 = f32[64,512]{1,0:T(8,128)S(1)} collective-permute-done((f32[64,512]{1,0:T(8,128)S(1)}, f32[64,512]{1,0:T(8,128)S(1)}, u32[]{:S(2)}, u32[]{:S(2)}) %collective-permute-start.15) | collective-permute-done | bytes 131104 | tf_op jit(solution)/shard_map/ppermute | solution.py:41
  108.8 1.6 %collective-permute-done.16.g3 = f32[64,512]{1,0:T(8,128)S(1)} collective-permute-done((f32[64,512]{1,0:T(8,128)S(1)}, f32[64,512]{1,0:T(8,128)S(1)}, u32[]{:S(2)}, u32[]{:S(2)}) %collective-permute-start.16) | collective-permute-done | bytes 131104 | tf_op jit(solution)/shard_map/ppermute | solution.py:41
  110.4 1.6 %shard_map.91 = (f32[256,512]{1,0:T(8,128)}, f32[256,512]{1,0:T(8,128)}, f32[384,512]{1,0:T(8,128)}, f32[384,512]{1,0:T(8,128)}) custom-call(f32[64,512]{1,0:T(8,128)S(1)} %get-tuple-element.58.f0, f32[64,512]{1,0:T(8,128)S(1)} %collective-permute-done.7.f1, f32[64,512]{1,0:T(8,128)S(1)} %collective-permute-done.8.f2, ...), custom_call_target="tpu_custom_call" | custom-call | tf_op jit(solution)/shard_map/pallas_call | solution.py:116
  (22 shorter events, 0.2 us)
Async XLA Ops:
  1.8 8.3 %collective-permute-start.2 = (f32[64,512]{1,0:T(8,128)S(1)}, f32[64,512]{1,0:T(8,128)S(1)}, u32[]{:S(2)}, u32[]{:S(2)}) collective-permute-start(f32[64,512]{1,0:T(8,128)S(1)} %get-tuple-element.104), channel_id=1, source_target_pairs={{0,24},{4,28},{8,16},{12,20},{16,8},{20,12},{24,0},{28,4},{1,25},{... | collective-permute-start | bytes 393224 | tf_op jit(solution)/shard_map/ppermute | solution.py:41
  5.8 7.6 %collective-permute-start = (f32[64,512]{1,0:T(8,128)S(1)}, f32[64,512]{1,0:T(8,128)S(1)}, u32[]{:S(2)}, u32[]{:S(2)}) collective-permute-start(f32[64,512]{1,0:T(8,128)S(1)} %get-tuple-element.105), channel_id=1, source_target_pairs={{0,8},{4,12},{8,0},{12,4},{16,24},{20,28},{24,16},{28,20},{1,9},{5... | collective-permute-start | bytes 393224 | tf_op jit(solution)/shard_map/ppermute | solution.py:41
  6.3 7.6 %collective-permute-start.1 = (f32[64,512]{1,0:T(8,128)S(1)}, f32[64,512]{1,0:T(8,128)S(1)}, u32[]{:S(2)}, u32[]{:S(2)}) collective-permute-start(f32[64,512]{1,0:T(8,128)S(1)} %get-tuple-element.107), channel_id=1, source_target_pairs={{0,16},{4,20},{8,24},{12,28},{16,0},{20,4},{24,8},{28,12},{1,17},{... | collective-permute-start | bytes 393224 | tf_op jit(solution)/shard_map/ppermute | solution.py:41
  6.4 9.5 %collective-permute-start.3 = (f32[64,512]{1,0:T(8,128)S(1)}, f32[64,512]{1,0:T(8,128)S(1)}, u32[]{:S(2)}, u32[]{:S(2)}) collective-permute-start(f32[64,512]{1,0:T(8,128)S(1)} %get-tuple-element.106.p0), channel_id=1, source_target_pairs={{0,4},{4,0},{8,12},{12,8},{16,20},{20,16},{24,28},{28,24},{1,5},{5... | collective-permute-start | bytes 393224 | tf_op jit(solution)/shard_map/ppermute | solution.py:41
  10.1 7.4 %collective-permute-start.6 = (f32[64,512]{1,0:T(8,128)S(1)}, f32[64,512]{1,0:T(8,128)S(1)}, u32[]{:S(2)}, u32[]{:S(2)}) collective-permute-start(f32[64,512]{1,0:T(8,128)S(1)} %collective-permute-done.2.p3), channel_id=1, source_target_pairs={{0,4},{4,0},{8,12},{12,8},{16,20},{20,16},{24,28},{28,24},{1,5},{5... | collective-permute-start | bytes 393224 | tf_op jit(solution)/shard_map/ppermute | solution.py:41
  13.3 4.2 %collective-permute-start.4 = (f32[64,512]{1,0:T(8,128)S(1)}, f32[64,512]{1,0:T(8,128)S(1)}, u32[]{:S(2)}, u32[]{:S(2)}) collective-permute-start(f32[64,512]{1,0:T(8,128)S(1)} %collective-permute-done.p1), channel_id=1, source_target_pairs={{0,4},{4,0},{8,12},{12,8},{16,20},{20,16},{24,28},{28,24},{1,5},{5... | collective-permute-start | bytes 393224 | tf_op jit(solution)/shard_map/ppermute | solution.py:41
  13.9 3.6 %collective-permute-start.5 = (f32[64,512]{1,0:T(8,128)S(1)}, f32[64,512]{1,0:T(8,128)S(1)}, u32[]{:S(2)}, u32[]{:S(2)}) collective-permute-start(f32[64,512]{1,0:T(8,128)S(1)} %collective-permute-done.1.p2), channel_id=1, source_target_pairs={{0,4},{4,0},{8,12},{12,8},{16,20},{20,16},{24,28},{28,24},{1,5},{5... | collective-permute-start | bytes 393224 | tf_op jit(solution)/shard_map/ppermute | solution.py:41
  14.0 6.6 %collective-permute-start.10 = (f32[64,512]{1,0:T(8,128)S(1)}, f32[64,512]{1,0:T(8,128)S(1)}, u32[]{:S(2)}, u32[]{:S(2)}) collective-permute-start(f32[64,512]{1,0:T(8,128)S(1)} %get-tuple-element.63), channel_id=1, source_target_pairs={{0,8},{4,12},{8,0},{12,4},{16,24},{20,28},{24,16},{28,20},{1,9},{5... | collective-permute-start | bytes 393224 | tf_op jit(solution)/shard_map/ppermute | solution.py:41
  16.0 8.4 %collective-permute-start.11 = (f32[64,512]{1,0:T(8,128)S(1)}, f32[64,512]{1,0:T(8,128)S(1)}, u32[]{:S(2)}, u32[]{:S(2)}) collective-permute-start(f32[64,512]{1,0:T(8,128)S(1)} %get-tuple-element.64), channel_id=1, source_target_pairs={{0,16},{4,20},{8,24},{12,28},{16,0},{20,4},{24,8},{28,12},{1,17},{... | collective-permute-start | bytes 393224 | tf_op jit(solution)/shard_map/ppermute | solution.py:41
  17.5 6.8 %collective-permute-start.12 = (f32[64,512]{1,0:T(8,128)S(1)}, f32[64,512]{1,0:T(8,128)S(1)}, u32[]{:S(2)}, u32[]{:S(2)}) collective-permute-start(f32[64,512]{1,0:T(8,128)S(1)} %get-tuple-element.65), channel_id=1, source_target_pairs={{0,24},{4,28},{8,16},{12,20},{16,8},{20,12},{24,0},{28,4},{1,25},{... | collective-permute-start | bytes 393224 | tf_op jit(solution)/shard_map/ppermute | solution.py:41
  25.2 6.6 %collective-permute-start.17 = (f32[1536,256]{1,0:T(8,128)S(1)}, f32[1536,256]{1,0:T(8,128)S(1)}, u32[]{:S(2)}, u32[]{:S(2)}) collective-permute-start(f32[1536,256]{1,0:T(8,128)S(1)} %get-tuple-element.81), channel_id=1, source_target_pairs={{0,4},{4,0},{8,12},{12,8},{16,20},{20,16},{24,28},{28,24},{1,5},{5... | collective-permute-start | bytes 4718600 | tf_op jit(solution)/shard_map/ppermute | solution.py:41
  26.9 2.5 %collective-permute-start.13 = (f32[256,512]{1,0:T(8,128)S(1)}, f32[256,512]{1,0:T(8,128)S(1)}, u32[]{:S(2)}, u32[]{:S(2)}) collective-permute-start(f32[256,512]{1,0:T(8,128)S(1)} %get-tuple-element.76), channel_id=1, source_target_pairs={{0,4},{4,0},{8,12},{12,8},{16,20},{20,16},{24,28},{28,24},{1,5},{5... | collective-permute-start | bytes 1572872 | tf_op jit(solution)/shard_map/ppermute | solution.py:41
  30.6 12.1 %collective-permute-start.25 = (f32[4,192,256]{2,1,0:T(8,128)S(1)}, f32[4,192,256]{2,1,0:T(8,128)S(1)}, u32[]{:S(2)}, u32[]{:S(2)}) collective-permute-start(f32[4,192,256]{2,1,0:T(8,128)S(1)} %get-tuple-element.93), channel_id=1, source_target_pairs={{0,8},{4,20},{8,0},{12,28},{16,24},{20,4},{24,16},{28,12},{1,9},{5... | collective-permute-start | bytes 2359304 | tf_op jit(solution)/shard_map/ppermute | solution.py:46
  32.9 22.3 %collective-permute-start.18 = (f32[4,192,256]{2,1,0:T(8,128)S(1)}, f32[4,192,256]{2,1,0:T(8,128)S(1)}, u32[]{:S(2)}, u32[]{:S(2)}) collective-permute-start(f32[4,192,256]{2,1,0:T(8,128)S(1)} %get-tuple-element.83), channel_id=1, source_target_pairs={{0,8},{4,20},{8,0},{12,28},{16,24},{20,4},{24,16},{28,12},{1,9},{5... | collective-permute-start | bytes 2359304 | tf_op jit(solution)/shard_map/ppermute | solution.py:46
  42.7 32.9 %collective-permute-start.26 = (f32[4,96,256]{2,1,0:T(8,128)S(1)}, f32[4,96,256]{2,1,0:T(8,128)S(1)}, u32[]{:S(2)}, u32[]{:S(2)}) collective-permute-start(f32[4,96,256]{2,1,0:T(8,128)S(1)} %get-tuple-element.95), channel_id=1, source_target_pairs={{0,16},{4,12},{8,24},{12,4},{16,0},{20,28},{24,8},{28,20},{1,17},{... | collective-permute-start | bytes 1179656 | tf_op jit(solution)/shard_map/ppermute | solution.py:46
  55.3 8.5 %collective-permute-start.19 = (f32[192,256]{1,0:T(8,128)S(1)}, f32[192,256]{1,0:T(8,128)S(1)}, u32[]{:S(2)}, u32[]{:S(2)}) collective-permute-start(f32[192,256]{1,0:T(8,128)S(1)} %get-tuple-element.85), channel_id=1, source_target_pairs={{0,1},{1,0},{2,3},{3,2},{4,5},{5,4},{6,7},{7,6},{8,9},{9,8},{10,11... | collective-permute-start | bytes 589832 | tf_op jit(solution)/shard_map/ppermute | solution.py:41
  57.0 16.9 %collective-permute-start.20 = (f32[192,256]{1,0:T(8,128)S(1)}, f32[192,256]{1,0:T(8,128)S(1)}, u32[]{:S(2)}, u32[]{:S(2)}) collective-permute-start(f32[192,256]{1,0:T(8,128)S(1)} %get-tuple-element.86), channel_id=1, source_target_pairs={{0,2},{1,3},{2,0},{3,1},{4,6},{5,7},{6,4},{7,5},{8,10},{9,11},{10,... | collective-permute-start | bytes 589832 | tf_op jit(solution)/shard_map/ppermute | solution.py:41
  59.6 14.4 %collective-permute-start.21 = (f32[192,256]{1,0:T(8,128)S(1)}, f32[192,256]{1,0:T(8,128)S(1)}, u32[]{:S(2)}, u32[]{:S(2)}) collective-permute-start(f32[192,256]{1,0:T(8,128)S(1)} %get-tuple-element.87), channel_id=1, source_target_pairs={{0,3},{1,2},{2,1},{3,0},{4,7},{5,6},{6,5},{7,4},{8,11},{9,10},{10,... | collective-permute-start | bytes 589832 | tf_op jit(solution)/shard_map/ppermute | solution.py:41
  74.0 6.9 %collective-permute-start.22 = (f32[192,256]{1,0:T(8,128)S(1)}, f32[192,256]{1,0:T(8,128)S(1)}, u32[]{:S(2)}, u32[]{:S(2)}) collective-permute-start(f32[192,256]{1,0:T(8,128)S(1)} %shard_map.82.own), channel_id=1, source_target_pairs={{0,16},{4,12},{8,24},{12,4},{16,0},{20,28},{24,8},{28,20},{1,17},{... | collective-permute-start | bytes 589832 | tf_op jit(solution)/shard_map/ppermute | solution.py:46
  75.6 5.8 %collective-permute-start.27 = (f32[96,256]{1,0:T(8,128)S(1)}, f32[96,256]{1,0:T(8,128)S(1)}, u32[]{:S(2)}, u32[]{:S(2)}) collective-permute-start(f32[96,256]{1,0:T(8,128)S(1)} %get-tuple-element.97), channel_id=1, source_target_pairs={{0,1},{1,0},{2,3},{3,2},{4,5},{5,4},{6,7},{7,6},{8,9},{9,8},{10,11... | collective-permute-start | bytes 294920 | tf_op jit(solution)/shard_map/ppermute | solution.py:41
  78.3 8.3 %collective-permute-start.28 = (f32[96,256]{1,0:T(8,128)S(1)}, f32[96,256]{1,0:T(8,128)S(1)}, u32[]{:S(2)}, u32[]{:S(2)}) collective-permute-start(f32[96,256]{1,0:T(8,128)S(1)} %get-tuple-element.98), channel_id=1, source_target_pairs={{0,2},{1,3},{2,0},{3,1},{4,6},{5,7},{6,4},{7,5},{8,10},{9,11},{10,... | collective-permute-start | bytes 294920 | tf_op jit(solution)/shard_map/ppermute | solution.py:41
  79.4 7.2 %collective-permute-start.29 = (f32[96,256]{1,0:T(8,128)S(1)}, f32[96,256]{1,0:T(8,128)S(1)}, u32[]{:S(2)}, u32[]{:S(2)}) collective-permute-start(f32[96,256]{1,0:T(8,128)S(1)} %get-tuple-element.99), channel_id=1, source_target_pairs={{0,3},{1,2},{2,1},{3,0},{4,7},{5,6},{6,5},{7,4},{8,11},{9,10},{10,... | collective-permute-start | bytes 294920 | tf_op jit(solution)/shard_map/ppermute | solution.py:41
  80.8 12.9 %collective-permute-start.23 = (f32[192,256]{1,0:T(8,128)S(1)}, f32[192,256]{1,0:T(8,128)S(1)}, u32[]{:S(2)}, u32[]{:S(2)}) collective-permute-start(f32[192,256]{1,0:T(8,128)S(1)} %shard_map.83.own), channel_id=1, source_target_pairs={{0,8},{4,20},{8,0},{12,28},{16,24},{20,4},{24,16},{28,12},{1,9},{5... | collective-permute-start | bytes 589832 | tf_op jit(solution)/shard_map/ppermute | solution.py:46
  86.7 5.6 %collective-permute-start.32 = (f32[96,256]{1,0:T(8,128)S(1)}, f32[96,256]{1,0:T(8,128)S(1)}, u32[]{:S(2)}, u32[]{:S(2)}) collective-permute-start(f32[96,256]{1,0:T(8,128)S(1)} %shard_map.89.s0), channel_id=1, source_target_pairs={{0,24},{4,28},{8,16},{12,20},{16,8},{20,12},{24,0},{28,4},{1,25},{... | collective-permute-start | bytes 294920 | tf_op jit(solution)/shard_map/ppermute | solution.py:41
  88.5 4.8 %collective-permute-start.31 = (f32[96,256]{1,0:T(8,128)S(1)}, f32[96,256]{1,0:T(8,128)S(1)}, u32[]{:S(2)}, u32[]{:S(2)}) collective-permute-start(f32[96,256]{1,0:T(8,128)S(1)} %shard_map.89.s0), channel_id=1, source_target_pairs={{0,16},{4,20},{8,24},{12,28},{16,0},{20,4},{24,8},{28,12},{1,17},{... | collective-permute-start | bytes 294920 | tf_op jit(solution)/shard_map/ppermute | solution.py:41
  89.0 4.6 %collective-permute-start.30 = (f32[96,256]{1,0:T(8,128)S(1)}, f32[96,256]{1,0:T(8,128)S(1)}, u32[]{:S(2)}, u32[]{:S(2)}) collective-permute-start(f32[96,256]{1,0:T(8,128)S(1)} %shard_map.89.s0), channel_id=1, source_target_pairs={{0,8},{4,12},{8,0},{12,4},{16,24},{20,28},{24,16},{28,20},{1,9},{5... | collective-permute-start | bytes 294920 | tf_op jit(solution)/shard_map/ppermute | solution.py:41
  93.7 16.7 %collective-permute-start.33 = (f32[384,256]{1,0:T(8,128)S(1)}, f32[384,256]{1,0:T(8,128)S(1)}, u32[]{:S(2)}, u32[]{:S(2)}) collective-permute-start(f32[384,256]{1,0:T(8,128)S(1)} %shard_map.90.near), channel_id=1, source_target_pairs={{0,4},{4,0},{8,12},{12,8},{16,20},{20,16},{24,28},{28,24},{1,5},{5... | collective-permute-start | bytes 1179656 | tf_op jit(solution)/shard_map/ppermute | solution.py:41
  93.8 16.6 %collective-permute-start.24 = (f32[384,256]{1,0:T(8,128)S(1)}, f32[384,256]{1,0:T(8,128)S(1)}, u32[]{:S(2)}, u32[]{:S(2)}) collective-permute-start(f32[384,256]{1,0:T(8,128)S(1)} %shard_map.84.far), channel_id=1, source_target_pairs={{0,4},{4,0},{8,12},{12,8},{16,20},{20,16},{24,28},{28,24},{1,5},{5... | collective-permute-start | bytes 1179656 | tf_op jit(solution)/shard_map/ppermute | solution.py:41
  94.4 6.2 %collective-permute-start.7 = (f32[64,512]{1,0:T(8,128)S(1)}, f32[64,512]{1,0:T(8,128)S(1)}, u32[]{:S(2)}, u32[]{:S(2)}) collective-permute-start(f32[64,512]{1,0:T(8,128)S(1)} %get-tuple-element.59), channel_id=1, source_target_pairs={{0,8},{4,12},{8,0},{12,4},{16,24},{20,28},{24,16},{28,20},{1,9},{5... | collective-permute-start | bytes 393224 | tf_op jit(solution)/shard_map/ppermute | solution.py:41
  95.6 6.4 %collective-permute-start.8 = (f32[64,512]{1,0:T(8,128)S(1)}, f32[64,512]{1,0:T(8,128)S(1)}, u32[]{:S(2)}, u32[]{:S(2)}) collective-permute-start(f32[64,512]{1,0:T(8,128)S(1)} %get-tuple-element.60), channel_id=1, source_target_pairs={{0,16},{4,20},{8,24},{12,28},{16,0},{20,4},{24,8},{28,12},{1,17},{... | collective-permute-start | bytes 393224 | tf_op jit(solution)/shard_map/ppermute | solution.py:41
  96.4 8.1 %collective-permute-start.9 = (f32[64,512]{1,0:T(8,128)S(1)}, f32[64,512]{1,0:T(8,128)S(1)}, u32[]{:S(2)}, u32[]{:S(2)}) collective-permute-start(f32[64,512]{1,0:T(8,128)S(1)} %get-tuple-element.61), channel_id=1, source_target_pairs={{0,24},{4,28},{8,16},{12,20},{16,8},{20,12},{24,0},{28,4},{1,25},{... | collective-permute-start | bytes 393224 | tf_op jit(solution)/shard_map/ppermute | solution.py:41
  100.5 5.2 %collective-permute-start.14 = (f32[64,512]{1,0:T(8,128)S(1)}, f32[64,512]{1,0:T(8,128)S(1)}, u32[]{:S(2)}, u32[]{:S(2)}) collective-permute-start(f32[64,512]{1,0:T(8,128)S(1)} %get-tuple-element.78), channel_id=1, source_target_pairs={{0,8},{4,12},{8,0},{12,4},{16,24},{20,28},{24,16},{28,20},{1,9},{5... | collective-permute-start | bytes 393224 | tf_op jit(solution)/shard_map/ppermute | solution.py:41
  102.0 6.8 %collective-permute-start.15 = (f32[64,512]{1,0:T(8,128)S(1)}, f32[64,512]{1,0:T(8,128)S(1)}, u32[]{:S(2)}, u32[]{:S(2)}) collective-permute-start(f32[64,512]{1,0:T(8,128)S(1)} %get-tuple-element.79), channel_id=1, source_target_pairs={{0,16},{4,20},{8,24},{12,28},{16,0},{20,4},{24,8},{28,12},{1,17},{... | collective-permute-start | bytes 393224 | tf_op jit(solution)/shard_map/ppermute | solution.py:41
  104.5 5.9 %collective-permute-start.16 = (f32[64,512]{1,0:T(8,128)S(1)}, f32[64,512]{1,0:T(8,128)S(1)}, u32[]{:S(2)}, u32[]{:S(2)}) collective-permute-start(f32[64,512]{1,0:T(8,128)S(1)} %get-tuple-element.80), channel_id=1, source_target_pairs={{0,24},{4,28},{8,16},{12,20},{16,8},{20,12},{24,0},{28,4},{1,25},{... | collective-permute-start | bytes 393224 | tf_op jit(solution)/shard_map/ppermute | solution.py:41

commit v3 on v2

--- a/solution.py
+++ b/solution.py
@@ -197,22 +197,27 @@
     far_term((hid_h, hid_l), half_columns((g_h, g_l), 1 - core), store)
 
 
-def halve(total, bit, keep, send):
-    count, half, _ = keep.shape
-    for z in range(count):
-        keep[z] = total[pl.ds(pl.multiple_of((2 * z + bit) * half, 32), half)]
-        send[z] = total[pl.ds(pl.multiple_of((2 * z + 1 - bit) * half, 32), half)]
-
-
-def far_own_body(hid_h, hid_l, g_h, g_l, got, keep, send, total):
-    core, chip, _ = bits()
+def halve(total, outs):
+    core, chip, lo = bits()
+    bit = turns(core, chip)[0]
+    for pair, masks in ((outs[:2], (3, 2)), (outs[2:], (1, 0))):
+        keep, send = pair
+        half = keep.shape[1]
+        for k, mask in enumerate(masks):
+            start = (lo ^ mask) * 2 * half
+            keep[k] = total[pl.ds(pl.multiple_of(start + bit * half, 32), half)]
+            send[k] = total[pl.ds(pl.multiple_of(start + (1 - bit) * half, 32), half)]
+
+
+def far_own_body(hid_h, hid_l, g_h, g_l, got, keep_a, send_a, keep_b, send_b, total):
+    core, _, _ = bits()
     width = hid_h.shape[1]
 
     def store(tap, value):
         total[tap * width : (tap + 1) * width] = value + got[tap * width : (tap + 1) * width]
 
     far_term((hid_h, hid_l), half_columns((g_h, g_l), core), store)
-    halve(total, turns(core, chip)[0], keep, send)
+    halve(total, (keep_a, send_a, keep_b, send_b))
 
 
 def backward_body(cot, g_h, g_l, far_h, far_l, slope, grad, gn, gn_h, gn_l):
@@ -237,8 +242,8 @@
     near_term(core, (own_h, own_l), (oth_h, oth_l), half_columns((gn_h, gn_l), core), store)
 
 
-def near_both_body(term, own_h, own_l, oth_h, oth_l, other, keep, send, total):
-    core, chip, _ = bits()
+def near_both_body(term, own_h, own_l, oth_h, oth_l, other, keep_a, send_a, keep_b, send_b, total):
+    core, _, _ = bits()
     width = own_h.shape[1]
     half = width // 2
 
@@ -247,7 +252,7 @@
 
     grad = split(jnp.where(core == 0, other[:, :half], other[:, half:]))
     near_term(1 - core, (oth_h, oth_l), (own_h, own_l), grad, store)
-    halve(total, turns(core, chip)[0], keep, send)
+    halve(total, (keep_a, send_a, keep_b, send_b))
 
 
 def track_body(grad, gn_h, gn_l, other, near_h, near_l, t0, t1, t2, t3, oth_h, oth_l, field):
@@ -280,10 +285,9 @@
     send[...] = kept[:, theirs] + got[:, theirs]
 
 
-def pick_body(kept, got, p0, p1, p2, p3):
-    lo = bits()[2]
-    for mask, out in enumerate((p0, p1, p2, p3)):
-        out[...] = kept[lo ^ mask] + got[lo ^ mask]
+def pair_body(kept, got, p0, p1):
+    p0[...] = kept[0] + got[0]
+    p1[...] = kept[1] + got[1]
 
 
 def total_body(scale, p0, p1, p2, p3, out):
@@ -396,20 +400,22 @@
         *cot, slope_far, *hid,
     )
     far_got = swap(far_other, "hi", 1)
-    halves = [((n_lo, part // 2, half), F32)] * 2
-    far_keep, far_send = call(far_own_body, halves, *hid, g_h, g_l, far_got, scratch=[((tall, half), F32)], room=12)
-    far_got = plane_swap(far_send, 0)
+    halves = [((2, part // 2, half), F32)] * 4
+    far_q = call(far_own_body, halves, *hid, g_h, g_l, far_got, scratch=[((tall, half), F32)], room=12)
+    far_a = far_q[0], plane_swap(far_q[1], 0)
+    far_b = far_q[2], plane_swap(far_q[3], 0)
     grad, gn, gn_h, gn_l = call(
         backward_body, [(full, F32), (full, F32), (full, BF16), (full, BF16)],
         cot, g_h, g_l, *far_w, slope_near,
     )
     gn_got = swap(gn, "hi", 1)
     (near_term,) = call(near_mine_body, [((tall, half), F32)], *own_pair, *oth_pair, gn_h, gn_l)
-    near_keep, near_send = call(
+    near_q = call(
         near_both_body, halves, near_term, *own_pair, *oth_pair, gn_got,
         scratch=[((tall, half), F32)], room=12,
     )
-    near_got = plane_swap(near_send, 0)
+    near_a = near_q[0], plane_swap(near_q[1], 0)
+    near_b = near_q[2], plane_swap(near_q[3], 0)
     grads = call(
         track_body, [(piece, F32)] * 4, grad, gn_h, gn_l, gn_got, *near_w,
         scratch=[(padded, BF16), (padded, BF16), (full, F32)], room=12,
@@ -419,21 +425,26 @@
     def scaled_total(*refs):
         total_body(scale, *refs)
 
-    def lo_sum(kept, got):
-        one = [(kept.shape[1:], F32)]
-        parts = call(pick_body, one * 4, kept, got)
-        parts = [parts[0]] + [swap(parts[mask], "lo", mask) for mask in (1, 2, 3)]
-        return call(scaled_total, one, *parts)[0]
-
-    far_mine = lo_sum(far_keep, far_got)
+    def lo_sum(pair_a, pair_b):
+        one = [(pair_a[0].shape[1:], F32)]
+        last, third = call(pair_body, one * 2, *pair_a)
+        second, mine = call(pair_body, one * 2, *pair_b)
+        parts = [swap(part, "lo", mask) for mask, part in ((1, second), (2, third), (3, last))]
+        return call(scaled_total, one, mine, *parts)[0]
+
+    far_mine = lo_sum(far_a, far_b)
     wide_half = [((part // 2, half), F32)]
     (far_mine,) = call(cross_body, wide_half, far_mine, plane_swap(far_mine, 1))
     rows_all = [((part, half), F32)]
     (rows_far,) = call(far_rows_body, rows_all, far_mine, plane_swap(far_mine, 0))
     far_cols = swap(rows_far, "hi", 1)
-    quarters = [((n_lo, part // 4, half), F32)] * 2
-    near_keep, near_send = call(plane_body, quarters, near_keep, near_got)
-    near_mine = lo_sum(near_keep, plane_swap(near_send, 1))
+    quarters = [((2, part // 4, half), F32)] * 2
+
+    def second_turn(pair):
+        kept, send = call(plane_body, quarters, *pair)
+        return kept, plane_swap(send, 1)
+
+    near_mine = lo_sum(second_turn(near_a), second_turn(near_b))
     near_all = over_chips([near_mine] * 4)
     (rows_near,) = call(near_rows_body, rows_all, *near_all)
     near_cols = swap(rows_near, "hi", 1)

time: 112 us -> 99.9 us (0.89)
  waiting for transfers between devices: 57.1 us -> 39.2 us
  starting transfers between devices: 37.7 us -> 43.6 us
    ppermute x5 -> x8, waiting for transfers between devices: 19.8 us -> 9.37 us  [plane_swap(): lax.ppermute(value, 'hi', [(i, i ^ 2 << (i + turn) % 2) for i in range(co...]
    ppermute x29, waiting for transfers between devices: 37.3 us -> 29.8 us  [swap(): return lax.ppermute(value, axis, [(i, i ^ mask) for i in range(count)])]
    ppermute x5 -> x8, starting transfers between devices: 5.92 us -> 9.53 us  [plane_swap(): lax.ppermute(value, 'hi', [(i, i ^ 2 << (i + turn) % 2) for i in range(co...]
    ppermute x29, starting transfers between devices: 31.8 us -> 34.1 us  [swap(): return lax.ppermute(value, axis, [(i, i ^ mask) for i in range(count)])]
    pallas_call x15 -> x18, Pallas kernels: 10.4 us -> 10.1 us  [call(): pl.pallas_call(body, out_shape=[make(shape, dtype) for shape, dtype in ou...]
  transfers between devices with their start and end apart: 34 -> 37, of which waited for: 15 -> 14; matrix products, arithmetic and copies ran while one was open for 0% -> 0% of each run, Pallas kernels for 11% -> 12%
where the time goes in v3:
time: 99.9 us; the launch traced here: 99.7 us
  starting transfers between devices  43.6 us (44%)
  waiting for transfers between devices  39.2 us (39%)
  Pallas kernels  14.9 us (15%)
  local copies, waits for them, and re-layouts  1.14 us (1%)
    ppermute x29, starting transfers between devices, swap(): return lax.ppermute(value, axis, [(i, i ^ mask) for i in range(count)])  34.1 us
    ppermute x29, waiting for transfers between devices, swap(): return lax.ppermute(value, axis, [(i, i ^ mask) for i in range(count)])  29.8 us
    pallas_call x18, Pallas kernels, call(): pl.pallas_call(body, out_shape=[make(shape, dtype) for shape, dtype in ou...  10.1 us
    ppermute x8, starting transfers between devices, plane_swap(): lax.ppermute(value, 'hi', [(i, i ^ 2 << (i + turn) % 2) for i in range(co...  9.53 us
    ppermute x8, waiting for transfers between devices, plane_swap(): lax.ppermute(value, 'hi', [(i, i ^ 2 << (i + turn) % 2) for i in range(co...  9.37 us
    pallas_call x2, Pallas kernels, hbm_call(): pl.pallas_call(body, out_shape=[out_place(shape, dtype) for shape, dtype...  4.79 us
  transfers between devices with their start and end apart: 37, of which 14 were waited for; matrix products, arithmetic and copies ran while one was open for 0% of the time, Pallas kernels for 12%

profile of v3, /device:TPU:0, one launch (start us, length us, event | category | flops | bytes accessed | tf_op | source)
XLA Modules:
  0.0 99.7 jit_solution(3801788852162580568)
XLA Ops:
  0.7 1.1 %constant_dynamic-slice_fusion = (f32[64,512]{1,0:T(8,128)S(1)}, f32[64,512]{1,0:T(8,128)S(1)}, f32[64,512]{1,0:T(8,128)S(1)}, f32[64,512]{1,0:T(8,128)S(1)}) fusion(f32[256,512]{1,0:T(8,128)} %param.4, s32[]{:T(128)S(6)} %select_n.15, s32[]{:T(128)S(6)} %select_n.13, s32[]{:T(128)S(6)} %select_n.12, s32[]{:T(128)S(6)} %select_n.14), kind=kLoop, calls=%fused_computation | loop fusion | bytes 1048592 | tf_op jit(solution)/shard_map/dynamic_slice | solution.py:356
  1.8 4.0 %collective-permute-start.2 = (f32[64,512]{1,0:T(8,128)S(1)}, f32[64,512]{1,0:T(8,128)S(1)}, u32[]{:S(2)}, u32[]{:S(2)}) collective-permute-start(f32[64,512]{1,0:T(8,128)S(1)} %get-tuple-element.116), channel_id=1, source_target_pairs={{0,24},{4,28},{8,16},{12,20},{16,8},{20,12},{24,0},{28,4},{1,25},{... | collective-permute-start | bytes 393224 | tf_op jit(solution)/shard_map/ppermute | solution.py:41
  5.8 0.5 collective-permute-start
  6.3 0.1 collective-permute-start.1
  6.4 0.0 collective-permute-start.3
  6.4 3.7 %collective-permute-done.2.p3 = f32[64,512]{1,0:T(8,128)S(1)} collective-permute-done((f32[64,512]{1,0:T(8,128)S(1)}, f32[64,512]{1,0:T(8,128)S(1)}, u32[]{:S(2)}, u32[]{:S(2)}) %collective-permute-start.2) | collective-permute-done | bytes 131104 | tf_op jit(solution)/shard_map/ppermute | solution.py:41
  10.1 3.2 %shard_map.75 = (bf16[1536,512]{1,0:T(8,128)(2,1)S(1)}, bf16[1536,512]{1,0:T(8,128)(2,1)S(1)}, bf16[1536,512]{1,0:T(8,128)(2,1)S(1)}, bf16[1536,512]{1,0:T(8,128...) custom-call(f32[1536,512]{1,0:T(8,128)} %near.1, ...), custom_call_target="tpu_custom_call" | custom-call | tf_op jit(solution)/shard_map/pallas_call | solution.py:116
  13.3 0.0 collective-permute-done.p1
  13.3 0.6 collective-permute-start.4
  13.9 0.1 collective-permute-start.5
  14.0 2.0 %collective-permute-start.10 = (f32[64,512]{1,0:T(8,128)S(1)}, f32[64,512]{1,0:T(8,128)S(1)}, u32[]{:S(2)}, u32[]{:S(2)}) collective-permute-start(f32[64,512]{1,0:T(8,128)S(1)} %get-tuple-element.69), channel_id=1, source_target_pairs={{0,8},{4,12},{8,0},{12,4},{16,24},{20,28},{24,16},{28,20},{1,9},{5... | collective-permute-start | bytes 393224 | tf_op jit(solution)/shard_map/ppermute | solution.py:41
  16.0 1.5 %collective-permute-start.11 = (f32[64,512]{1,0:T(8,128)S(1)}, f32[64,512]{1,0:T(8,128)S(1)}, u32[]{:S(2)}, u32[]{:S(2)}) collective-permute-start(f32[64,512]{1,0:T(8,128)S(1)} %get-tuple-element.70), channel_id=1, source_target_pairs={{0,16},{4,20},{8,24},{12,28},{16,0},{20,4},{24,8},{28,12},{1,17},{... | collective-permute-start | bytes 393224 | tf_op jit(solution)/shard_map/ppermute | solution.py:41
  17.5 0.0 collective-permute-start.12
  17.5 3.1 %shard_map.76 = (f32[64,512]{1,0:T(8,128)S(1)}, f32[64,512]{1,0:T(8,128)S(1)}, f32[64,512]{1,0:T(8,128)S(1)}, f32[64,512]{1,0:T(8,128)S(1)}, f32[256,512]{1,0:T(...) custom-call(f32[64,512]{1,0:T(8,128)S(1)} %get-tuple-element.118.p0,, ...), custom_call_target="tpu_custom_call" | custom-call | tf_op jit(solution)/shard_map/pallas_call | solution.py:29
  20.7 3.7 %collective-permute-done.11.c2 = f32[64,512]{1,0:T(8,128)S(1)} collective-permute-done((f32[64,512]{1,0:T(8,128)S(1)}, f32[64,512]{1,0:T(8,128)S(1)}, u32[]{:S(2)}, u32[]{:S(2)}) %collective-permute-start.11) | collective-permute-done | bytes 131104 | tf_op jit(solution)/shard_map/ppermute | solution.py:41
  24.3 0.9 shard_map.77
  25.2 0.1 collective-permute-start.17
  25.3 1.6 %shard_map.78 = (f32[256,512]{1,0:T(8,128)S(1)}, f32[256,512]{1,0:T(8,128)S(1)}, bf16[256,512]{1,0:T(8,128)(2,1)S(1)}, bf16[256,512]{1,0:T(8,128)(2,1)S(1)}) custom-call(f32[256,512]{1,0:T(8,128)S(1)} %get-tuple-element.75.cot, bf16[256,512]{1,0:T(8,128)(2,1)S(1)} %get-tuple-element.76.g_h, bf16[256,512]{1,0:T(8,128)(2,1)S(1)} %get-tuple-element.77.g_l, ...), custom_call_target="tpu_custom_call" | custom-call | tf_op jit(solution)/shard_map/pallas_call | solution.py:29
  26.9 0.6 collective-permute-start.13
  27.5 1.2 %collective-permute-done.17.got = f32[1536,256]{1,0:T(8,128)S(1)} collective-permute-done((f32[1536,256]{1,0:T(8,128)S(1)}, f32[1536,256]{1,0:T(8,128)S(1)}, u32[]{:S(2)}, u32[]{:S(2)}) %collective-permute-start.17) | collective-permute-done | bytes 1572896 | tf_op jit(solution)/shard_map/ppermute | solution.py:41
  28.7 0.9 shard_map.80
  29.6 1.3 %collective-permute-start.18 = (f32[2,192,256]{2,1,0:T(8,128)S(1)}, f32[2,192,256]{2,1,0:T(8,128)S(1)}, u32[]{:S(2)}, u32[]{:S(2)}) collective-permute-start(f32[2,192,256]{2,1,0:T(8,128)S(1)} %get-tuple-element.89), channel_id=1, source_target_pairs={{0,8},{4,20},{8,0},{12,28},{16,24},{20,4},{24,16},{28,12},{1,9},{5... | collective-permute-start | bytes 1179656 | tf_op jit(solution)/shard_map/ppermute | solution.py:46
  30.9 0.8 collective-permute-start.20
  31.7 0.8 shard_map.86.term
  32.6 0.0 collective-permute-done.13.other
  32.6 0.9 shard_map.87
  33.5 1.3 %collective-permute-start.26 = (f32[2,192,256]{2,1,0:T(8,128)S(1)}, f32[2,192,256]{2,1,0:T(8,128)S(1)}, u32[]{:S(2)}, u32[]{:S(2)}) collective-permute-start(f32[2,192,256]{2,1,0:T(8,128)S(1)} %get-tuple-element.101), channel_id=1, source_target_pairs={{0,8},{4,20},{8,0},{12,28},{16,24},{20,4},{24,16},{28,12},{1,9},{5... | collective-permute-start | bytes 1179656 | tf_op jit(solution)/shard_map/ppermute | solution.py:46
  34.8 0.8 collective-permute-start.29
  35.6 1.9 %collective-permute-done.18.got = f32[2,192,256]{2,1,0:T(8,128)S(1)} collective-permute-done((f32[2,192,256]{2,1,0:T(8,128)S(1)}, f32[2,192,256]{2,1,0:T(8,128)S(1)}, u32[]{:S(2)}, u32[]{:S(2)}) %collective-permute-start.18) | collective-permute-done | bytes 393248 | tf_op jit(solution)/shard_map/ppermute | solution.py:46
  37.5 1.6 %collective-permute-start.19 = (f32[192,256]{1,0:T(8,128)S(1)}, f32[192,256]{1,0:T(8,128)S(1)}, u32[]{:S(2)}, u32[]{:S(2)}) collective-permute-start(f32[192,256]{1,0:T(8,128)S(1)} %get-tuple-element.91), channel_id=1, source_target_pairs={{0,1},{1,0},{2,3},{3,2},{4,5},{5,4},{6,7},{7,6},{8,9},{9,8},{10,11... | collective-permute-start | bytes 589832 | tf_op jit(solution)/shard_map/ppermute | solution.py:41
  39.2 2.5 %collective-permute-done.20.got = f32[2,192,256]{2,1,0:T(8,128)S(1)} collective-permute-done((f32[2,192,256]{2,1,0:T(8,128)S(1)}, f32[2,192,256]{2,1,0:T(8,128)S(1)}, u32[]{:S(2)}, u32[]{:S(2)}) %collective-permute-start.20) | collective-permute-done | bytes 393248 | tf_op jit(solution)/shard_map/ppermute | solution.py:46
  41.7 2.7 %collective-permute-start.21 = (f32[192,256]{1,0:T(8,128)S(1)}, f32[192,256]{1,0:T(8,128)S(1)}, u32[]{:S(2)}, u32[]{:S(2)}) collective-permute-start(f32[192,256]{1,0:T(8,128)S(1)} %get-tuple-element.94), channel_id=1, source_target_pairs={{0,2},{1,3},{2,0},{3,1},{4,6},{5,7},{6,4},{7,5},{8,10},{9,11},{10,... | collective-permute-start | bytes 589832 | tf_op jit(solution)/shard_map/ppermute | solution.py:41
  44.4 1.3 %collective-permute-start.22 = (f32[192,256]{1,0:T(8,128)S(1)}, f32[192,256]{1,0:T(8,128)S(1)}, u32[]{:S(2)}, u32[]{:S(2)}) collective-permute-start(f32[192,256]{1,0:T(8,128)S(1)} %get-tuple-element.95), channel_id=1, source_target_pairs={{0,3},{1,2},{2,1},{3,0},{4,7},{5,6},{6,5},{7,4},{8,11},{9,10},{10,... | collective-permute-start | bytes 589832 | tf_op jit(solution)/shard_map/ppermute | solution.py:41
  45.8 0.2 collective-permute-done.26.got
  46.0 1.6 %collective-permute-start.27 = (f32[2,96,256]{2,1,0:T(8,128)S(1)}, f32[2,96,256]{2,1,0:T(8,128)S(1)}, u32[]{:S(2)}, u32[]{:S(2)}) collective-permute-start(f32[2,96,256]{2,1,0:T(8,128)S(1)} %get-tuple-element.103), channel_id=1, source_target_pairs={{0,16},{4,12},{8,24},{12,4},{16,0},{20,28},{24,8},{28,20},{1,17},{... | collective-permute-start | bytes 589832 | tf_op jit(solution)/shard_map/ppermute | solution.py:46
  47.5 4.8 %collective-permute-done.29.got = f32[2,192,256]{2,1,0:T(8,128)S(1)} collective-permute-done((f32[2,192,256]{2,1,0:T(8,128)S(1)}, f32[2,192,256]{2,1,0:T(8,128)S(1)}, u32[]{:S(2)}, u32[]{:S(2)}) %collective-permute-start.29) | collective-permute-done | bytes 393248 | tf_op jit(solution)/shard_map/ppermute | solution.py:46
  52.4 1.6 %collective-permute-start.30 = (f32[2,96,256]{2,1,0:T(8,128)S(1)}, f32[2,96,256]{2,1,0:T(8,128)S(1)}, u32[]{:S(2)}, u32[]{:S(2)}) collective-permute-start(f32[2,96,256]{2,1,0:T(8,128)S(1)} %get-tuple-element.109), channel_id=1, source_target_pairs={{0,16},{4,12},{8,24},{12,4},{16,0},{20,28},{24,8},{28,20},{1,17},{... | collective-permute-start | bytes 589832 | tf_op jit(solution)/shard_map/ppermute | solution.py:46
  54.0 4.5 %collective-permute-done.21.refs_2_ = f32[192,256]{1,0:T(8,128)S(1)} collective-permute-done((f32[192,256]{1,0:T(8,128)S(1)}, f32[192,256]{1,0:T(8,128)S(1)}, u32[]{:S(2)}, u32[]{:S(2)}) %collective-permute-start.21) | collective-permute-done | bytes 196640 | tf_op jit(solution)/shard_map/ppermute | solution.py:41
  58.5 1.6 %collective-permute-start.23 = (f32[192,256]{1,0:T(8,128)S(1)}, f32[192,256]{1,0:T(8,128)S(1)}, u32[]{:S(2)}, u32[]{:S(2)}) collective-permute-start(f32[192,256]{1,0:T(8,128)S(1)} %shard_map.83.own), channel_id=1, source_target_pairs={{0,16},{4,12},{8,24},{12,4},{16,0},{20,28},{24,8},{28,20},{1,17},{... | collective-permute-start | bytes 589832 | tf_op jit(solution)/shard_map/ppermute | solution.py:46
  60.1 0.0 collective-permute-done.27.got
  60.1 3.7 %collective-permute-start.28 = (f32[96,256]{1,0:T(8,128)S(1)}, f32[96,256]{1,0:T(8,128)S(1)}, u32[]{:S(2)}, u32[]{:S(2)}) collective-permute-start(f32[96,256]{1,0:T(8,128)S(1)} %get-tuple-element.105), channel_id=1, source_target_pairs={{0,1},{1,0},{2,3},{3,2},{4,5},{5,4},{6,7},{7,6},{8,9},{9,8},{10,11... | collective-permute-start | bytes 294920 | tf_op jit(solution)/shard_map/ppermute | solution.py:41
  63.8 0.0 collective-permute-done.30.got
  63.9 2.0 %collective-permute-start.31 = (f32[96,256]{1,0:T(8,128)S(1)}, f32[96,256]{1,0:T(8,128)S(1)}, u32[]{:S(2)}, u32[]{:S(2)}) collective-permute-start(f32[96,256]{1,0:T(8,128)S(1)} %get-tuple-element.110), channel_id=1, source_target_pairs={{0,2},{1,3},{2,0},{3,1},{4,6},{5,7},{6,4},{7,5},{8,10},{9,11},{10,... | collective-permute-start | bytes 294920 | tf_op jit(solution)/shard_map/ppermute | solution.py:41
  65.9 1.5 %collective-permute-start.32 = (f32[96,256]{1,0:T(8,128)S(1)}, f32[96,256]{1,0:T(8,128)S(1)}, u32[]{:S(2)}, u32[]{:S(2)}) collective-permute-start(f32[96,256]{1,0:T(8,128)S(1)} %get-tuple-element.111), channel_id=1, source_target_pairs={{0,3},{1,2},{2,1},{3,0},{4,7},{5,6},{6,5},{7,4},{8,11},{9,10},{10,... | collective-permute-start | bytes 294920 | tf_op jit(solution)/shard_map/ppermute | solution.py:41
  67.4 0.0 collective-permute-done.23.got
  67.4 0.6 collective-permute-start.24
  68.0 6.5 %collective-permute-done.31.refs_2_ = f32[96,256]{1,0:T(8,128)S(1)} collective-permute-done((f32[96,256]{1,0:T(8,128)S(1)}, f32[96,256]{1,0:T(8,128)S(1)}, u32[]{:S(2)}, u32[]{:S(2)}) %collective-permute-start.31) | collective-permute-done | bytes 98336 | tf_op jit(solution)/shard_map/ppermute | solution.py:41
  74.6 0.9 collective-permute-start.35
  75.5 1.0 %collective-permute-start.34 = (f32[96,256]{1,0:T(8,128)S(1)}, f32[96,256]{1,0:T(8,128)S(1)}, u32[]{:S(2)}, u32[]{:S(2)}) collective-permute-start(f32[96,256]{1,0:T(8,128)S(1)} %shard_map.92.s0), channel_id=1, source_target_pairs={{0,16},{4,20},{8,24},{12,28},{16,0},{20,4},{24,8},{28,12},{1,17},{... | collective-permute-start | bytes 294920 | tf_op jit(solution)/shard_map/ppermute | solution.py:41
  76.5 1.6 %collective-permute-start.33 = (f32[96,256]{1,0:T(8,128)S(1)}, f32[96,256]{1,0:T(8,128)S(1)}, u32[]{:S(2)}, u32[]{:S(2)}) collective-permute-start(f32[96,256]{1,0:T(8,128)S(1)} %shard_map.92.s0), channel_id=1, source_target_pairs={{0,8},{4,12},{8,0},{12,4},{16,24},{20,28},{24,16},{28,20},{1,9},{5... | collective-permute-start | bytes 294920 | tf_op jit(solution)/shard_map/ppermute | solution.py:41
  78.1 2.2 %collective-permute-done.35.s3 = f32[96,256]{1,0:T(8,128)S(1)} collective-permute-done((f32[96,256]{1,0:T(8,128)S(1)}, f32[96,256]{1,0:T(8,128)S(1)}, u32[]{:S(2)}, u32[]{:S(2)}) %collective-permute-start.35) | collective-permute-done | bytes 98336 | tf_op jit(solution)/shard_map/ppermute | solution.py:41
  80.3 0.8 collective-permute-done.34.s2
  81.2 0.1 collective-permute-start.36
  81.4 0.5 collective-permute-start.25
  81.9 1.6 %collective-permute-start.7 = (f32[64,512]{1,0:T(8,128)S(1)}, f32[64,512]{1,0:T(8,128)S(1)}, u32[]{:S(2)}, u32[]{:S(2)}) collective-permute-start(f32[64,512]{1,0:T(8,128)S(1)} %get-tuple-element.65), channel_id=1, source_target_pairs={{0,8},{4,12},{8,0},{12,4},{16,24},{20,28},{24,16},{28,20},{1,9},{5... | collective-permute-start | bytes 393224 | tf_op jit(solution)/shard_map/ppermute | solution.py:41
  83.5 0.3 collective-permute-start.8
  83.8 1.6 %collective-permute-start.9 = (f32[64,512]{1,0:T(8,128)S(1)}, f32[64,512]{1,0:T(8,128)S(1)}, u32[]{:S(2)}, u32[]{:S(2)}) collective-permute-start(f32[64,512]{1,0:T(8,128)S(1)} %get-tuple-element.67), channel_id=1, source_target_pairs={{0,24},{4,28},{8,16},{12,20},{16,8},{20,12},{24,0},{28,4},{1,25},{... | collective-permute-start | bytes 393224 | tf_op jit(solution)/shard_map/ppermute | solution.py:41
  85.4 1.4 %shard_map.79 = (f32[64,512]{1,0:T(8,128)S(1)}, f32[64,512]{1,0:T(8,128)S(1)}, f32[64,512]{1,0:T(8,128)S(1)}, f32[64,512]{1,0:T(8,128)S(1)}) custom-call(f32[256,512]{1,0:T(8,128)S(1)} %get-tuple-element.79.grad, bf16[256,512]{1,0:T(8,128)(2,1)S(1)} %get-tuple-element.80.gn_h, bf16[256,512]{1,0:T(8,128)(2,1)S(1)} %get-tuple-element.81.gn_l, ...), custom_call_target="tpu_custom_call" | custom-call | tf_op jit(solution)/shard_map/pallas_call | solution.py:29
  86.9 0.8 collective-permute-done.7.f1
  87.7 2.2 %collective-permute-start.14 = (f32[64,512]{1,0:T(8,128)S(1)}, f32[64,512]{1,0:T(8,128)S(1)}, u32[]{:S(2)}, u32[]{:S(2)}) collective-permute-start(f32[64,512]{1,0:T(8,128)S(1)} %get-tuple-element.84), channel_id=1, source_target_pairs={{0,8},{4,12},{8,0},{12,4},{16,24},{20,28},{24,16},{28,20},{1,9},{5... | collective-permute-start | bytes 393224 | tf_op jit(solution)/shard_map/ppermute | solution.py:41
  89.9 1.9 %collective-permute-done.8.f2 = f32[64,512]{1,0:T(8,128)S(1)} collective-permute-done((f32[64,512]{1,0:T(8,128)S(1)}, f32[64,512]{1,0:T(8,128)S(1)}, u32[]{:S(2)}, u32[]{:S(2)}) %collective-permute-start.8) | collective-permute-done | bytes 131104 | tf_op jit(solution)/shard_map/ppermute | solution.py:41
  91.7 1.9 %collective-permute-start.16 = (f32[64,512]{1,0:T(8,128)S(1)}, f32[64,512]{1,0:T(8,128)S(1)}, u32[]{:S(2)}, u32[]{:S(2)}) collective-permute-start(f32[64,512]{1,0:T(8,128)S(1)} %get-tuple-element.86), channel_id=1, source_target_pairs={{0,24},{4,28},{8,16},{12,20},{16,8},{20,12},{24,0},{28,4},{1,25},{... | collective-permute-start | bytes 393224 | tf_op jit(solution)/shard_map/ppermute | solution.py:41
  93.7 4.4 %collective-permute-done.15.g2 = f32[64,512]{1,0:T(8,128)S(1)} collective-permute-done((f32[64,512]{1,0:T(8,128)S(1)}, f32[64,512]{1,0:T(8,128)S(1)}, u32[]{:S(2)}, u32[]{:S(2)}) %collective-permute-start.15) | collective-permute-done | bytes 131104 | tf_op jit(solution)/shard_map/ppermute | solution.py:41
  98.1 1.6 %shard_map.94 = (f32[256,512]{1,0:T(8,128)}, f32[256,512]{1,0:T(8,128)}, f32[384,512]{1,0:T(8,128)}, f32[384,512]{1,0:T(8,128)}) custom-call(f32[64,512]{1,0:T(8,128)S(1)} %get-tuple-element.64.f0, f32[64,512]{1,0:T(8,128)S(1)} %collective-permute-done.7.f1, f32[64,512]{1,0:T(8,128)S(1)} %collective-permute-done.8.f2, ...), custom_call_target="tpu_custom_call" | custom-call | tf_op jit(solution)/shard_map/pallas_call | solution.py:116
  (31 shorter events, 0.4 us)
Async XLA Ops:
  1.8 8.3 %collective-permute-start.2 = (f32[64,512]{1,0:T(8,128)S(1)}, f32[64,512]{1,0:T(8,128)S(1)}, u32[]{:S(2)}, u32[]{:S(2)}) collective-permute-start(f32[64,512]{1,0:T(8,128)S(1)} %get-tuple-element.116), channel_id=1, source_target_pairs={{0,24},{4,28},{8,16},{12,20},{16,8},{20,12},{24,0},{28,4},{1,25},{... | collective-permute-start | bytes 393224 | tf_op jit(solution)/shard_map/ppermute | solution.py:41
  5.8 7.6 %collective-permute-start = (f32[64,512]{1,0:T(8,128)S(1)}, f32[64,512]{1,0:T(8,128)S(1)}, u32[]{:S(2)}, u32[]{:S(2)}) collective-permute-start(f32[64,512]{1,0:T(8,128)S(1)} %get-tuple-element.117), channel_id=1, source_target_pairs={{0,8},{4,12},{8,0},{12,4},{16,24},{20,28},{24,16},{28,20},{1,9},{5... | collective-permute-start | bytes 393224 | tf_op jit(solution)/shard_map/ppermute | solution.py:41
  6.3 7.6 %collective-permute-start.1 = (f32[64,512]{1,0:T(8,128)S(1)}, f32[64,512]{1,0:T(8,128)S(1)}, u32[]{:S(2)}, u32[]{:S(2)}) collective-permute-start(f32[64,512]{1,0:T(8,128)S(1)} %get-tuple-element.119), channel_id=1, source_target_pairs={{0,16},{4,20},{8,24},{12,28},{16,0},{20,4},{24,8},{28,12},{1,17},{... | collective-permute-start | bytes 393224 | tf_op jit(solution)/shard_map/ppermute | solution.py:41
  6.4 9.5 %collective-permute-start.3 = (f32[64,512]{1,0:T(8,128)S(1)}, f32[64,512]{1,0:T(8,128)S(1)}, u32[]{:S(2)}, u32[]{:S(2)}) collective-permute-start(f32[64,512]{1,0:T(8,128)S(1)} %get-tuple-element.118.p0), channel_id=1, source_target_pairs={{0,4},{4,0},{8,12},{12,8},{16,20},{20,16},{24,28},{28,24},{1,5},{5... | collective-permute-start | bytes 393224 | tf_op jit(solution)/shard_map/ppermute | solution.py:41
  10.1 7.4 %collective-permute-start.6 = (f32[64,512]{1,0:T(8,128)S(1)}, f32[64,512]{1,0:T(8,128)S(1)}, u32[]{:S(2)}, u32[]{:S(2)}) collective-permute-start(f32[64,512]{1,0:T(8,128)S(1)} %collective-permute-done.2.p3), channel_id=1, source_target_pairs={{0,4},{4,0},{8,12},{12,8},{16,20},{20,16},{24,28},{28,24},{1,5},{5... | collective-permute-start | bytes 393224 | tf_op jit(solution)/shard_map/ppermute | solution.py:41
  13.3 4.2 %collective-permute-start.4 = (f32[64,512]{1,0:T(8,128)S(1)}, f32[64,512]{1,0:T(8,128)S(1)}, u32[]{:S(2)}, u32[]{:S(2)}) collective-permute-start(f32[64,512]{1,0:T(8,128)S(1)} %collective-permute-done.p1), channel_id=1, source_target_pairs={{0,4},{4,0},{8,12},{12,8},{16,20},{20,16},{24,28},{28,24},{1,5},{5... | collective-permute-start | bytes 393224 | tf_op jit(solution)/shard_map/ppermute | solution.py:41
  13.9 3.6 %collective-permute-start.5 = (f32[64,512]{1,0:T(8,128)S(1)}, f32[64,512]{1,0:T(8,128)S(1)}, u32[]{:S(2)}, u32[]{:S(2)}) collective-permute-start(f32[64,512]{1,0:T(8,128)S(1)} %collective-permute-done.1.p2), channel_id=1, source_target_pairs={{0,4},{4,0},{8,12},{12,8},{16,20},{20,16},{24,28},{28,24},{1,5},{5... | collective-permute-start | bytes 393224 | tf_op jit(solution)/shard_map/ppermute | solution.py:41
  14.0 6.6 %collective-permute-start.10 = (f32[64,512]{1,0:T(8,128)S(1)}, f32[64,512]{1,0:T(8,128)S(1)}, u32[]{:S(2)}, u32[]{:S(2)}) collective-permute-start(f32[64,512]{1,0:T(8,128)S(1)} %get-tuple-element.69), channel_id=1, source_target_pairs={{0,8},{4,12},{8,0},{12,4},{16,24},{20,28},{24,16},{28,20},{1,9},{5... | collective-permute-start | bytes 393224 | tf_op jit(solution)/shard_map/ppermute | solution.py:41
  16.0 8.4 %collective-permute-start.11 = (f32[64,512]{1,0:T(8,128)S(1)}, f32[64,512]{1,0:T(8,128)S(1)}, u32[]{:S(2)}, u32[]{:S(2)}) collective-permute-start(f32[64,512]{1,0:T(8,128)S(1)} %get-tuple-element.70), channel_id=1, source_target_pairs={{0,16},{4,20},{8,24},{12,28},{16,0},{20,4},{24,8},{28,12},{1,17},{... | collective-permute-start | bytes 393224 | tf_op jit(solution)/shard_map/ppermute | solution.py:41
  17.5 6.8 %collective-permute-start.12 = (f32[64,512]{1,0:T(8,128)S(1)}, f32[64,512]{1,0:T(8,128)S(1)}, u32[]{:S(2)}, u32[]{:S(2)}) collective-permute-start(f32[64,512]{1,0:T(8,128)S(1)} %get-tuple-element.71), channel_id=1, source_target_pairs={{0,24},{4,28},{8,16},{12,20},{16,8},{20,12},{24,0},{28,4},{1,25},{... | collective-permute-start | bytes 393224 | tf_op jit(solution)/shard_map/ppermute | solution.py:41
  25.2 3.5 %collective-permute-start.17 = (f32[1536,256]{1,0:T(8,128)S(1)}, f32[1536,256]{1,0:T(8,128)S(1)}, u32[]{:S(2)}, u32[]{:S(2)}) collective-permute-start(f32[1536,256]{1,0:T(8,128)S(1)} %get-tuple-element.87), channel_id=1, source_target_pairs={{0,4},{4,0},{8,12},{12,8},{16,20},{20,16},{24,28},{28,24},{1,5},{5... | collective-permute-start | bytes 4718600 | tf_op jit(solution)/shard_map/ppermute | solution.py:41
  26.9 5.7 %collective-permute-start.13 = (f32[256,512]{1,0:T(8,128)S(1)}, f32[256,512]{1,0:T(8,128)S(1)}, u32[]{:S(2)}, u32[]{:S(2)}) collective-permute-start(f32[256,512]{1,0:T(8,128)S(1)} %get-tuple-element.82), channel_id=1, source_target_pairs={{0,4},{4,0},{8,12},{12,8},{16,20},{20,16},{24,28},{28,24},{1,5},{5... | collective-permute-start | bytes 1572872 | tf_op jit(solution)/shard_map/ppermute | solution.py:41
  29.6 7.8 %collective-permute-start.18 = (f32[2,192,256]{2,1,0:T(8,128)S(1)}, f32[2,192,256]{2,1,0:T(8,128)S(1)}, u32[]{:S(2)}, u32[]{:S(2)}) collective-permute-start(f32[2,192,256]{2,1,0:T(8,128)S(1)} %get-tuple-element.89), channel_id=1, source_target_pairs={{0,8},{4,20},{8,0},{12,28},{16,24},{20,4},{24,16},{28,12},{1,9},{5... | collective-permute-start | bytes 1179656 | tf_op jit(solution)/shard_map/ppermute | solution.py:46
  30.9 10.8 %collective-permute-start.20 = (f32[2,192,256]{2,1,0:T(8,128)S(1)}, f32[2,192,256]{2,1,0:T(8,128)S(1)}, u32[]{:S(2)}, u32[]{:S(2)}) collective-permute-start(f32[2,192,256]{2,1,0:T(8,128)S(1)} %get-tuple-element.93), channel_id=1, source_target_pairs={{0,8},{4,20},{8,0},{12,28},{16,24},{20,4},{24,16},{28,12},{1,9},{5... | collective-permute-start | bytes 1179656 | tf_op jit(solution)/shard_map/ppermute | solution.py:46
  33.5 12.4 %collective-permute-start.26 = (f32[2,192,256]{2,1,0:T(8,128)S(1)}, f32[2,192,256]{2,1,0:T(8,128)S(1)}, u32[]{:S(2)}, u32[]{:S(2)}) collective-permute-start(f32[2,192,256]{2,1,0:T(8,128)S(1)} %get-tuple-element.101), channel_id=1, source_target_pairs={{0,8},{4,20},{8,0},{12,28},{16,24},{20,4},{24,16},{28,12},{1,9},{5... | collective-permute-start | bytes 1179656 | tf_op jit(solution)/shard_map/ppermute | solution.py:46
  34.8 17.5 %collective-permute-start.29 = (f32[2,192,256]{2,1,0:T(8,128)S(1)}, f32[2,192,256]{2,1,0:T(8,128)S(1)}, u32[]{:S(2)}, u32[]{:S(2)}) collective-permute-start(f32[2,192,256]{2,1,0:T(8,128)S(1)} %get-tuple-element.107), channel_id=1, source_target_pairs={{0,8},{4,20},{8,0},{12,28},{16,24},{20,4},{24,16},{28,12},{1,9},{5... | collective-permute-start | bytes 1179656 | tf_op jit(solution)/shard_map/ppermute | solution.py:46
  37.5 16.4 %collective-permute-start.19 = (f32[192,256]{1,0:T(8,128)S(1)}, f32[192,256]{1,0:T(8,128)S(1)}, u32[]{:S(2)}, u32[]{:S(2)}) collective-permute-start(f32[192,256]{1,0:T(8,128)S(1)} %get-tuple-element.91), channel_id=1, source_target_pairs={{0,1},{1,0},{2,3},{3,2},{4,5},{5,4},{6,7},{7,6},{8,9},{9,8},{10,11... | collective-permute-start | bytes 589832 | tf_op jit(solution)/shard_map/ppermute | solution.py:41
  41.7 16.7 %collective-permute-start.21 = (f32[192,256]{1,0:T(8,128)S(1)}, f32[192,256]{1,0:T(8,128)S(1)}, u32[]{:S(2)}, u32[]{:S(2)}) collective-permute-start(f32[192,256]{1,0:T(8,128)S(1)} %get-tuple-element.94), channel_id=1, source_target_pairs={{0,2},{1,3},{2,0},{3,1},{4,6},{5,7},{6,4},{7,5},{8,10},{9,11},{10,... | collective-permute-start | bytes 589832 | tf_op jit(solution)/shard_map/ppermute | solution.py:41
  44.4 14.0 %collective-permute-start.22 = (f32[192,256]{1,0:T(8,128)S(1)}, f32[192,256]{1,0:T(8,128)S(1)}, u32[]{:S(2)}, u32[]{:S(2)}) collective-permute-start(f32[192,256]{1,0:T(8,128)S(1)} %get-tuple-element.95), channel_id=1, source_target_pairs={{0,3},{1,2},{2,1},{3,0},{4,7},{5,6},{6,5},{7,4},{8,11},{9,10},{10,... | collective-permute-start | bytes 589832 | tf_op jit(solution)/shard_map/ppermute | solution.py:41
  46.0 14.1 %collective-permute-start.27 = (f32[2,96,256]{2,1,0:T(8,128)S(1)}, f32[2,96,256]{2,1,0:T(8,128)S(1)}, u32[]{:S(2)}, u32[]{:S(2)}) collective-permute-start(f32[2,96,256]{2,1,0:T(8,128)S(1)} %get-tuple-element.103), channel_id=1, source_target_pairs={{0,16},{4,12},{8,24},{12,4},{16,0},{20,28},{24,8},{28,20},{1,17},{... | collective-permute-start | bytes 589832 | tf_op jit(solution)/shard_map/ppermute | solution.py:46
  52.4 11.4 %collective-permute-start.30 = (f32[2,96,256]{2,1,0:T(8,128)S(1)}, f32[2,96,256]{2,1,0:T(8,128)S(1)}, u32[]{:S(2)}, u32[]{:S(2)}) collective-permute-start(f32[2,96,256]{2,1,0:T(8,128)S(1)} %get-tuple-element.109), channel_id=1, source_target_pairs={{0,16},{4,12},{8,24},{12,4},{16,0},{20,28},{24,8},{28,20},{1,17},{... | collective-permute-start | bytes 589832 | tf_op jit(solution)/shard_map/ppermute | solution.py:46
  58.5 8.9 %collective-permute-start.23 = (f32[192,256]{1,0:T(8,128)S(1)}, f32[192,256]{1,0:T(8,128)S(1)}, u32[]{:S(2)}, u32[]{:S(2)}) collective-permute-start(f32[192,256]{1,0:T(8,128)S(1)} %shard_map.83.own), channel_id=1, source_target_pairs={{0,16},{4,12},{8,24},{12,4},{16,0},{20,28},{24,8},{28,20},{1,17},{... | collective-permute-start | bytes 589832 | tf_op jit(solution)/shard_map/ppermute | solution.py:46
  60.1 7.9 %collective-permute-start.28 = (f32[96,256]{1,0:T(8,128)S(1)}, f32[96,256]{1,0:T(8,128)S(1)}, u32[]{:S(2)}, u32[]{:S(2)}) collective-permute-start(f32[96,256]{1,0:T(8,128)S(1)} %get-tuple-element.105), channel_id=1, source_target_pairs={{0,1},{1,0},{2,3},{3,2},{4,5},{5,4},{6,7},{7,6},{8,9},{9,8},{10,11... | collective-permute-start | bytes 294920 | tf_op jit(solution)/shard_map/ppermute | solution.py:41
  63.9 10.7 %collective-permute-start.31 = (f32[96,256]{1,0:T(8,128)S(1)}, f32[96,256]{1,0:T(8,128)S(1)}, u32[]{:S(2)}, u32[]{:S(2)}) collective-permute-start(f32[96,256]{1,0:T(8,128)S(1)} %get-tuple-element.110), channel_id=1, source_target_pairs={{0,2},{1,3},{2,0},{3,1},{4,6},{5,7},{6,4},{7,5},{8,10},{9,11},{10,... | collective-permute-start | bytes 294920 | tf_op jit(solution)/shard_map/ppermute | solution.py:41
  65.9 8.7 %collective-permute-start.32 = (f32[96,256]{1,0:T(8,128)S(1)}, f32[96,256]{1,0:T(8,128)S(1)}, u32[]{:S(2)}, u32[]{:S(2)}) collective-permute-start(f32[96,256]{1,0:T(8,128)S(1)} %get-tuple-element.111), channel_id=1, source_target_pairs={{0,3},{1,2},{2,1},{3,0},{4,7},{5,6},{6,5},{7,4},{8,11},{9,10},{10,... | collective-permute-start | bytes 294920 | tf_op jit(solution)/shard_map/ppermute | solution.py:41
  67.4 13.9 %collective-permute-start.24 = (f32[192,256]{1,0:T(8,128)S(1)}, f32[192,256]{1,0:T(8,128)S(1)}, u32[]{:S(2)}, u32[]{:S(2)}) collective-permute-start(f32[192,256]{1,0:T(8,128)S(1)} %shard_map.84.own), channel_id=1, source_target_pairs={{0,8},{4,20},{8,0},{12,28},{16,24},{20,4},{24,16},{28,12},{1,9},{5... | collective-permute-start | bytes 589832 | tf_op jit(solution)/shard_map/ppermute | solution.py:46
  74.6 5.7 %collective-permute-start.35 = (f32[96,256]{1,0:T(8,128)S(1)}, f32[96,256]{1,0:T(8,128)S(1)}, u32[]{:S(2)}, u32[]{:S(2)}) collective-permute-start(f32[96,256]{1,0:T(8,128)S(1)} %shard_map.92.s0), channel_id=1, source_target_pairs={{0,24},{4,28},{8,16},{12,20},{16,8},{20,12},{24,0},{28,4},{1,25},{... | collective-permute-start | bytes 294920 | tf_op jit(solution)/shard_map/ppermute | solution.py:41
  75.5 5.7 %collective-permute-start.34 = (f32[96,256]{1,0:T(8,128)S(1)}, f32[96,256]{1,0:T(8,128)S(1)}, u32[]{:S(2)}, u32[]{:S(2)}) collective-permute-start(f32[96,256]{1,0:T(8,128)S(1)} %shard_map.92.s0), channel_id=1, source_target_pairs={{0,16},{4,20},{8,24},{12,28},{16,0},{20,4},{24,8},{28,12},{1,17},{... | collective-permute-start | bytes 294920 | tf_op jit(solution)/shard_map/ppermute | solution.py:41
  76.5 4.7 %collective-permute-start.33 = (f32[96,256]{1,0:T(8,128)S(1)}, f32[96,256]{1,0:T(8,128)S(1)}, u32[]{:S(2)}, u32[]{:S(2)}) collective-permute-start(f32[96,256]{1,0:T(8,128)S(1)} %shard_map.92.s0), channel_id=1, source_target_pairs={{0,8},{4,12},{8,0},{12,4},{16,24},{20,28},{24,16},{28,20},{1,9},{5... | collective-permute-start | bytes 294920 | tf_op jit(solution)/shard_map/ppermute | solution.py:41
  81.2 16.9 %collective-permute-start.36 = (f32[384,256]{1,0:T(8,128)S(1)}, f32[384,256]{1,0:T(8,128)S(1)}, u32[]{:S(2)}, u32[]{:S(2)}) collective-permute-start(f32[384,256]{1,0:T(8,128)S(1)} %shard_map.93.near), channel_id=1, source_target_pairs={{0,4},{4,0},{8,12},{12,8},{16,20},{20,16},{24,28},{28,24},{1,5},{5... | collective-permute-start | bytes 1179656 | tf_op jit(solution)/shard_map/ppermute | solution.py:41
  81.4 16.8 %collective-permute-start.25 = (f32[384,256]{1,0:T(8,128)S(1)}, f32[384,256]{1,0:T(8,128)S(1)}, u32[]{:S(2)}, u32[]{:S(2)}) collective-permute-start(f32[384,256]{1,0:T(8,128)S(1)} %shard_map.85.far), channel_id=1, source_target_pairs={{0,4},{4,0},{8,12},{12,8},{16,20},{20,16},{24,28},{28,24},{1,5},{5... | collective-permute-start | bytes 1179656 | tf_op jit(solution)/shard_map/ppermute | solution.py:41
  81.9 5.8 %collective-permute-start.7 = (f32[64,512]{1,0:T(8,128)S(1)}, f32[64,512]{1,0:T(8,128)S(1)}, u32[]{:S(2)}, u32[]{:S(2)}) collective-permute-start(f32[64,512]{1,0:T(8,128)S(1)} %get-tuple-element.65), channel_id=1, source_target_pairs={{0,8},{4,12},{8,0},{12,4},{16,24},{20,28},{24,16},{28,20},{1,9},{5... | collective-permute-start | bytes 393224 | tf_op jit(solution)/shard_map/ppermute | solution.py:41
  83.5 8.2 %collective-permute-start.8 = (f32[64,512]{1,0:T(8,128)S(1)}, f32[64,512]{1,0:T(8,128)S(1)}, u32[]{:S(2)}, u32[]{:S(2)}) collective-permute-start(f32[64,512]{1,0:T(8,128)S(1)} %get-tuple-element.66), channel_id=1, source_target_pairs={{0,16},{4,20},{8,24},{12,28},{16,0},{20,4},{24,8},{28,12},{1,17},{... | collective-permute-start | bytes 393224 | tf_op jit(solution)/shard_map/ppermute | solution.py:41
  83.8 8.0 %collective-permute-start.9 = (f32[64,512]{1,0:T(8,128)S(1)}, f32[64,512]{1,0:T(8,128)S(1)}, u32[]{:S(2)}, u32[]{:S(2)}) collective-permute-start(f32[64,512]{1,0:T(8,128)S(1)} %get-tuple-element.67), channel_id=1, source_target_pairs={{0,24},{4,28},{8,16},{12,20},{16,8},{20,12},{24,0},{28,4},{1,25},{... | collective-permute-start | bytes 393224 | tf_op jit(solution)/shard_map/ppermute | solution.py:41
  87.7 6.0 %collective-permute-start.14 = (f32[64,512]{1,0:T(8,128)S(1)}, f32[64,512]{1,0:T(8,128)S(1)}, u32[]{:S(2)}, u32[]{:S(2)}) collective-permute-start(f32[64,512]{1,0:T(8,128)S(1)} %get-tuple-element.84), channel_id=1, source_target_pairs={{0,8},{4,12},{8,0},{12,4},{16,24},{20,28},{24,16},{28,20},{1,9},{5... | collective-permute-start | bytes 393224 | tf_op jit(solution)/shard_map/ppermute | solution.py:41
  91.7 6.4 %collective-permute-start.15 = (f32[64,512]{1,0:T(8,128)S(1)}, f32[64,512]{1,0:T(8,128)S(1)}, u32[]{:S(2)}, u32[]{:S(2)}) collective-permute-start(f32[64,512]{1,0:T(8,128)S(1)} %get-tuple-element.85), channel_id=1, source_target_pairs={{0,16},{4,20},{8,24},{12,28},{16,0},{20,4},{24,8},{28,12},{1,17},{... | collective-permute-start | bytes 393224 | tf_op jit(solution)/shard_map/ppermute | solution.py:41
  91.7 6.4 %collective-permute-start.16 = (f32[64,512]{1,0:T(8,128)S(1)}, f32[64,512]{1,0:T(8,128)S(1)}, u32[]{:S(2)}, u32[]{:S(2)}) collective-permute-start(f32[64,512]{1,0:T(8,128)S(1)} %get-tuple-element.86), channel_id=1, source_target_pairs={{0,24},{4,28},{8,16},{12,20},{16,8},{20,12},{24,0},{28,4},{1,25},{... | collective-permute-start | bytes 393224 | tf_op jit(solution)/shard_map/ppermute | solution.py:41

commit v4 on v3

--- a/solution.py
+++ b/solution.py
@@ -321,16 +321,21 @@
         copy.wait()
 
 
-def collect_body(f0, f1, f2, f3, g0, g1, g2, g3, far, far_got, near, near_got,
-                 features, grads, grad_far, grad_near, sems):
-    core, chip, _ = bits()
+def fields_body(f0, f1, f2, f3, g0, g1, g2, g3, features, grads, sems):
+    chip = bits()[1]
     size = f0.shape[0]
+    run_copies(
+        [
+            pltpu.make_async_copy(piece, to.at[block(chip ^ mask, size)], sems.at[4 * k + mask])
+            for k, (to, parts) in enumerate(((features, (f0, f1, f2, f3)), (grads, (g0, g1, g2, g3))))
+            for mask, piece in enumerate(parts)
+        ]
+    )
+
+
+def columns_body(far, far_got, near, near_got, grad_far, grad_near, sems):
+    core = bits()[0]
     width = far.shape[1]
-    copies = [
-        (piece, to.at[block(chip ^ mask, size)])
-        for to, parts in ((features, (f0, f1, f2, f3)), (grads, (g0, g1, g2, g3)))
-        for mask, piece in enumerate(parts)
-    ]
 
     def place(swapped):
         columns = [
@@ -338,9 +343,7 @@
             for out, parts in ((grad_far, (far, far_got)), (grad_near, (near, near_got)))
             for k, part in enumerate(parts)
         ]
-        run_copies(
-            [pltpu.make_async_copy(*pair, sems.at[k]) for k, pair in enumerate(copies + columns)]
-        )
+        run_copies([pltpu.make_async_copy(*pair, sems.at[k]) for k, pair in enumerate(columns)])
 
     @pl.when(core == 0)
     def _():
@@ -448,10 +451,13 @@
     near_all = over_chips([near_mine] * 4)
     (rows_near,) = call(near_rows_body, rows_all, *near_all)
     near_cols = swap(rows_near, "hi", 1)
-    wide = ((part, width), F32)
-    features, grad_track, grad_far, grad_near = hbm_call(
-        collect_body, [(full, F32)] * 2 + [wide] * 2, (pltpu.VMEM, pltpu.HBM),
-        (*feats, *grads, rows_far, far_cols, rows_near, near_cols), [pltpu.SemaphoreType.DMA((12,))], 2,
+    to_hbm = (pltpu.VMEM, pltpu.HBM)
+    features, grad_track = hbm_call(
+        fields_body, [(full, F32)] * 2, to_hbm, (*feats, *grads), [pltpu.SemaphoreType.DMA((8,))], 2
+    )
+    grad_far, grad_near = hbm_call(
+        columns_body, [((part, width), F32)] * 2, to_hbm, (rows_far, far_cols, rows_near, near_cols),
+        [pltpu.SemaphoreType.DMA((4,))], 2,
     )
     return features, grad_track, grad_near, grad_far
 

time: 99.9 us -> 101 us (1.011)
    pallas_call x2 -> x3, Pallas kernels: 4.79 us -> 5.4 us  [hbm_call(): pl.pallas_call(body, out_shape=[out_place(shape, dtype) for shape, dtype...]
  transfers between devices with their start and end apart: 37 -> 37, of which waited for: 14 -> 14; matrix products, arithmetic and copies ran while one was open for 0% -> 0% of each run, Pallas kernels for 12% -> 13%
where the time goes in v4:
time: 101 us; the launch traced here: 100 us
  starting transfers between devices  43.6 us (43%)
  waiting for transfers between devices  39.2 us (39%)
  Pallas kernels  15.5 us (15%)
  local copies, waits for them, and re-layouts  1.14 us (1%)
    ppermute x29, starting transfers between devices, swap(): return lax.ppermute(value, axis, [(i, i ^ mask) for i in range(count)])  34.1 us
    ppermute x29, waiting for transfers between devices, swap(): return lax.ppermute(value, axis, [(i, i ^ mask) for i in range(count)])  29.8 us
    pallas_call x18, Pallas kernels, call(): pl.pallas_call(body, out_shape=[make(shape, dtype) for shape, dtype in ou...  10.1 us
    ppermute x8, starting transfers between devices, plane_swap(): lax.ppermute(value, 'hi', [(i, i ^ 2 << (i + turn) % 2) for i in range(co...  9.53 us
    ppermute x8, waiting for transfers between devices, plane_swap(): lax.ppermute(value, 'hi', [(i, i ^ 2 << (i + turn) % 2) for i in range(co...  9.37 us
    pallas_call x3, Pallas kernels, hbm_call(): pl.pallas_call(body, out_shape=[out_place(shape, dtype) for shape, dtype...  5.4 us
  transfers between devices with their start and end apart: 37, of which 14 were waited for; matrix products, arithmetic and copies ran while one was open for 0% of the time, Pallas kernels for 13%

profile of v4, /device:TPU:0, one launch (start us, length us, event | category | flops | bytes accessed | tf_op | source)
XLA Modules:
  0.0 100.4 jit_solution(8563694087319453174)
XLA Ops:
  0.7 1.1 %constant_dynamic-slice_fusion = (f32[64,512]{1,0:T(8,128)S(1)}, f32[64,512]{1,0:T(8,128)S(1)}, f32[64,512]{1,0:T(8,128)S(1)}, f32[64,512]{1,0:T(8,128)S(1)}) fusion(f32[256,512]{1,0:T(8,128)} %param.4, s32[]{:T(128)S(6)} %select_n.15, s32[]{:T(128)S(6)} %select_n.13, s32[]{:T(128)S(6)} %select_n.12, s32[]{:T(128)S(6)} %select_n.14), kind=kLoop, calls=%fused_computation | loop fusion | bytes 1048592 | tf_op jit(solution)/shard_map/dynamic_slice | solution.py:359
  1.8 4.0 %collective-permute-start.2 = (f32[64,512]{1,0:T(8,128)S(1)}, f32[64,512]{1,0:T(8,128)S(1)}, u32[]{:S(2)}, u32[]{:S(2)}) collective-permute-start(f32[64,512]{1,0:T(8,128)S(1)} %get-tuple-element.116), channel_id=1, source_target_pairs={{0,24},{4,28},{8,16},{12,20},{16,8},{20,12},{24,0},{28,4},{1,25},{... | collective-permute-start | bytes 393224 | tf_op jit(solution)/shard_map/ppermute | solution.py:41
  5.8 0.5 collective-permute-start
  6.3 0.1 collective-permute-start.1
  6.4 0.0 collective-permute-start.3
  6.4 3.7 %collective-permute-done.2.p3 = f32[64,512]{1,0:T(8,128)S(1)} collective-permute-done((f32[64,512]{1,0:T(8,128)S(1)}, f32[64,512]{1,0:T(8,128)S(1)}, u32[]{:S(2)}, u32[]{:S(2)}) %collective-permute-start.2) | collective-permute-done | bytes 131104 | tf_op jit(solution)/shard_map/ppermute | solution.py:41
  10.1 3.2 %shard_map.75 = (bf16[1536,512]{1,0:T(8,128)(2,1)S(1)}, bf16[1536,512]{1,0:T(8,128)(2,1)S(1)}, bf16[1536,512]{1,0:T(8,128)(2,1)S(1)}, bf16[1536,512]{1,0:T(8,128...) custom-call(f32[1536,512]{1,0:T(8,128)} %near.1, ...), custom_call_target="tpu_custom_call" | custom-call | tf_op jit(solution)/shard_map/pallas_call | solution.py:116
  13.3 0.0 collective-permute-done.p1
  13.3 0.6 collective-permute-start.4
  13.9 0.1 collective-permute-start.5
  14.0 2.0 %collective-permute-start.10 = (f32[64,512]{1,0:T(8,128)S(1)}, f32[64,512]{1,0:T(8,128)S(1)}, u32[]{:S(2)}, u32[]{:S(2)}) collective-permute-start(f32[64,512]{1,0:T(8,128)S(1)} %get-tuple-element.69), channel_id=1, source_target_pairs={{0,8},{4,12},{8,0},{12,4},{16,24},{20,28},{24,16},{28,20},{1,9},{5... | collective-permute-start | bytes 393224 | tf_op jit(solution)/shard_map/ppermute | solution.py:41
  16.0 1.5 %collective-permute-start.11 = (f32[64,512]{1,0:T(8,128)S(1)}, f32[64,512]{1,0:T(8,128)S(1)}, u32[]{:S(2)}, u32[]{:S(2)}) collective-permute-start(f32[64,512]{1,0:T(8,128)S(1)} %get-tuple-element.70), channel_id=1, source_target_pairs={{0,16},{4,20},{8,24},{12,28},{16,0},{20,4},{24,8},{28,12},{1,17},{... | collective-permute-start | bytes 393224 | tf_op jit(solution)/shard_map/ppermute | solution.py:41
  17.5 0.0 collective-permute-start.12
  17.5 3.1 %shard_map.76 = (f32[64,512]{1,0:T(8,128)S(1)}, f32[64,512]{1,0:T(8,128)S(1)}, f32[64,512]{1,0:T(8,128)S(1)}, f32[64,512]{1,0:T(8,128)S(1)}, f32[256,512]{1,0:T(...) custom-call(f32[64,512]{1,0:T(8,128)S(1)} %get-tuple-element.118.p0,, ...), custom_call_target="tpu_custom_call" | custom-call | tf_op jit(solution)/shard_map/pallas_call | solution.py:29
  20.7 3.7 %collective-permute-done.11.c2 = f32[64,512]{1,0:T(8,128)S(1)} collective-permute-done((f32[64,512]{1,0:T(8,128)S(1)}, f32[64,512]{1,0:T(8,128)S(1)}, u32[]{:S(2)}, u32[]{:S(2)}) %collective-permute-start.11) | collective-permute-done | bytes 131104 | tf_op jit(solution)/shard_map/ppermute | solution.py:41
  24.3 0.9 shard_map.77
  25.2 0.1 collective-permute-start.17
  25.3 1.6 %shard_map.78 = (f32[256,512]{1,0:T(8,128)S(1)}, f32[256,512]{1,0:T(8,128)S(1)}, bf16[256,512]{1,0:T(8,128)(2,1)S(1)}, bf16[256,512]{1,0:T(8,128)(2,1)S(1)}) custom-call(f32[256,512]{1,0:T(8,128)S(1)} %get-tuple-element.75.cot, bf16[256,512]{1,0:T(8,128)(2,1)S(1)} %get-tuple-element.76.g_h, bf16[256,512]{1,0:T(8,128)(2,1)S(1)} %get-tuple-element.77.g_l, ...), custom_call_target="tpu_custom_call" | custom-call | tf_op jit(solution)/shard_map/pallas_call | solution.py:29
  26.9 0.6 collective-permute-start.13
  27.5 1.2 %collective-permute-done.17.got = f32[1536,256]{1,0:T(8,128)S(1)} collective-permute-done((f32[1536,256]{1,0:T(8,128)S(1)}, f32[1536,256]{1,0:T(8,128)S(1)}, u32[]{:S(2)}, u32[]{:S(2)}) %collective-permute-start.17) | collective-permute-done | bytes 1572896 | tf_op jit(solution)/shard_map/ppermute | solution.py:41
  28.7 0.9 shard_map.81
  29.6 1.3 %collective-permute-start.18 = (f32[2,192,256]{2,1,0:T(8,128)S(1)}, f32[2,192,256]{2,1,0:T(8,128)S(1)}, u32[]{:S(2)}, u32[]{:S(2)}) collective-permute-start(f32[2,192,256]{2,1,0:T(8,128)S(1)} %get-tuple-element.91), channel_id=1, source_target_pairs={{0,8},{4,20},{8,0},{12,28},{16,24},{20,4},{24,16},{28,12},{1,9},{5... | collective-permute-start | bytes 1179656 | tf_op jit(solution)/shard_map/ppermute | solution.py:46
  30.9 0.8 collective-permute-start.20
  31.7 0.8 shard_map.87.term
  32.6 0.0 collective-permute-done.13.other
  32.6 0.9 shard_map.88
  33.5 1.3 %collective-permute-start.26 = (f32[2,192,256]{2,1,0:T(8,128)S(1)}, f32[2,192,256]{2,1,0:T(8,128)S(1)}, u32[]{:S(2)}, u32[]{:S(2)}) collective-permute-start(f32[2,192,256]{2,1,0:T(8,128)S(1)} %get-tuple-element.103), channel_id=1, source_target_pairs={{0,8},{4,20},{8,0},{12,28},{16,24},{20,4},{24,16},{28,12},{1,9},{5... | collective-permute-start | bytes 1179656 | tf_op jit(solution)/shard_map/ppermute | solution.py:46
  34.8 0.8 collective-permute-start.29
  35.6 1.9 %collective-permute-done.18.got = f32[2,192,256]{2,1,0:T(8,128)S(1)} collective-permute-done((f32[2,192,256]{2,1,0:T(8,128)S(1)}, f32[2,192,256]{2,1,0:T(8,128)S(1)}, u32[]{:S(2)}, u32[]{:S(2)}) %collective-permute-start.18) | collective-permute-done | bytes 393248 | tf_op jit(solution)/shard_map/ppermute | solution.py:46
  37.5 1.6 %collective-permute-start.19 = (f32[192,256]{1,0:T(8,128)S(1)}, f32[192,256]{1,0:T(8,128)S(1)}, u32[]{:S(2)}, u32[]{:S(2)}) collective-permute-start(f32[192,256]{1,0:T(8,128)S(1)} %get-tuple-element.93), channel_id=1, source_target_pairs={{0,1},{1,0},{2,3},{3,2},{4,5},{5,4},{6,7},{7,6},{8,9},{9,8},{10,11... | collective-permute-start | bytes 589832 | tf_op jit(solution)/shard_map/ppermute | solution.py:41
  39.2 2.5 %collective-permute-done.20.got = f32[2,192,256]{2,1,0:T(8,128)S(1)} collective-permute-done((f32[2,192,256]{2,1,0:T(8,128)S(1)}, f32[2,192,256]{2,1,0:T(8,128)S(1)}, u32[]{:S(2)}, u32[]{:S(2)}) %collective-permute-start.20) | collective-permute-done | bytes 393248 | tf_op jit(solution)/shard_map/ppermute | solution.py:46
  41.7 2.7 %collective-permute-start.21 = (f32[192,256]{1,0:T(8,128)S(1)}, f32[192,256]{1,0:T(8,128)S(1)}, u32[]{:S(2)}, u32[]{:S(2)}) collective-permute-start(f32[192,256]{1,0:T(8,128)S(1)} %get-tuple-element.96), channel_id=1, source_target_pairs={{0,2},{1,3},{2,0},{3,1},{4,6},{5,7},{6,4},{7,5},{8,10},{9,11},{10,... | collective-permute-start | bytes 589832 | tf_op jit(solution)/shard_map/ppermute | solution.py:41
  44.4 1.3 %collective-permute-start.22 = (f32[192,256]{1,0:T(8,128)S(1)}, f32[192,256]{1,0:T(8,128)S(1)}, u32[]{:S(2)}, u32[]{:S(2)}) collective-permute-start(f32[192,256]{1,0:T(8,128)S(1)} %get-tuple-element.97), channel_id=1, source_target_pairs={{0,3},{1,2},{2,1},{3,0},{4,7},{5,6},{6,5},{7,4},{8,11},{9,10},{10,... | collective-permute-start | bytes 589832 | tf_op jit(solution)/shard_map/ppermute | solution.py:41
  45.8 0.2 collective-permute-done.26.got
  46.0 1.6 %collective-permute-start.27 = (f32[2,96,256]{2,1,0:T(8,128)S(1)}, f32[2,96,256]{2,1,0:T(8,128)S(1)}, u32[]{:S(2)}, u32[]{:S(2)}) collective-permute-start(f32[2,96,256]{2,1,0:T(8,128)S(1)} %get-tuple-element.105), channel_id=1, source_target_pairs={{0,16},{4,12},{8,24},{12,4},{16,0},{20,28},{24,8},{28,20},{1,17},{... | collective-permute-start | bytes 589832 | tf_op jit(solution)/shard_map/ppermute | solution.py:46
  47.5 4.8 %collective-permute-done.29.got = f32[2,192,256]{2,1,0:T(8,128)S(1)} collective-permute-done((f32[2,192,256]{2,1,0:T(8,128)S(1)}, f32[2,192,256]{2,1,0:T(8,128)S(1)}, u32[]{:S(2)}, u32[]{:S(2)}) %collective-permute-start.29) | collective-permute-done | bytes 393248 | tf_op jit(solution)/shard_map/ppermute | solution.py:46
  52.4 1.6 %collective-permute-start.30 = (f32[2,96,256]{2,1,0:T(8,128)S(1)}, f32[2,96,256]{2,1,0:T(8,128)S(1)}, u32[]{:S(2)}, u32[]{:S(2)}) collective-permute-start(f32[2,96,256]{2,1,0:T(8,128)S(1)} %get-tuple-element.111), channel_id=1, source_target_pairs={{0,16},{4,12},{8,24},{12,4},{16,0},{20,28},{24,8},{28,20},{1,17},{... | collective-permute-start | bytes 589832 | tf_op jit(solution)/shard_map/ppermute | solution.py:46
  54.0 4.5 %collective-permute-done.21.refs_2_ = f32[192,256]{1,0:T(8,128)S(1)} collective-permute-done((f32[192,256]{1,0:T(8,128)S(1)}, f32[192,256]{1,0:T(8,128)S(1)}, u32[]{:S(2)}, u32[]{:S(2)}) %collective-permute-start.21) | collective-permute-done | bytes 196640 | tf_op jit(solution)/shard_map/ppermute | solution.py:41
  58.5 1.6 %collective-permute-start.23 = (f32[192,256]{1,0:T(8,128)S(1)}, f32[192,256]{1,0:T(8,128)S(1)}, u32[]{:S(2)}, u32[]{:S(2)}) collective-permute-start(f32[192,256]{1,0:T(8,128)S(1)} %shard_map.84.own), channel_id=1, source_target_pairs={{0,16},{4,12},{8,24},{12,4},{16,0},{20,28},{24,8},{28,20},{1,17},{... | collective-permute-start | bytes 589832 | tf_op jit(solution)/shard_map/ppermute | solution.py:46
  60.1 0.0 collective-permute-done.27.got
  60.1 3.7 %collective-permute-start.28 = (f32[96,256]{1,0:T(8,128)S(1)}, f32[96,256]{1,0:T(8,128)S(1)}, u32[]{:S(2)}, u32[]{:S(2)}) collective-permute-start(f32[96,256]{1,0:T(8,128)S(1)} %get-tuple-element.107), channel_id=1, source_target_pairs={{0,1},{1,0},{2,3},{3,2},{4,5},{5,4},{6,7},{7,6},{8,9},{9,8},{10,11... | collective-permute-start | bytes 294920 | tf_op jit(solution)/shard_map/ppermute | solution.py:41
  63.8 0.0 collective-permute-done.30.got
  63.9 2.0 %collective-permute-start.31 = (f32[96,256]{1,0:T(8,128)S(1)}, f32[96,256]{1,0:T(8,128)S(1)}, u32[]{:S(2)}, u32[]{:S(2)}) collective-permute-start(f32[96,256]{1,0:T(8,128)S(1)} %get-tuple-element.112), channel_id=1, source_target_pairs={{0,2},{1,3},{2,0},{3,1},{4,6},{5,7},{6,4},{7,5},{8,10},{9,11},{10,... | collective-permute-start | bytes 294920 | tf_op jit(solution)/shard_map/ppermute | solution.py:41
  65.9 1.5 %collective-permute-start.32 = (f32[96,256]{1,0:T(8,128)S(1)}, f32[96,256]{1,0:T(8,128)S(1)}, u32[]{:S(2)}, u32[]{:S(2)}) collective-permute-start(f32[96,256]{1,0:T(8,128)S(1)} %get-tuple-element.113), channel_id=1, source_target_pairs={{0,3},{1,2},{2,1},{3,0},{4,7},{5,6},{6,5},{7,4},{8,11},{9,10},{10,... | collective-permute-start | bytes 294920 | tf_op jit(solution)/shard_map/ppermute | solution.py:41
  67.4 0.6 collective-permute-start.24
  68.0 6.5 %collective-permute-done.31.refs_2_ = f32[96,256]{1,0:T(8,128)S(1)} collective-permute-done((f32[96,256]{1,0:T(8,128)S(1)}, f32[96,256]{1,0:T(8,128)S(1)}, u32[]{:S(2)}, u32[]{:S(2)}) %collective-permute-start.31) | collective-permute-done | bytes 98336 | tf_op jit(solution)/shard_map/ppermute | solution.py:41
  74.6 0.9 collective-permute-start.35
  75.5 1.0 %collective-permute-start.34 = (f32[96,256]{1,0:T(8,128)S(1)}, f32[96,256]{1,0:T(8,128)S(1)}, u32[]{:S(2)}, u32[]{:S(2)}) collective-permute-start(f32[96,256]{1,0:T(8,128)S(1)} %shard_map.93.s0), channel_id=1, source_target_pairs={{0,16},{4,20},{8,24},{12,28},{16,0},{20,4},{24,8},{28,12},{1,17},{... | collective-permute-start | bytes 294920 | tf_op jit(solution)/shard_map/ppermute | solution.py:41
  76.5 1.6 %collective-permute-start.33 = (f32[96,256]{1,0:T(8,128)S(1)}, f32[96,256]{1,0:T(8,128)S(1)}, u32[]{:S(2)}, u32[]{:S(2)}) collective-permute-start(f32[96,256]{1,0:T(8,128)S(1)} %shard_map.93.s0), channel_id=1, source_target_pairs={{0,8},{4,12},{8,0},{12,4},{16,24},{20,28},{24,16},{28,20},{1,9},{5... | collective-permute-start | bytes 294920 | tf_op jit(solution)/shard_map/ppermute | solution.py:41
  78.1 2.2 %collective-permute-done.35.s3 = f32[96,256]{1,0:T(8,128)S(1)} collective-permute-done((f32[96,256]{1,0:T(8,128)S(1)}, f32[96,256]{1,0:T(8,128)S(1)}, u32[]{:S(2)}, u32[]{:S(2)}) %collective-permute-start.35) | collective-permute-done | bytes 98336 | tf_op jit(solution)/shard_map/ppermute | solution.py:41
  80.3 0.8 collective-permute-done.34.s2
  81.2 0.1 collective-permute-start.36
  81.4 0.5 collective-permute-start.25
  81.9 1.6 %collective-permute-start.7 = (f32[64,512]{1,0:T(8,128)S(1)}, f32[64,512]{1,0:T(8,128)S(1)}, u32[]{:S(2)}, u32[]{:S(2)}) collective-permute-start(f32[64,512]{1,0:T(8,128)S(1)} %get-tuple-element.65), channel_id=1, source_target_pairs={{0,8},{4,12},{8,0},{12,4},{16,24},{20,28},{24,16},{28,20},{1,9},{5... | collective-permute-start | bytes 393224 | tf_op jit(solution)/shard_map/ppermute | solution.py:41
  83.5 0.3 collective-permute-start.8
  83.8 1.6 %collective-permute-start.9 = (f32[64,512]{1,0:T(8,128)S(1)}, f32[64,512]{1,0:T(8,128)S(1)}, u32[]{:S(2)}, u32[]{:S(2)}) collective-permute-start(f32[64,512]{1,0:T(8,128)S(1)} %get-tuple-element.67), channel_id=1, source_target_pairs={{0,24},{4,28},{8,16},{12,20},{16,8},{20,12},{24,0},{28,4},{1,25},{... | collective-permute-start | bytes 393224 | tf_op jit(solution)/shard_map/ppermute | solution.py:41
  85.4 1.4 %shard_map.79 = (f32[64,512]{1,0:T(8,128)S(1)}, f32[64,512]{1,0:T(8,128)S(1)}, f32[64,512]{1,0:T(8,128)S(1)}, f32[64,512]{1,0:T(8,128)S(1)}) custom-call(f32[256,512]{1,0:T(8,128)S(1)} %get-tuple-element.79.grad, bf16[256,512]{1,0:T(8,128)(2,1)S(1)} %get-tuple-element.80.gn_h, bf16[256,512]{1,0:T(8,128)(2,1)S(1)} %get-tuple-element.81.gn_l, ...), custom_call_target="tpu_custom_call" | custom-call | tf_op jit(solution)/shard_map/pallas_call | solution.py:29
  86.9 0.8 collective-permute-done.7.f1
  87.7 2.2 %collective-permute-start.14 = (f32[64,512]{1,0:T(8,128)S(1)}, f32[64,512]{1,0:T(8,128)S(1)}, u32[]{:S(2)}, u32[]{:S(2)}) collective-permute-start(f32[64,512]{1,0:T(8,128)S(1)} %get-tuple-element.84), channel_id=1, source_target_pairs={{0,8},{4,12},{8,0},{12,4},{16,24},{20,28},{24,16},{28,20},{1,9},{5... | collective-permute-start | bytes 393224 | tf_op jit(solution)/shard_map/ppermute | solution.py:41
  89.9 1.9 %collective-permute-done.8.f2 = f32[64,512]{1,0:T(8,128)S(1)} collective-permute-done((f32[64,512]{1,0:T(8,128)S(1)}, f32[64,512]{1,0:T(8,128)S(1)}, u32[]{:S(2)}, u32[]{:S(2)}) %collective-permute-start.8) | collective-permute-done | bytes 131104 | tf_op jit(solution)/shard_map/ppermute | solution.py:41
  91.7 1.9 %collective-permute-start.16 = (f32[64,512]{1,0:T(8,128)S(1)}, f32[64,512]{1,0:T(8,128)S(1)}, u32[]{:S(2)}, u32[]{:S(2)}) collective-permute-start(f32[64,512]{1,0:T(8,128)S(1)} %get-tuple-element.86), channel_id=1, source_target_pairs={{0,24},{4,28},{8,16},{12,20},{16,8},{20,12},{24,0},{28,4},{1,25},{... | collective-permute-start | bytes 393224 | tf_op jit(solution)/shard_map/ppermute | solution.py:41
  93.7 4.4 %collective-permute-done.15.g2 = f32[64,512]{1,0:T(8,128)S(1)} collective-permute-done((f32[64,512]{1,0:T(8,128)S(1)}, f32[64,512]{1,0:T(8,128)S(1)}, u32[]{:S(2)}, u32[]{:S(2)}) %collective-permute-start.15) | collective-permute-done | bytes 131104 | tf_op jit(solution)/shard_map/ppermute | solution.py:41
  98.1 1.0 %shard_map.80 = (f32[256,512]{1,0:T(8,128)}, f32[256,512]{1,0:T(8,128)}) custom-call(f32[64,512]{1,0:T(8,128)S(1)} %get-tuple-element.64.f0, f32[64,512]{1,0:T(8,128)S(1)} %collective-permute-done.7.f1, f32[64,512]{1,0:T(8,128)S(1)} %collective-permute-done.8.f2, f32[64,512]{1,0:T(8,128)S(1)} %collective-permute-done.9.f3, ...), custom_call_target="tpu_custom_call" | custom-call | tf_op jit(solution)/shard_map/pallas_call | solution.py:116
  99.2 1.2 %shard_map.95 = (f32[384,512]{1,0:T(8,128)}, f32[384,512]{1,0:T(8,128)}) custom-call(f32[384,256]{1,0:T(8,128)S(1)} %shard_map.86.far, f32[384,256]{1,0:T(8,128)S(1)} %collective-permute-done.25.far_got, f32[384,256]{1,0:T(8,128)S(1)} %shard_map.94.near, f32[384,256]{1,0:T(8,128)S(1)} %collective-permute-done.36.near_got), custom_call_target="tpu_custom_call" | custom-call | tf_op jit(solution)/shard_map/pallas_call | solution.py:116
  (32 shorter events, 0.4 us)
Async XLA Ops:
  1.8 8.3 %collective-permute-start.2 = (f32[64,512]{1,0:T(8,128)S(1)}, f32[64,512]{1,0:T(8,128)S(1)}, u32[]{:S(2)}, u32[]{:S(2)}) collective-permute-start(f32[64,512]{1,0:T(8,128)S(1)} %get-tuple-element.116), channel_id=1, source_target_pairs={{0,24},{4,28},{8,16},{12,20},{16,8},{20,12},{24,0},{28,4},{1,25},{... | collective-permute-start | bytes 393224 | tf_op jit(solution)/shard_map/ppermute | solution.py:41
  5.8 7.6 %collective-permute-start = (f32[64,512]{1,0:T(8,128)S(1)}, f32[64,512]{1,0:T(8,128)S(1)}, u32[]{:S(2)}, u32[]{:S(2)}) collective-permute-start(f32[64,512]{1,0:T(8,128)S(1)} %get-tuple-element.117), channel_id=1, source_target_pairs={{0,8},{4,12},{8,0},{12,4},{16,24},{20,28},{24,16},{28,20},{1,9},{5... | collective-permute-start | bytes 393224 | tf_op jit(solution)/shard_map/ppermute | solution.py:41
  6.3 7.6 %collective-permute-start.1 = (f32[64,512]{1,0:T(8,128)S(1)}, f32[64,512]{1,0:T(8,128)S(1)}, u32[]{:S(2)}, u32[]{:S(2)}) collective-permute-start(f32[64,512]{1,0:T(8,128)S(1)} %get-tuple-element.119), channel_id=1, source_target_pairs={{0,16},{4,20},{8,24},{12,28},{16,0},{20,4},{24,8},{28,12},{1,17},{... | collective-permute-start | bytes 393224 | tf_op jit(solution)/shard_map/ppermute | solution.py:41
  6.4 9.5 %collective-permute-start.3 = (f32[64,512]{1,0:T(8,128)S(1)}, f32[64,512]{1,0:T(8,128)S(1)}, u32[]{:S(2)}, u32[]{:S(2)}) collective-permute-start(f32[64,512]{1,0:T(8,128)S(1)} %get-tuple-element.118.p0), channel_id=1, source_target_pairs={{0,4},{4,0},{8,12},{12,8},{16,20},{20,16},{24,28},{28,24},{1,5},{5... | collective-permute-start | bytes 393224 | tf_op jit(solution)/shard_map/ppermute | solution.py:41
  10.1 7.4 %collective-permute-start.6 = (f32[64,512]{1,0:T(8,128)S(1)}, f32[64,512]{1,0:T(8,128)S(1)}, u32[]{:S(2)}, u32[]{:S(2)}) collective-permute-start(f32[64,512]{1,0:T(8,128)S(1)} %collective-permute-done.2.p3), channel_id=1, source_target_pairs={{0,4},{4,0},{8,12},{12,8},{16,20},{20,16},{24,28},{28,24},{1,5},{5... | collective-permute-start | bytes 393224 | tf_op jit(solution)/shard_map/ppermute | solution.py:41
  13.3 4.2 %collective-permute-start.4 = (f32[64,512]{1,0:T(8,128)S(1)}, f32[64,512]{1,0:T(8,128)S(1)}, u32[]{:S(2)}, u32[]{:S(2)}) collective-permute-start(f32[64,512]{1,0:T(8,128)S(1)} %collective-permute-done.p1), channel_id=1, source_target_pairs={{0,4},{4,0},{8,12},{12,8},{16,20},{20,16},{24,28},{28,24},{1,5},{5... | collective-permute-start | bytes 393224 | tf_op jit(solution)/shard_map/ppermute | solution.py:41
  13.9 3.6 %collective-permute-start.5 = (f32[64,512]{1,0:T(8,128)S(1)}, f32[64,512]{1,0:T(8,128)S(1)}, u32[]{:S(2)}, u32[]{:S(2)}) collective-permute-start(f32[64,512]{1,0:T(8,128)S(1)} %collective-permute-done.1.p2), channel_id=1, source_target_pairs={{0,4},{4,0},{8,12},{12,8},{16,20},{20,16},{24,28},{28,24},{1,5},{5... | collective-permute-start | bytes 393224 | tf_op jit(solution)/shard_map/ppermute | solution.py:41
  14.0 6.6 %collective-permute-start.10 = (f32[64,512]{1,0:T(8,128)S(1)}, f32[64,512]{1,0:T(8,128)S(1)}, u32[]{:S(2)}, u32[]{:S(2)}) collective-permute-start(f32[64,512]{1,0:T(8,128)S(1)} %get-tuple-element.69), channel_id=1, source_target_pairs={{0,8},{4,12},{8,0},{12,4},{16,24},{20,28},{24,16},{28,20},{1,9},{5... | collective-permute-start | bytes 393224 | tf_op jit(solution)/shard_map/ppermute | solution.py:41
  16.0 8.4 %collective-permute-start.11 = (f32[64,512]{1,0:T(8,128)S(1)}, f32[64,512]{1,0:T(8,128)S(1)}, u32[]{:S(2)}, u32[]{:S(2)}) collective-permute-start(f32[64,512]{1,0:T(8,128)S(1)} %get-tuple-element.70), channel_id=1, source_target_pairs={{0,16},{4,20},{8,24},{12,28},{16,0},{20,4},{24,8},{28,12},{1,17},{... | collective-permute-start | bytes 393224 | tf_op jit(solution)/shard_map/ppermute | solution.py:41
  17.5 6.8 %collective-permute-start.12 = (f32[64,512]{1,0:T(8,128)S(1)}, f32[64,512]{1,0:T(8,128)S(1)}, u32[]{:S(2)}, u32[]{:S(2)}) collective-permute-start(f32[64,512]{1,0:T(8,128)S(1)} %get-tuple-element.71), channel_id=1, source_target_pairs={{0,24},{4,28},{8,16},{12,20},{16,8},{20,12},{24,0},{28,4},{1,25},{... | collective-permute-start | bytes 393224 | tf_op jit(solution)/shard_map/ppermute | solution.py:41
  25.2 3.5 %collective-permute-start.17 = (f32[1536,256]{1,0:T(8,128)S(1)}, f32[1536,256]{1,0:T(8,128)S(1)}, u32[]{:S(2)}, u32[]{:S(2)}) collective-permute-start(f32[1536,256]{1,0:T(8,128)S(1)} %get-tuple-element.89), channel_id=1, source_target_pairs={{0,4},{4,0},{8,12},{12,8},{16,20},{20,16},{24,28},{28,24},{1,5},{5... | collective-permute-start | bytes 4718600 | tf_op jit(solution)/shard_map/ppermute | solution.py:41
  26.9 5.7 %collective-permute-start.13 = (f32[256,512]{1,0:T(8,128)S(1)}, f32[256,512]{1,0:T(8,128)S(1)}, u32[]{:S(2)}, u32[]{:S(2)}) collective-permute-start(f32[256,512]{1,0:T(8,128)S(1)} %get-tuple-element.82), channel_id=1, source_target_pairs={{0,4},{4,0},{8,12},{12,8},{16,20},{20,16},{24,28},{28,24},{1,5},{5... | collective-permute-start | bytes 1572872 | tf_op jit(solution)/shard_map/ppermute | solution.py:41
  29.6 7.8 %collective-permute-start.18 = (f32[2,192,256]{2,1,0:T(8,128)S(1)}, f32[2,192,256]{2,1,0:T(8,128)S(1)}, u32[]{:S(2)}, u32[]{:S(2)}) collective-permute-start(f32[2,192,256]{2,1,0:T(8,128)S(1)} %get-tuple-element.91), channel_id=1, source_target_pairs={{0,8},{4,20},{8,0},{12,28},{16,24},{20,4},{24,16},{28,12},{1,9},{5... | collective-permute-start | bytes 1179656 | tf_op jit(solution)/shard_map/ppermute | solution.py:46
  30.9 10.8 %collective-permute-start.20 = (f32[2,192,256]{2,1,0:T(8,128)S(1)}, f32[2,192,256]{2,1,0:T(8,128)S(1)}, u32[]{:S(2)}, u32[]{:S(2)}) collective-permute-start(f32[2,192,256]{2,1,0:T(8,128)S(1)} %get-tuple-element.95), channel_id=1, source_target_pairs={{0,8},{4,20},{8,0},{12,28},{16,24},{20,4},{24,16},{28,12},{1,9},{5... | collective-permute-start | bytes 1179656 | tf_op jit(solution)/shard_map/ppermute | solution.py:46
  33.5 12.4 %collective-permute-start.26 = (f32[2,192,256]{2,1,0:T(8,128)S(1)}, f32[2,192,256]{2,1,0:T(8,128)S(1)}, u32[]{:S(2)}, u32[]{:S(2)}) collective-permute-start(f32[2,192,256]{2,1,0:T(8,128)S(1)} %get-tuple-element.103), channel_id=1, source_target_pairs={{0,8},{4,20},{8,0},{12,28},{16,24},{20,4},{24,16},{28,12},{1,9},{5... | collective-permute-start | bytes 1179656 | tf_op jit(solution)/shard_map/ppermute | solution.py:46
  34.8 17.5 %collective-permute-start.29 = (f32[2,192,256]{2,1,0:T(8,128)S(1)}, f32[2,192,256]{2,1,0:T(8,128)S(1)}, u32[]{:S(2)}, u32[]{:S(2)}) collective-permute-start(f32[2,192,256]{2,1,0:T(8,128)S(1)} %get-tuple-element.109), channel_id=1, source_target_pairs={{0,8},{4,20},{8,0},{12,28},{16,24},{20,4},{24,16},{28,12},{1,9},{5... | collective-permute-start | bytes 1179656 | tf_op jit(solution)/shard_map/ppermute | solution.py:46
  37.5 16.4 %collective-permute-start.19 = (f32[192,256]{1,0:T(8,128)S(1)}, f32[192,256]{1,0:T(8,128)S(1)}, u32[]{:S(2)}, u32[]{:S(2)}) collective-permute-start(f32[192,256]{1,0:T(8,128)S(1)} %get-tuple-element.93), channel_id=1, source_target_pairs={{0,1},{1,0},{2,3},{3,2},{4,5},{5,4},{6,7},{7,6},{8,9},{9,8},{10,11... | collective-permute-start | bytes 589832 | tf_op jit(solution)/shard_map/ppermute | solution.py:41
  41.7 16.7 %collective-permute-start.21 = (f32[192,256]{1,0:T(8,128)S(1)}, f32[192,256]{1,0:T(8,128)S(1)}, u32[]{:S(2)}, u32[]{:S(2)}) collective-permute-start(f32[192,256]{1,0:T(8,128)S(1)} %get-tuple-element.96), channel_id=1, source_target_pairs={{0,2},{1,3},{2,0},{3,1},{4,6},{5,7},{6,4},{7,5},{8,10},{9,11},{10,... | collective-permute-start | bytes 589832 | tf_op jit(solution)/shard_map/ppermute | solution.py:41
  44.4 14.0 %collective-permute-start.22 = (f32[192,256]{1,0:T(8,128)S(1)}, f32[192,256]{1,0:T(8,128)S(1)}, u32[]{:S(2)}, u32[]{:S(2)}) collective-permute-start(f32[192,256]{1,0:T(8,128)S(1)} %get-tuple-element.97), channel_id=1, source_target_pairs={{0,3},{1,2},{2,1},{3,0},{4,7},{5,6},{6,5},{7,4},{8,11},{9,10},{10,... | collective-permute-start | bytes 589832 | tf_op jit(solution)/shard_map/ppermute | solution.py:41
  46.0 14.1 %collective-permute-start.27 = (f32[2,96,256]{2,1,0:T(8,128)S(1)}, f32[2,96,256]{2,1,0:T(8,128)S(1)}, u32[]{:S(2)}, u32[]{:S(2)}) collective-permute-start(f32[2,96,256]{2,1,0:T(8,128)S(1)} %get-tuple-element.105), channel_id=1, source_target_pairs={{0,16},{4,12},{8,24},{12,4},{16,0},{20,28},{24,8},{28,20},{1,17},{... | collective-permute-start | bytes 589832 | tf_op jit(solution)/shard_map/ppermute | solution.py:46
  52.4 11.4 %collective-permute-start.30 = (f32[2,96,256]{2,1,0:T(8,128)S(1)}, f32[2,96,256]{2,1,0:T(8,128)S(1)}, u32[]{:S(2)}, u32[]{:S(2)}) collective-permute-start(f32[2,96,256]{2,1,0:T(8,128)S(1)} %get-tuple-element.111), channel_id=1, source_target_pairs={{0,16},{4,12},{8,24},{12,4},{16,0},{20,28},{24,8},{28,20},{1,17},{... | collective-permute-start | bytes 589832 | tf_op jit(solution)/shard_map/ppermute | solution.py:46
  58.5 8.9 %collective-permute-start.23 = (f32[192,256]{1,0:T(8,128)S(1)}, f32[192,256]{1,0:T(8,128)S(1)}, u32[]{:S(2)}, u32[]{:S(2)}) collective-permute-start(f32[192,256]{1,0:T(8,128)S(1)} %shard_map.84.own), channel_id=1, source_target_pairs={{0,16},{4,12},{8,24},{12,4},{16,0},{20,28},{24,8},{28,20},{1,17},{... | collective-permute-start | bytes 589832 | tf_op jit(solution)/shard_map/ppermute | solution.py:46
  60.1 7.9 %collective-permute-start.28 = (f32[96,256]{1,0:T(8,128)S(1)}, f32[96,256]{1,0:T(8,128)S(1)}, u32[]{:S(2)}, u32[]{:S(2)}) collective-permute-start(f32[96,256]{1,0:T(8,128)S(1)} %get-tuple-element.107), channel_id=1, source_target_pairs={{0,1},{1,0},{2,3},{3,2},{4,5},{5,4},{6,7},{7,6},{8,9},{9,8},{10,11... | collective-permute-start | bytes 294920 | tf_op jit(solution)/shard_map/ppermute | solution.py:41
  63.9 10.7 %collective-permute-start.31 = (f32[96,256]{1,0:T(8,128)S(1)}, f32[96,256]{1,0:T(8,128)S(1)}, u32[]{:S(2)}, u32[]{:S(2)}) collective-permute-start(f32[96,256]{1,0:T(8,128)S(1)} %get-tuple-element.112), channel_id=1, source_target_pairs={{0,2},{1,3},{2,0},{3,1},{4,6},{5,7},{6,4},{7,5},{8,10},{9,11},{10,... | collective-permute-start | bytes 294920 | tf_op jit(solution)/shard_map/ppermute | solution.py:41
  65.9 8.7 %collective-permute-start.32 = (f32[96,256]{1,0:T(8,128)S(1)}, f32[96,256]{1,0:T(8,128)S(1)}, u32[]{:S(2)}, u32[]{:S(2)}) collective-permute-start(f32[96,256]{1,0:T(8,128)S(1)} %get-tuple-element.113), channel_id=1, source_target_pairs={{0,3},{1,2},{2,1},{3,0},{4,7},{5,6},{6,5},{7,4},{8,11},{9,10},{10,... | collective-permute-start | bytes 294920 | tf_op jit(solution)/shard_map/ppermute | solution.py:41
  67.4 13.9 %collective-permute-start.24 = (f32[192,256]{1,0:T(8,128)S(1)}, f32[192,256]{1,0:T(8,128)S(1)}, u32[]{:S(2)}, u32[]{:S(2)}) collective-permute-start(f32[192,256]{1,0:T(8,128)S(1)} %shard_map.85.own), channel_id=1, source_target_pairs={{0,8},{4,20},{8,0},{12,28},{16,24},{20,4},{24,16},{28,12},{1,9},{5... | collective-permute-start | bytes 589832 | tf_op jit(solution)/shard_map/ppermute | solution.py:46
  74.6 5.7 %collective-permute-start.35 = (f32[96,256]{1,0:T(8,128)S(1)}, f32[96,256]{1,0:T(8,128)S(1)}, u32[]{:S(2)}, u32[]{:S(2)}) collective-permute-start(f32[96,256]{1,0:T(8,128)S(1)} %shard_map.93.s0), channel_id=1, source_target_pairs={{0,24},{4,28},{8,16},{12,20},{16,8},{20,12},{24,0},{28,4},{1,25},{... | collective-permute-start | bytes 294920 | tf_op jit(solution)/shard_map/ppermute | solution.py:41
  75.5 5.7 %collective-permute-start.34 = (f32[96,256]{1,0:T(8,128)S(1)}, f32[96,256]{1,0:T(8,128)S(1)}, u32[]{:S(2)}, u32[]{:S(2)}) collective-permute-start(f32[96,256]{1,0:T(8,128)S(1)} %shard_map.93.s0), channel_id=1, source_target_pairs={{0,16},{4,20},{8,24},{12,28},{16,0},{20,4},{24,8},{28,12},{1,17},{... | collective-permute-start | bytes 294920 | tf_op jit(solution)/shard_map/ppermute | solution.py:41
  76.5 4.7 %collective-permute-start.33 = (f32[96,256]{1,0:T(8,128)S(1)}, f32[96,256]{1,0:T(8,128)S(1)}, u32[]{:S(2)}, u32[]{:S(2)}) collective-permute-start(f32[96,256]{1,0:T(8,128)S(1)} %shard_map.93.s0), channel_id=1, source_target_pairs={{0,8},{4,12},{8,0},{12,4},{16,24},{20,28},{24,16},{28,20},{1,9},{5... | collective-permute-start | bytes 294920 | tf_op jit(solution)/shard_map/ppermute | solution.py:41
  81.2 17.9 %collective-permute-start.36 = (f32[384,256]{1,0:T(8,128)S(1)}, f32[384,256]{1,0:T(8,128)S(1)}, u32[]{:S(2)}, u32[]{:S(2)}) collective-permute-start(f32[384,256]{1,0:T(8,128)S(1)} %shard_map.94.near), channel_id=1, source_target_pairs={{0,4},{4,0},{8,12},{12,8},{16,20},{20,16},{24,28},{28,24},{1,5},{5... | collective-permute-start | bytes 1179656 | tf_op jit(solution)/shard_map/ppermute | solution.py:41
  81.4 17.8 %collective-permute-start.25 = (f32[384,256]{1,0:T(8,128)S(1)}, f32[384,256]{1,0:T(8,128)S(1)}, u32[]{:S(2)}, u32[]{:S(2)}) collective-permute-start(f32[384,256]{1,0:T(8,128)S(1)} %shard_map.86.far), channel_id=1, source_target_pairs={{0,4},{4,0},{8,12},{12,8},{16,20},{20,16},{24,28},{28,24},{1,5},{5... | collective-permute-start | bytes 1179656 | tf_op jit(solution)/shard_map/ppermute | solution.py:41
  81.9 5.8 %collective-permute-start.7 = (f32[64,512]{1,0:T(8,128)S(1)}, f32[64,512]{1,0:T(8,128)S(1)}, u32[]{:S(2)}, u32[]{:S(2)}) collective-permute-start(f32[64,512]{1,0:T(8,128)S(1)} %get-tuple-element.65), channel_id=1, source_target_pairs={{0,8},{4,12},{8,0},{12,4},{16,24},{20,28},{24,16},{28,20},{1,9},{5... | collective-permute-start | bytes 393224 | tf_op jit(solution)/shard_map/ppermute | solution.py:41
  83.5 8.2 %collective-permute-start.8 = (f32[64,512]{1,0:T(8,128)S(1)}, f32[64,512]{1,0:T(8,128)S(1)}, u32[]{:S(2)}, u32[]{:S(2)}) collective-permute-start(f32[64,512]{1,0:T(8,128)S(1)} %get-tuple-element.66), channel_id=1, source_target_pairs={{0,16},{4,20},{8,24},{12,28},{16,0},{20,4},{24,8},{28,12},{1,17},{... | collective-permute-start | bytes 393224 | tf_op jit(solution)/shard_map/ppermute | solution.py:41
  83.8 8.0 %collective-permute-start.9 = (f32[64,512]{1,0:T(8,128)S(1)}, f32[64,512]{1,0:T(8,128)S(1)}, u32[]{:S(2)}, u32[]{:S(2)}) collective-permute-start(f32[64,512]{1,0:T(8,128)S(1)} %get-tuple-element.67), channel_id=1, source_target_pairs={{0,24},{4,28},{8,16},{12,20},{16,8},{20,12},{24,0},{28,4},{1,25},{... | collective-permute-start | bytes 393224 | tf_op jit(solution)/shard_map/ppermute | solution.py:41
  87.7 6.0 %collective-permute-start.14 = (f32[64,512]{1,0:T(8,128)S(1)}, f32[64,512]{1,0:T(8,128)S(1)}, u32[]{:S(2)}, u32[]{:S(2)}) collective-permute-start(f32[64,512]{1,0:T(8,128)S(1)} %get-tuple-element.84), channel_id=1, source_target_pairs={{0,8},{4,12},{8,0},{12,4},{16,24},{20,28},{24,16},{28,20},{1,9},{5... | collective-permute-start | bytes 393224 | tf_op jit(solution)/shard_map/ppermute | solution.py:41
  91.7 6.4 %collective-permute-start.15 = (f32[64,512]{1,0:T(8,128)S(1)}, f32[64,512]{1,0:T(8,128)S(1)}, u32[]{:S(2)}, u32[]{:S(2)}) collective-permute-start(f32[64,512]{1,0:T(8,128)S(1)} %get-tuple-element.85), channel_id=1, source_target_pairs={{0,16},{4,20},{8,24},{12,28},{16,0},{20,4},{24,8},{28,12},{1,17},{... | collective-permute-start | bytes 393224 | tf_op jit(solution)/shard_map/ppermute | solution.py:41
  91.7 6.4 %collective-permute-start.16 = (f32[64,512]{1,0:T(8,128)S(1)}, f32[64,512]{1,0:T(8,128)S(1)}, u32[]{:S(2)}, u32[]{:S(2)}) collective-permute-start(f32[64,512]{1,0:T(8,128)S(1)} %get-tuple-element.86), channel_id=1, source_target_pairs={{0,24},{4,28},{8,16},{12,20},{16,8},{20,12},{24,0},{28,4},{1,25},{... | collective-permute-start | bytes 393224 | tf_op jit(solution)/shard_map/ppermute | solution.py:41
